TPU v7x, 32 devices: a whole 2x2x4 slice. The times are simulated.
32 devices in a mesh: group: 2 (over y), row: 4 (over x, core), col: 4 (over z).
Axes of the slice: x: 2, y: 2, z: 4, core: 2. Of those that a mesh axis runs over, the one named last changes fastest.
Arguments:
- tokens: bfloat16 [4096, 4096], P(('group', 'col'), 'row'), parts along dimension 0, may hold values from -6 to 6
- norm_gain: bfloat16 [4096], replicated, may hold values from 0.099609375 to 1.8984375
- gate_weight: bfloat16 [4096, 14336], P('col', 'row'), may hold values from -0.125 to 0.125
- up_weight: bfloat16 [4096, 14336], P('col', 'row'), may hold values from -0.125 to 0.125
- down_weight: bfloat16 [14336, 4096], P('col', 'row'), may hold values from -0.0625 to 0.0625
- block_mask: int32 [3, 64, 64], replicated, may hold values from 0 to 1, as said below
Outputs:
- mixed: bfloat16 [4096, 4096], P(('group', 'col'), 'row'), parts along dimension 0
There are 2 independent parts, one for each index of `group`. A program takes and returns all parts, laid end to end along the dimension named above; an argument that names none is the same for every part. Nothing has to cross between parts.
Inputs may be any that keep to these rules, and one draw needn't show every extreme that they name: `block_mask`: in every mask and every block column, each aligned group of 16 block rows (those of one index of col) holds 1 to 12 ones, and in every block column some group holds exactly 12.
All inputs are finite; a program needn't handle non-finite values.
Results may differ from a plain program's by a relative error of at most 0.0064.
Values may be sent and summed in bfloat16 or wider, within the bound.
No kernel may reach another device: no remote copies, remote signals or barrier semaphores. Data moves between devices by JAX's collectives and lax.ppermute only.
A program may use at most 256 MiB of HBM per device.

v0:
```python
import jax
import jax.numpy as jnp
from jax import lax
from jax.sharding import PartitionSpec as P


def masked_tile(weight, mask, col_at, row_at, n_col, n_row):
    per_col = mask.shape[0] // n_col
    per_row = mask.shape[1] // n_row
    tile = lax.dynamic_slice(mask, (col_at * per_col, row_at * per_row), (per_col, per_row))
    tall = weight.shape[0] // per_col
    broad = weight.shape[1] // per_row
    shaped = (
        weight.reshape(per_col, tall, per_row, broad) * tile.astype(weight.dtype)[:, None, :, None]
    )
    return shaped.reshape(weight.shape)


def body(tokens, norm_gain, gate_weight, up_weight, down_weight, block_mask):
    n_row = lax.axis_size("row")
    n_col = lax.axis_size("col")
    row_at = lax.axis_index("row")
    col_at = lax.axis_index("col")
    whole = lax.all_gather(tokens, "row", axis=1, tiled=True)
    values = whole.astype(jnp.float32)
    square_mean = jnp.mean(values * values, axis=-1, keepdims=True)
    normed = (values * lax.rsqrt(square_mean + 1e-05) * norm_gain.astype(jnp.float32)).astype(
        jnp.bfloat16
    )
    gate_tile = masked_tile(gate_weight, block_mask[0], col_at, row_at, n_col, n_row)
    up_tile = masked_tile(up_weight, block_mask[1], col_at, row_at, n_col, n_row)
    gate = jnp.dot(
        normed,
        lax.all_gather(gate_tile, "col", axis=0, tiled=True),
        preferred_element_type=jnp.float32,
    )
    up = jnp.dot(
        normed,
        lax.all_gather(up_tile, "col", axis=0, tiled=True),
        preferred_element_type=jnp.float32,
    )
    hidden = (jax.nn.silu(gate) * up).astype(jnp.bfloat16)
    down_tile = masked_tile(down_weight, block_mask[2], col_at, row_at, n_col, n_row)
    down_full = lax.all_gather(down_tile, "col", axis=0, tiled=True)
    mixed = jnp.dot(
        lax.all_gather(hidden, "row", axis=1, tiled=True),
        down_full,
        preferred_element_type=jnp.float32,
    )
    return mixed.astype(jnp.bfloat16)


def solution(mesh):
    in_specs = (
        P(("group", "col"), "row"),
        P(),
        P("col", "row"),
        P("col", "row"),
        P("col", "row"),
        P(),
    )
    out_specs = P(("group", "col"), "row")
    return jax.shard_map(body, mesh=mesh, in_specs=in_specs, out_specs=out_specs, check_vma=False)
```

profile of v0, /device:TPU:0, one launch (start us, length us, event | category | flops | bytes accessed | tf_op | source)
XLA Modules:
  0.0 1649.1 jit_solution(17445840301177124153)
XLA Ops:
  6.5 0.0 all-gather.6.cloned.1.call-start
  6.5 0.7 all-gather.6.cloned.1.call-update
  7.3 0.0 all-gather.8.cloned.1.call-start
  7.3 0.8 fusion.9
  8.1 0.1 fusion.6
  8.2 3.8 mul.76
  12.0 16.7 %mul.77 = bf16[1024,3584]{1,0:T(8,128)(2,1)} reshape(bf16[16,64,16,224]{3,2,1,0:T(8,128)(2,1)} %mul.76) | data formatting | bytes 14680064 | tf_op jit(solution)/shard_map/mul | solution.py:14
  28.7 10.1 mul.78
  38.9 0.0 all-gather.8.cloned.1.call-update
  38.9 0.0 all-gather.10.cloned.1.call-start
  38.9 4.0 mul.80
  42.9 16.9 %mul.81 = bf16[1024,3584]{1,0:T(8,128)(2,1)} reshape(bf16[16,64,16,224]{3,2,1,0:T(8,128)(2,1)} %mul.80) | data formatting | bytes 14680064 | tf_op jit(solution)/shard_map/mul | solution.py:14
  59.8 12.4 mul.82
  72.2 0.0 all-gather.10.cloned.1.call-update
  72.2 0.2 all-gather.14.cloned.1.call-start
  72.5 0.1 fusion.8
  72.5 0.1 copy.7
  72.6 3.8 mul.84
  76.5 16.6 %mul.85 = bf16[3584,1024]{0,1:T(8,128)(2,1)} reshape(bf16[16,224,16,64]{1,0,3,2:T(8,128)(2,1)} %mul.84) | data formatting | bytes 14680064 | tf_op jit(solution)/shard_map/mul | solution.py:14
  93.1 10.1 copy.8
  103.2 10.1 mul.86
  113.3 0.0 copy-start
  113.3 0.0 all-gather.14.cloned.1.call-update
  113.3 0.0 all-gather.12.cloned.1.call-start
  113.4 0.6 copy-done
  114.0 0.0 all-gather.6.cloned.1.call-done
  114.0 3.1 fusion
  117.2 423.7 %all-gather.8.cloned.1.call-done = bf16[4096,3584]{1,0:T(8,128)(2,1)} async-done(((bf16[1024,3584]{1,0:T(8,128)(2,1)}), bf16[4096,3584]{1,0:T(8,128)(2,1)}) %all-gather.8.cloned.1.call-update) | async-done | bytes 29360144 | tf_op jit(solution)/shard_map/all_gather | solution.py:34
  540.8 24.2 %fusion.4 = f32[512,3584]{1,0:T(8,128)} fusion(bf16[4096,3584]{1,0:T(8,128)(2,1)} %all-gather.8.cloned.1.call-done, bf16[512,4096]{1,0:T(8,128)(2,1)} %all-gather.6.cloned.1.call-done, f32[4096]{0:T(1024)S(1)} %convert_element_type.46, f32[512]{0:T(512)S(1)} %add_rsqrt_fusion), kind=kOutput, calls=%fused_computation.7 | convolution fusion | flops 15040774144 | bytes 40912896 | tf_op jit(solution)/shard_map/dot_general | solution.py:32
  565.0 468.7 %all-gather.10.cloned.1.call-done = bf16[4096,3584]{1,0:T(8,128)(2,1)} async-done(((bf16[1024,3584]{1,0:T(8,128)(2,1)}), bf16[4096,3584]{1,0:T(8,128)(2,1)}) %all-gather.10.cloned.1.call-update) | async-done | bytes 29360144 | tf_op jit(solution)/shard_map/all_gather | solution.py:39
  1033.7 27.3 %multiply_convert_fusion = bf16[512,3584]{1,0:T(8,128)(2,1)} fusion(f32[512,3584]{1,0:T(8,128)} %fusion.4, bf16[4096,3584]{1,0:T(8,128)(2,1)} %all-gather.10.cloned.1.call-done, bf16[512,4096]{1,0:T(8,128)(2,1)} %all-gather.6.cloned.1.call-done, f32[4096]{0:T(1024)S(1)} %convert_element_type.46, f32[512]{0:T(512)S(1)} %add_rsqrt_fusion), kind=kOutput, calls=%fused_computation.5 | convolution fusion | flops 15051784192 | bytes 44582912 | tf_op jit(solution)/shard_map/dot_general | solution.py:37
  1061.1 0.0 all-gather.12.cloned.1.call-update
  1061.1 465.4 %all-gather.14.cloned.1.call-done = bf16[14336,1024]{0,1:T(8,128)(2,1)} async-done(((bf16[3584,1024]{0,1:T(8,128)(2,1)}), bf16[14336,1024]{0,1:T(8,128)(2,1)}) %all-gather.14.cloned.1.call-update) | async-done | bytes 29360144 | tf_op jit(solution)/shard_map/all_gather | solution.py:44
  1526.5 93.6 %all-gather.12.cloned.1.call-done = bf16[512,14336]{1,0:T(8,128)(2,1)} async-done(((bf16[512,3584]{1,0:T(8,128)(2,1)}), bf16[512,14336]{1,0:T(8,128)(2,1)}) %all-gather.12.cloned.1.call-update) | async-done | bytes 14680080 | tf_op jit(solution)/shard_map/all_gather | solution.py:46
  1620.1 22.5 %convolution_convert_fusion = bf16[512,1024]{1,0:T(8,128)(2,1)} fusion(bf16[512,14336]{1,0:T(8,128)(2,1)} %all-gather.12.cloned.1.call-done, bf16[14336,1024]{0,1:T(8,128)(2,1)} %all-gather.14.cloned.1.call-done), kind=kOutput, calls=%fused_computation.6 | convolution fusion | flops 15032909824 | bytes 45088768 | tf_op jit(solution)/shard_map/dot_general | solution.py:45
  (2 shorter events, 0.0 us)
Async XLA Ops:
  6.5 107.5 %all-gather.6.cloned.1.call-start = ((), (), s32[]{:S(2)}) async-start(), calls=%async_computation | async-start | bytes 5242880 | tf_op jit(solution)/shard_map/all_gather | solution.py:24
  7.3 533.6 %all-gather.8.cloned.1.call-start = ((), (), s32[]{:S(2)}) async-start(), calls=%async_computation.1 | async-start | bytes 36700160 | tf_op jit(solution)/shard_map/all_gather | solution.py:34
  38.9 994.9 %all-gather.10.cloned.1.call-start = ((), (), s32[]{:S(2)}) async-start(), calls=%async_computation.2 | async-start | bytes 36700160 | tf_op jit(solution)/shard_map/all_gather | solution.py:39
  72.2 1454.3 %all-gather.14.cloned.1.call-start = ((), (), s32[]{:S(2)}) async-start(), calls=%async_computation.4 | async-start | bytes 36700160 | tf_op jit(solution)/shard_map/all_gather | solution.py:44
  113.3 0.7 copy-start
  113.3 1506.8 %all-gather.12.cloned.1.call-start = ((), (), s32[]{:S(2)}) async-start(), calls=%async_computation.3 | async-start | bytes 18350080 | tf_op jit(solution)/shard_map/all_gather | solution.py:46
Sparse Core Ops, SparseCore 0:
  8.9 37.1 all-gather.5
  47.7 493.0 all-gather.7
  542.4 491.2 all-gather.9
  1035.2 491.2 all-gather.13
  1527.9 92.1 all-gather.11
where the time goes:
time: 1650 us
  waiting for transfers between devices  1450 us (88%)
  matrix products  74 us (4%)
  local copies, waits for them, and re-layouts  73.5 us (4%)
  other arithmetic  36 us (2%)
    all_gather x1, waiting for transfers between devices, body(): lax.all_gather(up_tile, 'col', axis=0, tiled=True)  469 us
    all_gather x1, waiting for transfers between devices, body(): down_full = lax.all_gather(down_tile, 'col', axis=0, tiled=True)  465 us
    all_gather x1, waiting for transfers between devices, body(): lax.all_gather(gate_tile, 'col', axis=0, tiled=True)  424 us
    all_gather x1, waiting for transfers between devices, body(): lax.all_gather(hidden, 'row', axis=1, tiled=True)  93.6 us
    mul x6, local copies, waits for them, and re-layouts, masked_tile(): weight.reshape(per_col, tall, per_row, broad)  61.8 us
  transfers between devices with their start and end apart: 5, of which 4 were waited for; matrix products, arithmetic and copies ran while one was open for 10% of the time, Pallas kernels for 0%

commit v1 on v0

v1 whole, which is shorter than its diff:
```python
import jax
import jax.numpy as jnp
from jax import lax
from jax.experimental import pallas as pl
from jax.experimental.pallas import tpu as pltpu
from jax.sharding import PartitionSpec as P

F32 = jnp.float32
BF16 = jnp.bfloat16


def masked_tile(weight, mask, col_at, row_at, n_col, n_row):
    per_col = mask.shape[0] // n_col
    per_row = mask.shape[1] // n_row
    tile = lax.dynamic_slice(mask, (col_at * per_col, row_at * per_row), (per_col, per_row))
    tall = weight.shape[0] // per_col
    broad = weight.shape[1] // per_row
    shaped = (
        weight.reshape(per_col, tall, per_row, broad) * tile.astype(weight.dtype)[:, None, :, None]
    )
    return shaped.reshape(weight.shape)


def plain_body(tokens, norm_gain, gate_weight, up_weight, down_weight, block_mask):
    n_row = lax.axis_size("row")
    n_col = lax.axis_size("col")
    row_at = lax.axis_index("row")
    col_at = lax.axis_index("col")
    whole = lax.all_gather(tokens, "row", axis=1, tiled=True)
    values = whole.astype(F32)
    square_mean = jnp.mean(values * values, axis=-1, keepdims=True)
    normed = (values * lax.rsqrt(square_mean + 1e-05) * norm_gain.astype(F32)).astype(BF16)
    gate_tile = masked_tile(gate_weight, block_mask[0], col_at, row_at, n_col, n_row)
    up_tile = masked_tile(up_weight, block_mask[1], col_at, row_at, n_col, n_row)
    gate = jnp.dot(
        normed, lax.all_gather(gate_tile, "col", axis=0, tiled=True), preferred_element_type=F32
    )
    up = jnp.dot(
        normed, lax.all_gather(up_tile, "col", axis=0, tiled=True), preferred_element_type=F32
    )
    hidden = (jax.nn.silu(gate) * up).astype(BF16)
    down_tile = masked_tile(down_weight, block_mask[2], col_at, row_at, n_col, n_row)
    down_full = lax.all_gather(down_tile, "col", axis=0, tiled=True)
    mixed = jnp.dot(
        lax.all_gather(hidden, "row", axis=1, tiled=True), down_full, preferred_element_type=F32
    )
    return mixed.astype(BF16)


def cap_of(per_col):
    return per_col * 3 // 4


def lane_parts(tile, broad):
    first = tile * 128 // broad
    last = (tile * 128 + 127) // broad
    return first, last, last * broad - tile * 128


def pack(gate_weight, up_weight, table, where_at, shift, per_col, per_row, n_col, n_blocks):
    rows, cols = gate_weight.shape
    width = cols // n_col
    tall = rows // per_col
    broad = cols // per_row
    cap = cap_of(per_col)
    per_dest = per_row // n_col

    def kernel(table_ref, at_ref, gate_ref, up_ref, out_ref):
        group, row, col = at_ref[0], at_ref[1], at_ref[2]
        dest = lax.rem(col + shift, n_col)
        left = row * per_row + dest * per_dest

        def copy_from(src):
            @pl.loop(0, cap)
            def _(slot):
                base = ((group * n_col + col) * cap + slot) * n_blocks + left
                to = pl.ds(pl.multiple_of(slot * tall, tall), tall)
                for tile in range(width // 128):
                    first, last, cut = lane_parts(tile, broad)
                    lanes = slice(tile * 128, tile * 128 + 128)
                    at = table_ref[base + first]
                    val = src[pl.ds(pl.multiple_of(at * tall, tall), tall), lanes]
                    if last != first:
                        lane = lax.broadcasted_iota(jnp.int32, (1, 128), 1)
                        early = (lane < cut).astype(F32)
                        at = table_ref[base + last]
                        val2 = src[pl.ds(pl.multiple_of(at * tall, tall), tall), lanes]
                        val = val * early.astype(BF16) + val2 * (1.0 - early).astype(BF16)
                    out_ref[to, lanes] = val

        @pl.when(group == 0)
        def _():
            copy_from(gate_ref)

        @pl.when(group != 0)
        def _():
            copy_from(up_ref)

    spec = pl.BlockSpec((rows, width), lambda i, table, at: (0, lax.rem(at[2] + shift, n_col)))
    return pl.pallas_call(
        kernel,
        grid_spec=pltpu.PrefetchScalarGridSpec(
            num_scalar_prefetch=2,
            grid=(1,),
            in_specs=[spec, spec],
            out_specs=pl.BlockSpec((cap * tall, width), lambda i, table, at: (0, 0)),
        ),
        out_shape=jax.ShapeDtypeStruct((cap * tall, width), BF16),
        cost_estimate=pl.CostEstimate(flops=0, bytes_accessed=6 * rows * width, transcendentals=0),
        name=f"pack{shift}",
    )(table, where_at, gate_weight, up_weight)


def expand(mine, other, slots, where_at, shift, dense, sizes):
    rows, width, per_col, per_row, n_col, n_blocks = sizes
    tall = rows // per_col
    per_dest = per_row // n_col
    broad = width // per_dest
    own = shift == 0

    def kernel(slots_ref, at_ref, mine_ref, other_ref, *rest):
        out_ref = rest[-1]
        group, row, col = at_ref[0], at_ref[1], at_ref[2]
        source = lax.rem(col - shift + n_col, n_col)
        left = row * per_row + col * per_dest

        @pl.loop(0, per_col)
        def _(block):
            to = pl.ds(pl.multiple_of(block * tall, tall), tall)
            for which, src in ((0, mine_ref), (1, other_ref)):
                matrix = group if which == 0 else 1 - group
                base = ((matrix * n_col + source) * per_col + block) * n_blocks + left
                for tile in range(width // 128):
                    first, last, cut = lane_parts(tile, broad)
                    lanes = slice(tile * 128, tile * 128 + 128)
                    total = None
                    for part in range(first, last + 1):
                        slot = slots_ref[base + part]
                        keep = jnp.where(slot >= 0, 1.0, 0.0).astype(F32)
                        at = block if own else jnp.maximum(slot, 0)
                        val = src[pl.ds(pl.multiple_of(at * tall, tall), tall), lanes]
                        weight = jnp.full((1, 128), keep, F32)
                        if last != first:
                            lane = lax.broadcasted_iota(jnp.int32, (1, 128), 1)
                            side = lane < cut if part == first else lane >= cut
                            weight = jnp.where(side, weight, 0.0)
                        val = val * weight.astype(BF16)
                        total = val if total is None else total + val
                    start = tile * 256 + which * 128
                    out_ref[0, to, start : start + 128] = total

    src_spec = [pl.BlockSpec(mine.shape, lambda i, slots, at: (0, 0))] * 2
    args = [slots, where_at, mine, other]
    aliases = {}
    if dense is not None:
        args.append(dense)
        src_spec = src_spec + [pl.BlockSpec(memory_space=pl.ANY)]
        aliases = {4: 0}
    return pl.pallas_call(
        kernel,
        grid_spec=pltpu.PrefetchScalarGridSpec(
            num_scalar_prefetch=2,
            grid=(1,),
            in_specs=src_spec,
            out_specs=pl.BlockSpec(
                (1, rows, 2 * width),
                lambda i, slots, at: (lax.rem(at[2] - shift + n_col, n_col), 0, 0),
            ),
        ),
        out_shape=jax.ShapeDtypeStruct((n_col, rows, 2 * width), BF16),
        input_output_aliases=aliases,
        cost_estimate=pl.CostEstimate(flops=0, bytes_accessed=8 * rows * width, transcendentals=0),
        name=f"expand{shift}",
    )(*args)


def gate_up(pieces, dense, where_at, name):
    tokens, depth = pieces[0].shape
    n_col, rows, double = dense.shape
    tiles = double // 256

    def kernel(at_ref, x0, x1, x2, x3, w_ref, out_ref):
        group, row = at_ref[0], at_ref[1]
        total = None
        for m, x in enumerate((x0, x1, x2, x3)):
            part = jnp.dot(x[...], w_ref[row ^ m], preferred_element_type=F32)
            total = part if total is None else total + part
        mine, other = total[:, :128], total[:, 128:]
        gate = jnp.where(group == 0, mine, other)
        up = jnp.where(group == 0, other, mine)
        out_ref[...] = (gate / (1.0 + jnp.exp(-gate)) * up).astype(BF16)

    return pl.pallas_call(
        kernel,
        grid_spec=pltpu.PrefetchScalarGridSpec(
            num_scalar_prefetch=1,
            grid=(tiles,),
            in_specs=[pl.BlockSpec((tokens, depth), lambda n, at: (0, 0))] * 4
            + [pl.BlockSpec((n_col, rows, 256), lambda n, at: (0, 0, n))],
            out_specs=pl.BlockSpec((tokens, 128), lambda n, at: (0, n)),
        ),
        out_shape=jax.ShapeDtypeStruct((tokens, tiles * 128), BF16),
        cost_estimate=pl.CostEstimate(
            flops=2 * tokens * n_col * rows * double,
            bytes_accessed=2 * (4 * tokens * depth + dense.size),
            transcendentals=tokens * tiles * 128,
        ),
        name=name,
    )(where_at, *pieces, dense)


def down_part(pieces, weights, where_at, so_far, name):
    tokens, depth = pieces[0].shape
    n_col, _, _, half = weights.shape

    def kernel(at_ref, h0, h1, h2, h3, w_ref, *rest):
        out_ref = rest[-1]
        row, col = at_ref[1], at_ref[2]
        total = None
        for m, h in enumerate((h0, h1, h2, h3)):
            at = lax.rem(col - (row ^ m) + n_col, n_col)
            part = jnp.dot(h[...], w_ref[at, 0], preferred_element_type=F32)
            total = part if total is None else total + part
        if so_far is not None:
            total = total + rest[0][...].astype(F32)
        out_ref[...] = total.astype(BF16)

    extra = [] if so_far is None else [so_far]
    out_spec = pl.BlockSpec((tokens, half), lambda n, at: (0, n))
    return pl.pallas_call(
        kernel,
        grid_spec=pltpu.PrefetchScalarGridSpec(
            num_scalar_prefetch=1,
            grid=(2,),
            in_specs=[pl.BlockSpec((tokens, depth), lambda n, at: (0, 0))] * 4
            + [pl.BlockSpec((n_col, 1, depth, half), lambda n, at: (0, n ^ at[0], 0, 0))]
            + [out_spec] * len(extra),
            out_specs=out_spec,
        ),
        out_shape=jax.ShapeDtypeStruct((tokens, 2 * half), BF16),
        cost_estimate=pl.CostEstimate(
            flops=4 * tokens * n_col * depth * half,
            bytes_accessed=2 * (4 * tokens * depth + weights.size + tokens * half * 2),
            transcendentals=0,
        ),
        name=name,
    )(where_at, *pieces, weights, *extra)


def body(tokens, norm_gain, gate_weight, up_weight, down_weight, block_mask):
    n_row = lax.axis_size("row")
    n_col = lax.axis_size("col")
    group = lax.axis_index("group")
    row = lax.axis_index("row")
    col = lax.axis_index("col")
    n_blocks = block_mask.shape[-1]
    per_col = n_blocks // n_col
    per_row = n_blocks // n_row
    cap = cap_of(per_col)
    rows, cols = gate_weight.shape
    width = cols // n_col

    def along(axis, shift):
        size = lax.axis_size(axis)
        pairs = [(i, (i + shift) % size) for i in range(size)]
        return lambda v: lax.ppermute(v, axis, pairs)

    def by_xor(bit):
        pairs = [(i, i ^ bit) for i in range(n_row)]
        return lambda v: lax.ppermute(v, "row", pairs)

    z = {s: along("col", s) for s in range(1, n_col)}
    y_swap = along("group", 1)
    core_swap = by_xor(1)
    x_swap = by_xor(2)

    three = lax.iota(jnp.int32, 3)
    where_at = jnp.where(three == 0, group, jnp.where(three == 1, row, col)).astype(jnp.int32)
    grouped = block_mask[:2].reshape(2, n_col, per_col, n_blocks)
    ids = jnp.arange(per_col, dtype=jnp.int32)
    before = (ids[None, :] < ids[:, None]).astype(jnp.int32)
    rank = jnp.sum(before[None, None, :, :, None] * grouped[:, :, None, :, :], axis=3)
    slots = jnp.where(grouped > 0, rank, -1).astype(jnp.int32)
    wanted = jnp.arange(cap, dtype=jnp.int32)
    table = jnp.sum(
        jnp.where(
            slots[:, :, None, :, :] == wanted[None, None, :, None, None],
            ids[None, None, None, :, None],
            0,
        ),
        axis=3,
    ).astype(jnp.int32)
    slots = slots.reshape(-1)
    table = table.reshape(-1)

    values = tokens.astype(F32)
    squares = jnp.sum(values * values, axis=-1)
    squares = squares + core_swap(squares)
    squares = squares + x_swap(squares)
    depth = tokens.shape[1]
    gain = lax.dynamic_slice(norm_gain, (row * depth,), (depth,)).astype(F32)
    mean = (squares / norm_gain.shape[0])[:, None]
    normed = (values * lax.rsqrt(mean + 1e-05) * gain).astype(BF16)
    shards = [normed]
    for _ in range(n_col - 1):
        shards.append(z[1](shards[-1]))

    def over_row(v):
        across = x_swap(v)
        return v, core_swap(v), across, core_swap(across)

    chunks = [over_row(v) for v in shards]

    sizes = (rows, width, per_col, per_row, n_col, n_blocks)
    order = [s for s in range(1, n_col) if 2 * s != n_col] + [n_col // 2]
    dense = None
    mine = {}
    for s in order:
        packed = pack(
            gate_weight, up_weight, table, where_at, s, per_col, per_row, n_col, n_blocks
        )
        mine[s] = z[s](packed)
    first = jnp.where(group == 0, 1, 0) > 0
    own_gate = lax.dynamic_slice(gate_weight, (0, col * width), (rows, width))
    own_up = lax.dynamic_slice(up_weight, (0, col * width), (rows, width))
    own_mine = jnp.where(first, own_gate, own_up)
    own_other = jnp.where(first, own_up, own_gate)
    dense = expand_own(own_mine, own_other, slots, where_at, sizes)
    for s in order:
        dense = expand(mine[s], y_swap(mine[s]), slots, where_at, s, dense, sizes)

    down_rows = down_weight.shape[0] // n_col
    half = down_weight.shape[1] // 2
    tile = lax.dynamic_slice(block_mask[2], (col * per_col, row * per_row), (per_col, per_row))
    wide = jnp.repeat(tile.astype(BF16), down_weight.shape[1] // per_row, axis=1)
    sub = per_col // n_col

    def down_piece(dest, side):
        at = (dest * down_rows, side * half)
        block = lax.dynamic_slice(down_weight, at, (down_rows, half))
        ones = lax.dynamic_slice(wide, (dest * sub, side * half), (sub, half))
        return (block.reshape(sub, -1, half) * ones[:, None, :]).reshape(down_rows, half)

    parts = [[down_piece(col, group), down_piece(col, 1 - group)]] + [None] * (n_col - 1)
    for s in order:
        got = z[s](down_piece(lax.rem(col + s, n_col), group))
        parts[s] = [got, y_swap(got)]
    weights = jnp.stack([v for pair in parts for v in pair]).reshape(n_col, 2, down_rows, half)

    so_far = None
    for s in list(range(1, n_col)) + [0]:
        hidden = gate_up(chunks[s], dense, where_at, f"gate_up{s}")
        out = down_part(over_row(hidden), weights, where_at, so_far, f"down{s}")
        so_far = z[1](out) if s else out
    return so_far


def expand_own(own_mine, own_other, slots, where_at, sizes):
    return expand(own_mine, own_other, slots, where_at, 0, None, sizes)


def solution(mesh):
    in_specs = (
        P(("group", "col"), "row"),
        P(),
        P("col", "row"),
        P("col", "row"),
        P("col", "row"),
        P(),
    )
    out_specs = P(("group", "col"), "row")
    sizes = dict(mesh.shape)
    fits = sizes["row"] == 4 and sizes["col"] == 4 and sizes["group"] == 2

    def step(tokens, norm_gain, gate_weight, up_weight, down_weight, block_mask):
        lanes = gate_weight.shape[1] // (sizes["row"] * sizes["col"])
        chosen = body if fits and lanes % 128 == 0 else plain_body
        return jax.shard_map(
            chosen, mesh=mesh, in_specs=in_specs, out_specs=out_specs, check_vma=False
        )(tokens, norm_gain, gate_weight, up_weight, down_weight, block_mask)

    return step
```

time: 1650 us -> 484 us (0.29)
  waiting for transfers between devices: 1450 us -> 251 us
  Pallas kernels: 0 us -> 134 us
  matrix products: 74 us -> 0 us
  starting transfers between devices: 0.35 us -> 62.6 us
  local copies, waits for them, and re-layouts: 73.5 us -> 18.7 us
  other arithmetic: 36 us -> 15.1 us
    all_gather x5 -> x0, waiting for transfers between devices: 1450 us -> none  [the longest x1 469 us: body(): lax.all_gather(up_tile, 'col', axis=0, tiled=True)]
    ppermute x0 -> x44, waiting for transfers between devices: none -> 251 us  [the longest x18 232 us: along(): return lambda v: lax.ppermute(v, axis, pairs)]
    pallas_call x0 -> x15, Pallas kernels: none -> 134 us  [the longest x4 57.1 us: gate_up(): pl.pallas_call(kernel, grid_spec=pltpu.PrefetchScalarGridSpec(num_scalar_...]
    dot_general x3 -> x0, matrix products: 74 us -> none  [the longest x1 27.3 us: body(): jnp.dot(normed, lax.all_gather(up_tile, 'col', axis=0, tiled=True), prefe...]
    ppermute x0 -> x44, starting transfers between devices: none -> 62.6 us  [the longest x18 47.8 us: along(): return lambda v: lax.ppermute(v, axis, pairs)]
    mul x6 -> x0, local copies, waits for them, and re-layouts: 61.8 us -> none  [masked_tile(): weight.reshape(per_col, tall, per_row, broad)]
    mul x3 -> x1, other arithmetic: 32.7 us -> 4.47 us  [down_piece(): block.reshape(sub, -1, half) * ones[:, None, :]]
  transfers between devices with their start and end apart: 5 -> 44, of which waited for: 4 -> 15; matrix products, arithmetic and copies ran while one was open for 10% -> 6% of each run, Pallas kernels for 0% -> 26%
where the time goes in v1:
time: 484 us; the launch traced here: 482 us
  waiting for transfers between devices  251 us (52%)
  Pallas kernels  134 us (28%)
  starting transfers between devices  62.6 us (13%)
  local copies, waits for them, and re-layouts  18.7 us (4%)
  other arithmetic  15.1 us (3%)
    ppermute x18, waiting for transfers between devices, along(): return lambda v: lax.ppermute(v, axis, pairs)  232 us
    pallas_call x4, Pallas kernels, gate_up(): pl.pallas_call(kernel, grid_spec=pltpu.PrefetchScalarGridSpec(num_scalar_...  57.1 us
    ppermute x18, starting transfers between devices, along(): return lambda v: lax.ppermute(v, axis, pairs)  47.8 us
    pallas_call x4, Pallas kernels, down_part(): pl.pallas_call(kernel, grid_spec=pltpu.PrefetchScalarGridSpec(num_scalar_...  38 us
    pallas_call x4, Pallas kernels, expand(): pl.pallas_call(kernel, grid_spec=pltpu.PrefetchScalarGridSpec(num_scalar_...  24.7 us
    ppermute x26, waiting for transfers between devices, by_xor(): return lambda v: lax.ppermute(v, 'row', pairs)  19.3 us
    unnamed x33, local copies, waits for them, and re-layouts  15.7 us
    ppermute x26, starting transfers between devices, by_xor(): return lambda v: lax.ppermute(v, 'row', pairs)  14.8 us
  transfers between devices with their start and end apart: 44, of which 15 were waited for; matrix products, arithmetic and copies ran while one was open for 6% of the time, Pallas kernels for 26%

profile of v1, /device:TPU:0, one launch (start us, length us, event | category | flops | bytes accessed | tf_op | source)
XLA Modules:
  0.0 482.2 jit_solution(11623824371312448881)
XLA Ops:
  0.0 1.5 fusion
  5.5 4.7 pack1.1
  10.3 2.6 collective-permute-start.9
  12.9 4.7 pack3.1
  17.6 2.2 collective-permute-start.7
  19.8 1.7 collective-permute-start.1
  22.2 1.2 collective-permute-done.1
  23.4 1.3 fusion.2.x0
  25.1 4.5 bitcast_multiply_fusion
  29.6 1.4 collective-permute-start.14
  31.0 4.7 pack2.1
  35.7 2.9 collective-permute-start.5
  38.6 59.7 %collective-permute-done.20.x0 = bf16[512,1024]{1,0:T(8,128)(2,1)} collective-permute-done((bf16[512,1024]{1,0:T(8,128)(2,1)}, bf16[512,1024]{1,0:T(8,128)(2,1)}, u32[]{:S(2)}, u32[]{:S(2)}) %collective-permute-start.20) | collective-permute-done | bytes 1048608 | tf_op jit(solution)/shard_map/ppermute | solution.py:266
  98.3 1.7 collective-permute-start.36
  100.1 18.0 %collective-permute-done.14 = bf16[896,512]{1,0:T(8,128)(2,1)} collective-permute-done((bf16[896,512]{1,0:T(8,128)(2,1)}, bf16[896,512]{1,0:T(8,128)(2,1)}, u32[]{:S(2)}, u32[]{:S(2)}) %collective-permute-start.14) | collective-permute-done | bytes 917536 | tf_op jit(solution)/shard_map/ppermute | solution.py:266
  118.0 28.0 %collective-permute-start.21 = (bf16[512,1024]{1,0:T(8,128)(2,1)}, bf16[512,1024]{1,0:T(8,128)(2,1)S(1)}, u32[]{:S(2)}, u32[]{:S(2)}) collective-permute-start(bf16[512,1024]{1,0:T(8,128)(2,1)} %collective-permute-done.20.x0), channel_id=1, source_target_pairs={{0,1},{1,2},{2,3},{3,0},{4,5},{5,6},{6,7},{7,4},{8,9},{9,10},{10,1... | collective-permute-start | bytes 3145736 | tf_op jit(solution)/shard_map/ppermute | solution.py:266
  146.0 1.5 collective-permute-start.10
  148.0 51.1 %collective-permute-done.5.mine_ref = bf16[768,896]{1,0:T(8,128)(2,1)} collective-permute-done((bf16[768,896]{1,0:T(8,128)(2,1)}, bf16[768,896]{1,0:T(8,128)(2,1)}, u32[]{:S(2)}, u32[]{:S(2)}) %collective-permute-start.5) | collective-permute-done | bytes 1376288 | tf_op jit(solution)/shard_map/ppermute | solution.py:266
  199.1 1.5 collective-permute-start.6
  200.6 1.0 copy-done.4
  203.6 28.9 %collective-permute-done.6.other_ref = bf16[768,896]{1,0:T(8,128)(2,1)} collective-permute-done((bf16[768,896]{1,0:T(8,128)(2,1)}, bf16[768,896]{1,0:T(8,128)(2,1)}, u32[]{:S(2)}, u32[]{:S(2)}) %collective-permute-start.6) | collective-permute-done | bytes 1376288 | tf_op jit(solution)/shard_map/ppermute | solution.py:266
  232.5 1.5 collective-permute-start.30
  234.0 4.6 broadcast_select_fusion
  238.5 5.9 %expand0.1.rest_0_ = bf16[4,1024,1792]{2,1,0:T(8,128)(2,1)} custom-call(s32[8192]{0:T(1024)} %broadcast_select_fusion.2.slots_ref, s32[3]{0:T(128)} %compare_select_fusion.2.at_ref, bf16[1024,896]{1,0:T(8,128)(2,1)} %get-tuple-element.6.mine_ref, bf16[1024,896]{1,0:T(8,128)(2,1)} %get-tuple-element.5.other_ref), custom_call_target="tpu_custom_call" | custom-call | bytes 7340032 | tf_op jit(solution)/shard_map/expand0/pallas_call | solution.py:159
  244.5 6.2 %expand1.1.rest_0_ = bf16[4,1024,1792]{2,1,0:T(8,128)(2,1)} custom-call(s32[8192]{0:T(1024)} %broadcast_select_fusion.2.slots_ref, s32[3]{0:T(128)} %compare_select_fusion.2.at_ref, bf16[768,896]{1,0:T(8,128)(2,1)} %copy-done.1, bf16[768,896]{1,0:T(8,128)(2,1)} %collective-permute-done.10.other_ref, ...), custom_call_target="tpu_custom_call", output_to_operand_aliasing={{}: (4, {})} | custom-call | bytes 7340032 | tf_op jit(solution)/shard_map/expand1/pallas_call | solution.py:159
  250.7 6.1 %expand3.1.rest_0_ = bf16[4,1024,1792]{2,1,0:T(8,128)(2,1)} custom-call(s32[8192]{0:T(1024)} %broadcast_select_fusion.2.slots_ref, s32[3]{0:T(128)} %compare_select_fusion.2.at_ref, bf16[768,896]{1,0:T(8,128)(2,1)} %collective-permute-done.7.mine_ref, bf16[768,896]{1,0:T(8,128)(2,1)} %collective-permute-done.8.other_ref, ...), custom_call_target="tpu_custom_call", output_to_operand_aliasing={{}: (4, {})} | custom-call | bytes 7340032 | tf_op jit(solution)/shard_map/expand3/pallas_call | solution.py:159
  256.8 6.4 %expand2.1.w_ref = bf16[4,1024,1792]{2,1,0:T(8,128)(2,1)} custom-call(s32[8192]{0:T(1024)} %broadcast_select_fusion.2.slots_ref, s32[3]{0:T(128)} %compare_select_fusion.2.at_ref, bf16[768,896]{1,0:T(8,128)(2,1)} %collective-permute-done.5.mine_ref, bf16[768,896]{1,0:T(8,128)(2,1)} %collective-permute-done.6.other_ref, ...), custom_call_target="tpu_custom_call", output_to_operand_aliasing={{}: (4, {})} | custom-call | bytes 7340032 | tf_op jit(solution)/shard_map/expand2/pallas_call | solution.py:159
  263.2 2.0 collective-permute-start.22
  265.2 14.3 %gate_up1.1.h0 = bf16[512,896]{1,0:T(8,128)(2,1)} custom-call(s32[3]{0:T(128)} %compare_select_fusion.2.at_ref, bf16[512,1024]{1,0:T(8,128)(2,1)} %collective-permute-done.20.x0, bf16[512,1024]{1,0:T(8,128)(2,1)} %collective-permute-done.35.x1, bf16[512,1024]{1,0:T(8,128)(2,1)} %collective-permute-done.36.x2, bf16[512,1024]{1,0:T(8,128)(2,1)} %collective-permute-done.37.x3, ...), custom_call_target="tpu_custom_call" | custom-call | flops 7516192768 | bytes 18874368 | tf_op jit(solution)/shard_map/gate_up1/pallas_call | solution.py:193
  280.1 1.0 bitcast_dynamic-update-slice_fusion.7
  281.3 1.0 bitcast_dynamic-update-slice_fusion.6
  282.3 2.2 bitcast_dynamic-update-slice_fusion.5
  284.5 20.6 %collective-permute-done.22.x0 = bf16[512,1024]{1,0:T(8,128)(2,1)} collective-permute-done((bf16[512,1024]{1,0:T(8,128)(2,1)}, bf16[512,1024]{1,0:T(8,128)(2,1)}, u32[]{:S(2)}, u32[]{:S(2)}) %collective-permute-start.22) | collective-permute-done | bytes 1048608 | tf_op jit(solution)/shard_map/ppermute | solution.py:266
  305.6 2.2 bitcast_dynamic-update-slice_fusion.4
  307.8 1.5 collective-permute-start.17
  309.8 2.2 bitcast_dynamic-update-slice_fusion.3
  312.5 14.3 %gate_up2.1.h0 = bf16[512,896]{1,0:T(8,128)(2,1)} custom-call(s32[3]{0:T(128)} %compare_select_fusion.2.at_ref, bf16[512,1024]{1,0:T(8,128)(2,1)} %copy-done.4, bf16[512,1024]{1,0:T(8,128)(2,1)} %collective-permute-done.29.x1, bf16[512,1024]{1,0:T(8,128)(2,1)} %collective-permute-done.30.x2, bf16[512,1024]{1,0:T(8,128)(2,1)} %collective-permute-done.31.x3, ...), custom_call_target="tpu_custom_call" | custom-call | flops 7516192768 | bytes 18874368 | tf_op jit(solution)/shard_map/gate_up2/pallas_call | solution.py:193
  326.8 4.4 collective-permute-done.17
  331.2 1.5 collective-permute-start.3
  332.7 13.9 %collective-permute-done.19 = bf16[896,512]{1,0:T(8,128)(2,1)S(1)} collective-permute-done((bf16[896,512]{1,0:T(8,128)(2,1)}, bf16[896,512]{1,0:T(8,128)(2,1)S(1)}, u32[]{:S(2)}, u32[]{:S(2)}) %collective-permute-start.19) | collective-permute-done | bytes 917536 | tf_op jit(solution)/shard_map/ppermute | solution.py:266
  346.7 1.5 collective-permute-start.33
  348.4 1.1 bitcast_dynamic-update-slice_fusion.2
  349.5 2.2 bitcast_dynamic-update-slice_fusion.1
  351.6 1.0 bitcast_dynamic-update-slice_fusion
  352.9 9.3 %down1.1 = bf16[512,1024]{1,0:T(8,128)(2,1)} custom-call(s32[3]{0:T(128)} %compare_select_fusion.2.at_ref, bf16[512,896]{1,0:T(8,128)(2,1)} %gate_up1.1.h0, bf16[512,896]{1,0:T(8,128)(2,1)} %collective-permute-done.38.h1, bf16[512,896]{1,0:T(8,128)(2,1)} %collective-permute-done.39.h2, bf16[512,896]{1,0:T(8,128)(2,1)} %collective-permute-done.40.h3, ...), custom_call_target="tpu_custom_call" | custom-call | flops 3758096384 | bytes 12058624 | tf_op jit(solution)/shard_map/down1/pallas_call | solution.py:230
  362.7 9.1 %collective-permute-done.33.h2 = bf16[512,896]{1,0:T(8,128)(2,1)} collective-permute-done((bf16[512,896]{1,0:T(8,128)(2,1)}, bf16[512,896]{1,0:T(8,128)(2,1)}, u32[]{:S(2)}, u32[]{:S(2)}) %collective-permute-start.33) | collective-permute-done | bytes 917536 | tf_op jit(solution)/shard_map/ppermute | solution.py:270
  371.8 1.2 collective-permute-start.41
  373.1 14.3 %gate_up3.1.h0 = bf16[512,896]{1,0:T(8,128)(2,1)} custom-call(s32[3]{0:T(128)} %compare_select_fusion.2.at_ref, bf16[512,1024]{1,0:T(8,128)(2,1)} %collective-permute-done.22.x0, bf16[512,1024]{1,0:T(8,128)(2,1)} %collective-permute-done.23.x1, bf16[512,1024]{1,0:T(8,128)(2,1)} %copy-done.5, bf16[512,1024]{1,0:T(8,128)(2,1)} %collective-permute-done.25.x3, ...), custom_call_target="tpu_custom_call" | custom-call | flops 7516192768 | bytes 18874368 | tf_op jit(solution)/shard_map/gate_up3/pallas_call | solution.py:193
  387.4 1.6 collective-permute-start.27
  388.9 8.3 %collective-permute-done.41.rest_0_ = bf16[512,1024]{1,0:T(8,128)(2,1)} collective-permute-done((bf16[512,1024]{1,0:T(8,128)(2,1)}, bf16[512,1024]{1,0:T(8,128)(2,1)}, u32[]{:S(2)}, u32[]{:S(2)}) %collective-permute-start.41) | collective-permute-done | bytes 1048608 | tf_op jit(solution)/shard_map/ppermute | solution.py:266
  397.2 9.5 %down2.1 = bf16[512,1024]{1,0:T(8,128)(2,1)} custom-call(s32[3]{0:T(128)} %compare_select_fusion.2.at_ref, bf16[512,896]{1,0:T(8,128)(2,1)} %gate_up2.1.h0, bf16[512,896]{1,0:T(8,128)(2,1)} %copy-done.9, bf16[512,896]{1,0:T(8,128)(2,1)} %collective-permute-done.33.h2, bf16[512,896]{1,0:T(8,128)(2,1)} %collective-permute-done.34.h3, ...), custom_call_target="tpu_custom_call" | custom-call | flops 3758096384 | bytes 12058624 | tf_op jit(solution)/shard_map/down2/pallas_call | solution.py:230
  406.8 1.2 collective-permute-start.42
  408.0 2.4 collective-permute-done.27.h2
  410.5 1.0 copy-done.6
  411.4 14.3 %gate_up0.1.h0 = bf16[512,896]{1,0:T(8,128)(2,1)} custom-call(s32[3]{0:T(128)} %compare_select_fusion.2.at_ref, bf16[512,1024]{1,0:T(8,128)(2,1)} %fusion.2.x0, bf16[512,1024]{1,0:T(8,128)(2,1)} %copy-done.6, bf16[512,1024]{1,0:T(8,128)(2,1)} %collective-permute-done.3.x2, bf16[512,1024]{1,0:T(8,128)(2,1)} %collective-permute-done.4.x3, ...), custom_call_target="tpu_custom_call" | custom-call | flops 7516192768 | bytes 18874368 | tf_op jit(solution)/shard_map/gate_up0/pallas_call | solution.py:193
  425.7 1.5 collective-permute-start.12
  427.2 7.1 %collective-permute-done.42.rest_0_ = bf16[512,1024]{1,0:T(8,128)(2,1)S(1)} collective-permute-done((bf16[512,1024]{1,0:T(8,128)(2,1)}, bf16[512,1024]{1,0:T(8,128)(2,1)S(1)}, u32[]{:S(2)}, u32[]{:S(2)}) %collective-permute-start.42) | collective-permute-done | bytes 1048608 | tf_op jit(solution)/shard_map/ppermute | solution.py:266
  434.3 1.0 copy-done.7
  435.3 9.6 %down3.1 = bf16[512,1024]{1,0:T(8,128)(2,1)} custom-call(s32[3]{0:T(128)} %compare_select_fusion.2.at_ref, bf16[512,896]{1,0:T(8,128)(2,1)} %gate_up3.1.h0, bf16[512,896]{1,0:T(8,128)(2,1)} %collective-permute-done.26.h1, bf16[512,896]{1,0:T(8,128)(2,1)} %copy-done.10, bf16[512,896]{1,0:T(8,128)(2,1)} %collective-permute-done.28.h3, ...), custom_call_target="tpu_custom_call" | custom-call | flops 3758096384 | bytes 12058624 | tf_op jit(solution)/shard_map/down3/pallas_call | solution.py:230
  445.0 3.7 collective-permute-done.12.h2
  448.8 2.8 collective-permute-done.13.h3
  451.6 20.1 %collective-permute-done.43.rest_0_ = bf16[512,1024]{1,0:T(8,128)(2,1)S(1)} collective-permute-done((bf16[512,1024]{1,0:T(8,128)(2,1)}, bf16[512,1024]{1,0:T(8,128)(2,1)S(1)}, u32[]{:S(2)}, u32[]{:S(2)}) %collective-permute-start.43) | collective-permute-done | bytes 1048608 | tf_op jit(solution)/shard_map/ppermute | solution.py:266
  471.7 1.0 copy-done.8
  472.6 9.6 %down0.1 = bf16[512,1024]{1,0:T(8,128)(2,1)} custom-call(s32[3]{0:T(128)} %compare_select_fusion.2.at_ref, bf16[512,896]{1,0:T(8,128)(2,1)} %gate_up0.1.h0, bf16[512,896]{1,0:T(8,128)(2,1)} %copy-done.12, bf16[512,896]{1,0:T(8,128)(2,1)} %collective-permute-done.12.h2, bf16[512,896]{1,0:T(8,128)(2,1)} %collective-permute-done.13.h3, ...), custom_call_target="tpu_custom_call" | custom-call | flops 3758096384 | bytes 12058624 | tf_op jit(solution)/shard_map/down0/pallas_call | solution.py:230
  (97 shorter events, 11.1 us)
Async XLA Ops:
  1.5 18.3 %collective-permute-start = (f32[512]{0:T(512)S(1)}, f32[512]{0:T(512)S(1)}, u32[]{:S(2)}, u32[]{:S(2)}) collective-permute-start(f32[512]{0:T(512)S(1)} %fusion), channel_id=1, source_target_pairs={{0,4},{4,0},{8,12},{12,8},{1,5},{5,1},{9,13},{13,9},{2,6},{6,2},{1... | collective-permute-start | bytes 6152 | tf_op jit(solution)/shard_map/ppermute | solution.py:270
  10.3 13.1 %copy-start = (bf16[512,1024]{1,0:T(8,128)(2,1)S(1)}, bf16[512,1024]{1,0:T(8,128)(2,1)}, u32[]{:S(2)}) copy-start(bf16[512,1024]{1,0:T(8,128)(2,1)} %param.6) | copy-start | bytes 3145732
  10.3 135.7 %collective-permute-start.9 = (bf16[768,896]{1,0:T(8,128)(2,1)}, bf16[768,896]{1,0:T(8,128)(2,1)S(1)}, u32[]{:S(2)}, u32[]{:S(2)}) collective-permute-start(bf16[768,896]{1,0:T(8,128)(2,1)} %pack1.1), channel_id=1, source_target_pairs={{0,1},{1,2},{2,3},{3,0},{4,5},{5,6},{6,7},{7,4},{8,9},{9,10},{10,1... | collective-permute-start | bytes 4128776 | tf_op jit(solution)/shard_map/ppermute | solution.py:266
  17.6 7.1 %slice-start = ((s32[3,64,64]{2,1,0:T(8,128)}), s32[1,64,64]{2,1,0:T(8,128)S(1)}, s32[]{:S(2)}) async-start(s32[3,64,64]{2,1,0:T(8,128)} %param.11), calls=%async_computation | async-start | bytes 65536 | tf_op jit(solution)/shard_map/slice | solution.py:334
  17.6 129.9 %collective-permute-start.7 = (bf16[768,896]{1,0:T(8,128)(2,1)}, bf16[768,896]{1,0:T(8,128)(2,1)}, u32[]{:S(2)}, u32[]{:S(2)}) collective-permute-start(bf16[768,896]{1,0:T(8,128)(2,1)} %pack3.1), channel_id=1, source_target_pairs={{0,3},{1,0},{2,1},{3,2},{4,7},{5,4},{6,5},{7,6},{8,11},{9,8},{10,9... | collective-permute-start | bytes 4128776 | tf_op jit(solution)/shard_map/ppermute | solution.py:266
  19.8 3.6 collective-permute-start.1
  24.7 73.7 %collective-permute-start.20 = (bf16[512,1024]{1,0:T(8,128)(2,1)}, bf16[512,1024]{1,0:T(8,128)(2,1)}, u32[]{:S(2)}, u32[]{:S(2)}) collective-permute-start(bf16[512,1024]{1,0:T(8,128)(2,1)} %fusion.2.x0), channel_id=1, source_target_pairs={{0,1},{1,2},{2,3},{3,0},{4,5},{5,6},{6,7},{7,4},{8,9},{9,10},{10,1... | collective-permute-start | bytes 3145736 | tf_op jit(solution)/shard_map/ppermute | solution.py:266
  29.6 172.6 %copy-start.3 = (s32[3,64,64]{2,1,0:T(8,128)S(1)}, s32[3,64,64]{2,1,0:T(8,128)}, u32[]{:S(2)}) copy-start(s32[3,64,64]{2,1,0:T(8,128)} %param.11) | copy-start | bytes 147460
  29.6 88.4 %collective-permute-start.14 = (bf16[896,512]{1,0:T(8,128)(2,1)}, bf16[896,512]{1,0:T(8,128)(2,1)}, u32[]{:S(2)}, u32[]{:S(2)}) collective-permute-start(bf16[896,512]{1,0:T(8,128)(2,1)} %get-tuple-element.8), channel_id=1, source_target_pairs={{0,1},{1,2},{2,3},{3,0},{4,5},{5,6},{6,7},{7,4},{8,9},{9,10},{10,1... | collective-permute-start | bytes 2752520 | tf_op jit(solution)/shard_map/ppermute | solution.py:266
  35.7 163.4 %collective-permute-start.5 = (bf16[768,896]{1,0:T(8,128)(2,1)}, bf16[768,896]{1,0:T(8,128)(2,1)}, u32[]{:S(2)}, u32[]{:S(2)}) collective-permute-start(bf16[768,896]{1,0:T(8,128)(2,1)} %pack2.1), channel_id=1, source_target_pairs={{0,2},{1,3},{2,0},{3,1},{4,6},{5,7},{6,4},{7,5},{8,10},{9,11},{10,... | collective-permute-start | bytes 4128776 | tf_op jit(solution)/shard_map/ppermute | solution.py:266
  98.3 102.3 %collective-permute-start.36 = (bf16[512,1024]{1,0:T(8,128)(2,1)}, bf16[512,1024]{1,0:T(8,128)(2,1)}, u32[]{:S(2)}, u32[]{:S(2)}) collective-permute-start(bf16[512,1024]{1,0:T(8,128)(2,1)} %collective-permute-done.20.x0), channel_id=1, source_target_pairs={{0,8},{4,12},{8,0},{12,4},{1,9},{5,13},{9,1},{13,5},{2,10},{6,14},... | collective-permute-start | bytes 3145736 | tf_op jit(solution)/shard_map/ppermute | solution.py:270
  118.0 82.6 %collective-permute-start.21 = (bf16[512,1024]{1,0:T(8,128)(2,1)}, bf16[512,1024]{1,0:T(8,128)(2,1)S(1)}, u32[]{:S(2)}, u32[]{:S(2)}) collective-permute-start(bf16[512,1024]{1,0:T(8,128)(2,1)} %collective-permute-done.20.x0), channel_id=1, source_target_pairs={{0,1},{1,2},{2,3},{3,0},{4,5},{5,6},{6,7},{7,4},{8,9},{9,10},{10,1... | collective-permute-start | bytes 3145736 | tf_op jit(solution)/shard_map/ppermute | solution.py:266
  146.0 92.6 %copy-start.1 = (bf16[768,896]{1,0:T(8,128)(2,1)}, bf16[768,896]{1,0:T(8,128)(2,1)S(1)}, u32[]{:S(2)}) copy-start(bf16[768,896]{1,0:T(8,128)(2,1)S(1)} %collective-permute-done.9.mine_ref) | copy-start | bytes 4128772
  146.0 56.3 %collective-permute-start.10 = (bf16[768,896]{1,0:T(8,128)(2,1)S(1)}, bf16[768,896]{1,0:T(8,128)(2,1)}, u32[]{:S(2)}, u32[]{:S(2)}) collective-permute-start(bf16[768,896]{1,0:T(8,128)(2,1)S(1)} %collective-permute-done.9.mine_ref), channel_id=1, source_target_pairs={{0,16},{16,0},{1,17},{17,1},{2,18},{18,2},{3,19},{19,3},{4,20},{20... | collective-permute-start | bytes 4128776 | tf_op jit(solution)/shard_map/ppermute | solution.py:266
  147.5 54.9 %collective-permute-start.8 = (bf16[768,896]{1,0:T(8,128)(2,1)}, bf16[768,896]{1,0:T(8,128)(2,1)}, u32[]{:S(2)}, u32[]{:S(2)}) collective-permute-start(bf16[768,896]{1,0:T(8,128)(2,1)} %collective-permute-done.7.mine_ref), channel_id=1, source_target_pairs={{0,16},{16,0},{1,17},{17,1},{2,18},{18,2},{3,19},{19,3},{4,20},{20... | collective-permute-start | bytes 4128776 | tf_op jit(solution)/shard_map/ppermute | solution.py:266
  199.1 33.4 %collective-permute-start.6 = (bf16[768,896]{1,0:T(8,128)(2,1)}, bf16[768,896]{1,0:T(8,128)(2,1)}, u32[]{:S(2)}, u32[]{:S(2)}) collective-permute-start(bf16[768,896]{1,0:T(8,128)(2,1)} %collective-permute-done.5.mine_ref), channel_id=1, source_target_pairs={{0,16},{16,0},{1,17},{17,1},{2,18},{18,2},{3,19},{19,3},{4,20},{20... | collective-permute-start | bytes 4128776 | tf_op jit(solution)/shard_map/ppermute | solution.py:266
  200.6 62.6 %collective-permute-start.35 = (bf16[512,1024]{1,0:T(8,128)(2,1)}, bf16[512,1024]{1,0:T(8,128)(2,1)}, u32[]{:S(2)}, u32[]{:S(2)}) collective-permute-start(bf16[512,1024]{1,0:T(8,128)(2,1)} %collective-permute-done.20.x0), channel_id=1, source_target_pairs={{0,4},{4,0},{8,12},{12,8},{1,5},{5,1},{9,13},{13,9},{2,6},{6,2},{1... | collective-permute-start | bytes 3145736 | tf_op jit(solution)/shard_map/ppermute | solution.py:270
  200.6 1.0 copy-start.4
  201.6 61.6 %collective-permute-start.37 = (bf16[512,1024]{1,0:T(8,128)(2,1)}, bf16[512,1024]{1,0:T(8,128)(2,1)}, u32[]{:S(2)}, u32[]{:S(2)}) collective-permute-start(bf16[512,1024]{1,0:T(8,128)(2,1)} %collective-permute-done.36.x2), channel_id=1, source_target_pairs={{0,4},{4,0},{8,12},{12,8},{1,5},{5,1},{9,13},{13,9},{2,6},{6,2},{1... | collective-permute-start | bytes 3145736 | tf_op jit(solution)/shard_map/ppermute | solution.py:270
  202.3 77.2 %collective-permute-start.16 = (bf16[896,512]{1,0:T(8,128)(2,1)}, bf16[896,512]{1,0:T(8,128)(2,1)}, u32[]{:S(2)}, u32[]{:S(2)}) collective-permute-start(bf16[896,512]{1,0:T(8,128)(2,1)} %get-tuple-element.11), channel_id=1, source_target_pairs={{0,2},{1,3},{2,0},{3,1},{4,6},{5,7},{6,4},{7,5},{8,10},{9,11},{10,... | collective-permute-start | bytes 2752520 | tf_op jit(solution)/shard_map/ppermute | solution.py:266
  202.4 77.1 %collective-permute-start.15 = (bf16[896,512]{1,0:T(8,128)(2,1)}, bf16[896,512]{1,0:T(8,128)(2,1)}, u32[]{:S(2)}, u32[]{:S(2)}) collective-permute-start(bf16[896,512]{1,0:T(8,128)(2,1)} %collective-permute-done.14), channel_id=1, source_target_pairs={{0,16},{16,0},{1,17},{17,1},{2,18},{18,2},{3,19},{19,3},{4,20},{20... | collective-permute-start | bytes 2752520 | tf_op jit(solution)/shard_map/ppermute | solution.py:266
  232.5 48.7 %collective-permute-start.30 = (bf16[512,1024]{1,0:T(8,128)(2,1)}, bf16[512,1024]{1,0:T(8,128)(2,1)}, u32[]{:S(2)}, u32[]{:S(2)}) collective-permute-start(bf16[512,1024]{1,0:T(8,128)(2,1)} %copy-done.4), channel_id=1, source_target_pairs={{0,8},{4,12},{8,0},{12,4},{1,9},{5,13},{9,1},{13,5},{2,10},{6,14},... | collective-permute-start | bytes 3145736 | tf_op jit(solution)/shard_map/ppermute | solution.py:270
  256.8 6.4 %copy-start.2 = (bf16[896,512]{1,0:T(8,128)(2,1)S(1)}, bf16[896,512]{1,0:T(8,128)(2,1)}, u32[]{:S(2)}) copy-start(bf16[896,512]{1,0:T(8,128)(2,1)} %get-tuple-element.7) | copy-start | bytes 2752516
  263.2 44.6 %collective-permute-start.18 = (bf16[896,512]{1,0:T(8,128)(2,1)S(1)}, bf16[896,512]{1,0:T(8,128)(2,1)}, u32[]{:S(2)}, u32[]{:S(2)}) collective-permute-start(bf16[896,512]{1,0:T(8,128)(2,1)S(1)} %copy-done.2), channel_id=1, source_target_pairs={{0,3},{1,0},{2,1},{3,2},{4,7},{5,4},{6,5},{7,6},{8,11},{9,8},{10,9... | collective-permute-start | bytes 2752520 | tf_op jit(solution)/shard_map/ppermute | solution.py:266
  263.2 41.9 %collective-permute-start.22 = (bf16[512,1024]{1,0:T(8,128)(2,1)}, bf16[512,1024]{1,0:T(8,128)(2,1)}, u32[]{:S(2)}, u32[]{:S(2)}) collective-permute-start(bf16[512,1024]{1,0:T(8,128)(2,1)} %copy-done.4), channel_id=1, source_target_pairs={{0,1},{1,2},{2,3},{3,0},{4,5},{5,6},{6,7},{7,4},{8,9},{9,10},{10,1... | collective-permute-start | bytes 3145736 | tf_op jit(solution)/shard_map/ppermute | solution.py:266
  279.5 29.8 %collective-permute-start.29 = (bf16[512,1024]{1,0:T(8,128)(2,1)}, bf16[512,1024]{1,0:T(8,128)(2,1)}, u32[]{:S(2)}, u32[]{:S(2)}) collective-permute-start(bf16[512,1024]{1,0:T(8,128)(2,1)} %copy-done.4), channel_id=1, source_target_pairs={{0,4},{4,0},{8,12},{12,8},{1,5},{5,1},{9,13},{13,9},{2,6},{6,2},{1... | collective-permute-start | bytes 3145736 | tf_op jit(solution)/shard_map/ppermute | solution.py:270
  279.5 30.3 %collective-permute-start.39 = (bf16[512,896]{1,0:T(8,128)(2,1)}, bf16[512,896]{1,0:T(8,128)(2,1)}, u32[]{:S(2)}, u32[]{:S(2)}) collective-permute-start(bf16[512,896]{1,0:T(8,128)(2,1)} %gate_up1.1.h0), channel_id=1, source_target_pairs={{0,8},{4,12},{8,0},{12,4},{1,9},{5,13},{9,1},{13,5},{2,10},{6,14},... | collective-permute-start | bytes 2752520 | tf_op jit(solution)/shard_map/ppermute | solution.py:270
  281.2 30.8 %collective-permute-start.31 = (bf16[512,1024]{1,0:T(8,128)(2,1)}, bf16[512,1024]{1,0:T(8,128)(2,1)}, u32[]{:S(2)}, u32[]{:S(2)}) collective-permute-start(bf16[512,1024]{1,0:T(8,128)(2,1)} %collective-permute-done.30.x2), channel_id=1, source_target_pairs={{0,4},{4,0},{8,12},{12,8},{1,5},{5,1},{9,13},{13,9},{2,6},{6,2},{1... | collective-permute-start | bytes 3145736 | tf_op jit(solution)/shard_map/ppermute | solution.py:270
  305.1 43.1 %collective-permute-start.24 = (bf16[512,1024]{1,0:T(8,128)(2,1)}, bf16[512,1024]{1,0:T(8,128)(2,1)S(1)}, u32[]{:S(2)}, u32[]{:S(2)}) collective-permute-start(bf16[512,1024]{1,0:T(8,128)(2,1)} %collective-permute-done.22.x0), channel_id=1, source_target_pairs={{0,8},{4,12},{8,0},{12,4},{1,9},{5,13},{9,1},{13,5},{2,10},{6,14},... | collective-permute-start | bytes 3145736 | tf_op jit(solution)/shard_map/ppermute | solution.py:270
  307.8 23.4 %collective-permute-start.17 = (bf16[896,512]{1,0:T(8,128)(2,1)}, bf16[896,512]{1,0:T(8,128)(2,1)S(1)}, u32[]{:S(2)}, u32[]{:S(2)}) collective-permute-start(bf16[896,512]{1,0:T(8,128)(2,1)} %collective-permute-done.16), channel_id=1, source_target_pairs={{0,16},{16,0},{1,17},{17,1},{2,18},{18,2},{3,19},{19,3},{4,20},{20... | collective-permute-start | bytes 2752520 | tf_op jit(solution)/shard_map/ppermute | solution.py:266
  309.3 37.3 %collective-permute-start.19 = (bf16[896,512]{1,0:T(8,128)(2,1)}, bf16[896,512]{1,0:T(8,128)(2,1)S(1)}, u32[]{:S(2)}, u32[]{:S(2)}) collective-permute-start(bf16[896,512]{1,0:T(8,128)(2,1)} %collective-permute-done.18), channel_id=1, source_target_pairs={{0,16},{16,0},{1,17},{17,1},{2,18},{18,2},{3,19},{19,3},{4,20},{20... | collective-permute-start | bytes 2752520 | tf_op jit(solution)/shard_map/ppermute | solution.py:266
  309.8 36.8 %collective-permute-start.38 = (bf16[512,896]{1,0:T(8,128)(2,1)}, bf16[512,896]{1,0:T(8,128)(2,1)}, u32[]{:S(2)}, u32[]{:S(2)}) collective-permute-start(bf16[512,896]{1,0:T(8,128)(2,1)} %gate_up1.1.h0), channel_id=1, source_target_pairs={{0,4},{4,0},{8,12},{12,8},{1,5},{5,1},{9,13},{13,9},{2,6},{6,2},{1... | collective-permute-start | bytes 2752520 | tf_op jit(solution)/shard_map/ppermute | solution.py:270
  312.0 40.7 %collective-permute-start.40 = (bf16[512,896]{1,0:T(8,128)(2,1)}, bf16[512,896]{1,0:T(8,128)(2,1)}, u32[]{:S(2)}, u32[]{:S(2)}) collective-permute-start(bf16[512,896]{1,0:T(8,128)(2,1)} %collective-permute-done.39.h2), channel_id=1, source_target_pairs={{0,4},{4,0},{8,12},{12,8},{1,5},{5,1},{9,13},{13,9},{2,6},{6,2},{1... | collective-permute-start | bytes 2752520 | tf_op jit(solution)/shard_map/ppermute | solution.py:270
  331.2 31.0 %collective-permute-start.3 = (bf16[512,1024]{1,0:T(8,128)(2,1)}, bf16[512,1024]{1,0:T(8,128)(2,1)}, u32[]{:S(2)}, u32[]{:S(2)}) collective-permute-start(bf16[512,1024]{1,0:T(8,128)(2,1)} %fusion.2.x0), channel_id=1, source_target_pairs={{0,8},{4,12},{8,0},{12,4},{1,9},{5,13},{9,1},{13,5},{2,10},{6,14},... | collective-permute-start | bytes 3145736 | tf_op jit(solution)/shard_map/ppermute | solution.py:270
  346.7 15.8 %collective-permute-start.23 = (bf16[512,1024]{1,0:T(8,128)(2,1)}, bf16[512,1024]{1,0:T(8,128)(2,1)}, u32[]{:S(2)}, u32[]{:S(2)}) collective-permute-start(bf16[512,1024]{1,0:T(8,128)(2,1)} %collective-permute-done.22.x0), channel_id=1, source_target_pairs={{0,4},{4,0},{8,12},{12,8},{1,5},{5,1},{9,13},{13,9},{2,6},{6,2},{1... | collective-permute-start | bytes 3145736 | tf_op jit(solution)/shard_map/ppermute | solution.py:270
  346.7 25.2 %collective-permute-start.33 = (bf16[512,896]{1,0:T(8,128)(2,1)}, bf16[512,896]{1,0:T(8,128)(2,1)}, u32[]{:S(2)}, u32[]{:S(2)}) collective-permute-start(bf16[512,896]{1,0:T(8,128)(2,1)} %gate_up2.1.h0), channel_id=1, source_target_pairs={{0,8},{4,12},{8,0},{12,4},{1,9},{5,13},{9,1},{13,5},{2,10},{6,14},... | collective-permute-start | bytes 2752520 | tf_op jit(solution)/shard_map/ppermute | solution.py:270
  348.2 4.5 copy-start.5
  348.2 24.9 %collective-permute-start.25 = (bf16[512,1024]{1,0:T(8,128)(2,1)S(1)}, bf16[512,1024]{1,0:T(8,128)(2,1)}, u32[]{:S(2)}, u32[]{:S(2)}) collective-permute-start(bf16[512,1024]{1,0:T(8,128)(2,1)S(1)} %collective-permute-done.24.x2), channel_id=1, source_target_pairs={{0,4},{4,0},{8,12},{12,8},{1,5},{5,1},{9,13},{13,9},{2,6},{6,2},{1... | collective-permute-start | bytes 3145736 | tf_op jit(solution)/shard_map/ppermute | solution.py:270
  352.6 34.7 %collective-permute-start.32 = (bf16[512,896]{1,0:T(8,128)(2,1)}, bf16[512,896]{1,0:T(8,128)(2,1)S(1)}, u32[]{:S(2)}, u32[]{:S(2)}) collective-permute-start(bf16[512,896]{1,0:T(8,128)(2,1)} %gate_up2.1.h0), channel_id=1, source_target_pairs={{0,4},{4,0},{8,12},{12,8},{1,5},{5,1},{9,13},{13,9},{2,6},{6,2},{1... | collective-permute-start | bytes 2752520 | tf_op jit(solution)/shard_map/ppermute | solution.py:270
  362.2 48.2 %collective-permute-start.2 = (bf16[512,1024]{1,0:T(8,128)(2,1)}, bf16[512,1024]{1,0:T(8,128)(2,1)S(1)}, u32[]{:S(2)}, u32[]{:S(2)}) collective-permute-start(bf16[512,1024]{1,0:T(8,128)(2,1)} %fusion.2.x0), channel_id=1, source_target_pairs={{0,4},{4,0},{8,12},{12,8},{1,5},{5,1},{9,13},{13,9},{2,6},{6,2},{1... | collective-permute-start | bytes 3145736 | tf_op jit(solution)/shard_map/ppermute | solution.py:270
  362.5 48.0 %collective-permute-start.4 = (bf16[512,1024]{1,0:T(8,128)(2,1)}, bf16[512,1024]{1,0:T(8,128)(2,1)}, u32[]{:S(2)}, u32[]{:S(2)}) collective-permute-start(bf16[512,1024]{1,0:T(8,128)(2,1)} %collective-permute-done.3.x2), channel_id=1, source_target_pairs={{0,4},{4,0},{8,12},{12,8},{1,5},{5,1},{9,13},{13,9},{2,6},{6,2},{1... | collective-permute-start | bytes 3145736 | tf_op jit(solution)/shard_map/ppermute | solution.py:270
  371.8 25.4 %collective-permute-start.41 = (bf16[512,1024]{1,0:T(8,128)(2,1)}, bf16[512,1024]{1,0:T(8,128)(2,1)}, u32[]{:S(2)}, u32[]{:S(2)}) collective-permute-start(bf16[512,1024]{1,0:T(8,128)(2,1)} %down1.1), channel_id=1, source_target_pairs={{0,1},{1,2},{2,3},{3,0},{4,5},{5,6},{6,7},{7,4},{8,9},{9,10},{10,1... | collective-permute-start | bytes 3145736 | tf_op jit(solution)/shard_map/ppermute | solution.py:266
  373.1 24.1 %collective-permute-start.34 = (bf16[512,896]{1,0:T(8,128)(2,1)}, bf16[512,896]{1,0:T(8,128)(2,1)}, u32[]{:S(2)}, u32[]{:S(2)}) collective-permute-start(bf16[512,896]{1,0:T(8,128)(2,1)} %collective-permute-done.33.h2), channel_id=1, source_target_pairs={{0,4},{4,0},{8,12},{12,8},{1,5},{5,1},{9,13},{13,9},{2,6},{6,2},{1... | collective-permute-start | bytes 2752520 | tf_op jit(solution)/shard_map/ppermute | solution.py:270
  387.4 9.8 %copy-start.9 = (bf16[512,896]{1,0:T(8,128)(2,1)}, bf16[512,896]{1,0:T(8,128)(2,1)S(1)}, u32[]{:S(2)}) copy-start(bf16[512,896]{1,0:T(8,128)(2,1)S(1)} %collective-permute-done.32.h1) | copy-start | bytes 2752516
  387.4 23.0 %collective-permute-start.27 = (bf16[512,896]{1,0:T(8,128)(2,1)}, bf16[512,896]{1,0:T(8,128)(2,1)S(1)}, u32[]{:S(2)}, u32[]{:S(2)}) collective-permute-start(bf16[512,896]{1,0:T(8,128)(2,1)} %gate_up3.1.h0), channel_id=1, source_target_pairs={{0,8},{4,12},{8,0},{12,4},{1,9},{5,13},{9,1},{13,5},{2,10},{6,14},... | collective-permute-start | bytes 2752520 | tf_op jit(solution)/shard_map/ppermute | solution.py:270
  397.2 30.0 %collective-permute-start.26 = (bf16[512,896]{1,0:T(8,128)(2,1)}, bf16[512,896]{1,0:T(8,128)(2,1)}, u32[]{:S(2)}, u32[]{:S(2)}) collective-permute-start(bf16[512,896]{1,0:T(8,128)(2,1)} %gate_up3.1.h0), channel_id=1, source_target_pairs={{0,4},{4,0},{8,12},{12,8},{1,5},{5,1},{9,13},{13,9},{2,6},{6,2},{1... | collective-permute-start | bytes 2752520 | tf_op jit(solution)/shard_map/ppermute | solution.py:270
  406.8 27.6 %collective-permute-start.42 = (bf16[512,1024]{1,0:T(8,128)(2,1)}, bf16[512,1024]{1,0:T(8,128)(2,1)S(1)}, u32[]{:S(2)}, u32[]{:S(2)}) collective-permute-start(bf16[512,1024]{1,0:T(8,128)(2,1)} %down2.1), channel_id=1, source_target_pairs={{0,1},{1,2},{2,3},{3,0},{4,5},{5,6},{6,7},{7,4},{8,9},{9,10},{10,1... | collective-permute-start | bytes 3145736 | tf_op jit(solution)/shard_map/ppermute | solution.py:266
  410.4 15.3 %copy-start.10 = (bf16[512,896]{1,0:T(8,128)(2,1)}, bf16[512,896]{1,0:T(8,128)(2,1)S(1)}, u32[]{:S(2)}) copy-start(bf16[512,896]{1,0:T(8,128)(2,1)S(1)} %collective-permute-done.27.h2) | copy-start | bytes 2752516
  410.4 23.9 %collective-permute-start.28 = (bf16[512,896]{1,0:T(8,128)(2,1)S(1)}, bf16[512,896]{1,0:T(8,128)(2,1)}, u32[]{:S(2)}, u32[]{:S(2)}) collective-permute-start(bf16[512,896]{1,0:T(8,128)(2,1)S(1)} %collective-permute-done.27.h2), channel_id=1, source_target_pairs={{0,4},{4,0},{8,12},{12,8},{1,5},{5,1},{9,13},{13,9},{2,6},{6,2},{1... | collective-permute-start | bytes 2752520 | tf_op jit(solution)/shard_map/ppermute | solution.py:270
  410.4 1.0 copy-start.6
  425.7 23.0 %collective-permute-start.12 = (bf16[512,896]{1,0:T(8,128)(2,1)}, bf16[512,896]{1,0:T(8,128)(2,1)}, u32[]{:S(2)}, u32[]{:S(2)}) collective-permute-start(bf16[512,896]{1,0:T(8,128)(2,1)} %gate_up0.1.h0), channel_id=1, source_target_pairs={{0,8},{4,12},{8,0},{12,4},{1,9},{5,13},{9,1},{13,5},{2,10},{6,14},... | collective-permute-start | bytes 2752520 | tf_op jit(solution)/shard_map/ppermute | solution.py:270
  434.3 1.0 copy-start.7
  435.3 9.6 %copy-start.11 = (bf16[512,896]{1,0:T(8,128)(2,1)S(1)}, bf16[512,896]{1,0:T(8,128)(2,1)}, u32[]{:S(2)}) copy-start(bf16[512,896]{1,0:T(8,128)(2,1)} %gate_up0.1.h0) | copy-start | bytes 2752516
  444.9 26.7 %collective-permute-start.43 = (bf16[512,1024]{1,0:T(8,128)(2,1)}, bf16[512,1024]{1,0:T(8,128)(2,1)S(1)}, u32[]{:S(2)}, u32[]{:S(2)}) collective-permute-start(bf16[512,1024]{1,0:T(8,128)(2,1)} %down3.1), channel_id=1, source_target_pairs={{0,1},{1,2},{2,3},{3,0},{4,5},{5,6},{6,7},{7,4},{8,9},{9,10},{10,1... | collective-permute-start | bytes 3145736 | tf_op jit(solution)/shard_map/ppermute | solution.py:266
  444.9 3.8 collective-permute-start.11
  448.7 2.8 collective-permute-start.13
  448.7 22.9 %copy-start.12 = (bf16[512,896]{1,0:T(8,128)(2,1)}, bf16[512,896]{1,0:T(8,128)(2,1)S(1)}, u32[]{:S(2)}) copy-start(bf16[512,896]{1,0:T(8,128)(2,1)S(1)} %collective-permute-done.11.h1) | copy-start | bytes 2752516
  471.7 1.0 copy-start.8

commit v2 on v1

v2 whole, which is shorter than its diff:
```python
import jax
import jax.numpy as jnp
from jax import lax
from jax.experimental import pallas as pl
from jax.experimental.pallas import tpu as pltpu
from jax.sharding import PartitionSpec as P


F32 = jnp.float32
BF16 = jnp.bfloat16


def masked_tile(weight, mask, col_at, row_at, n_col, n_row):
    per_col = mask.shape[0] // n_col
    per_row = mask.shape[1] // n_row
    tile = lax.dynamic_slice(mask, (col_at * per_col, row_at * per_row), (per_col, per_row))
    tall = weight.shape[0] // per_col
    broad = weight.shape[1] // per_row
    shaped = (
        weight.reshape(per_col, tall, per_row, broad) * tile.astype(weight.dtype)[:, None, :, None]
    )
    return shaped.reshape(weight.shape)


def plain_body(tokens, norm_gain, gate_weight, up_weight, down_weight, block_mask):
    n_row = lax.axis_size("row")
    n_col = lax.axis_size("col")
    row_at = lax.axis_index("row")
    col_at = lax.axis_index("col")
    whole = lax.all_gather(tokens, "row", axis=1, tiled=True)
    values = whole.astype(F32)
    square_mean = jnp.mean(values * values, axis=-1, keepdims=True)
    normed = (values * lax.rsqrt(square_mean + 1e-05) * norm_gain.astype(F32)).astype(BF16)
    gate_tile = masked_tile(gate_weight, block_mask[0], col_at, row_at, n_col, n_row)
    up_tile = masked_tile(up_weight, block_mask[1], col_at, row_at, n_col, n_row)
    gate = jnp.dot(
        normed, lax.all_gather(gate_tile, "col", axis=0, tiled=True), preferred_element_type=F32
    )
    up = jnp.dot(
        normed, lax.all_gather(up_tile, "col", axis=0, tiled=True), preferred_element_type=F32
    )
    hidden = (jax.nn.silu(gate) * up).astype(BF16)
    down_tile = masked_tile(down_weight, block_mask[2], col_at, row_at, n_col, n_row)
    down_full = lax.all_gather(down_tile, "col", axis=0, tiled=True)
    mixed = jnp.dot(
        lax.all_gather(hidden, "row", axis=1, tiled=True), down_full, preferred_element_type=F32
    )
    return mixed.astype(BF16)


def cap_of(per_col):
    return per_col * 3 // 4


def lane_parts(tile, broad):
    first = tile * 128 // broad
    last = (tile * 128 + 127) // broad
    return first, last, last * broad - tile * 128


def pack(gate_weight, up_weight, table, where_at, m, per_col, per_row, n_col, n_blocks):
    rows, cols = gate_weight.shape
    width = cols // n_col
    tall = rows // per_col
    broad = cols // per_row
    cap = cap_of(per_col)
    per_dest = per_row // n_col
    half = cap // 2

    def kernel(table_ref, at_ref, gate_ref, up_ref, low_ref, high_ref):
        group, row, col = at_ref[0], at_ref[1], at_ref[2]
        left = row * per_row + (row ^ col ^ m) * per_dest

        def copy_from(src):
            for side, out_ref in enumerate((low_ref, high_ref)):

                @pl.loop(0, half)
                def _(step):
                    slot = step + side * half
                    base = ((group * n_col + col) * cap + slot) * n_blocks + left
                    to = pl.ds(pl.multiple_of(step * tall, tall), tall)
                    for tile in range(width // 128):
                        first, last, cut = lane_parts(tile, broad)
                        lanes = slice(tile * 128, tile * 128 + 128)
                        at = table_ref[base + first]
                        val = src[pl.ds(pl.multiple_of(at * tall, tall), tall), lanes]
                        if last != first:
                            lane = lax.broadcasted_iota(jnp.int32, (1, 128), 1)
                            early = (lane < cut).astype(F32)
                            at = table_ref[base + last]
                            val2 = src[pl.ds(pl.multiple_of(at * tall, tall), tall), lanes]
                            val = val * early.astype(BF16) + val2 * (1.0 - early).astype(BF16)
                        out_ref[to, lanes] = val

        @pl.when(group == 0)
        def _():
            copy_from(gate_ref)

        @pl.when(group != 0)
        def _():
            copy_from(up_ref)

    spec = pl.BlockSpec((rows, width), lambda i, table, at: (0, at[1] ^ at[2] ^ m))
    shape = (half * tall, width)
    return pl.pallas_call(
        kernel,
        grid_spec=pltpu.PrefetchScalarGridSpec(
            num_scalar_prefetch=2,
            grid=(1,),
            in_specs=[spec, spec],
            out_specs=[pl.BlockSpec(shape, lambda i, table, at: (0, 0))] * 2,
        ),
        out_shape=[jax.ShapeDtypeStruct(shape, BF16)] * 2,
        cost_estimate=pl.CostEstimate(flops=0, bytes_accessed=6 * rows * width, transcendentals=0),
    )(table, where_at, gate_weight, up_weight)


def expand(mine, other, slots, where_at, m, dense, sizes):
    rows, width, per_col, per_row, n_col, n_blocks = sizes
    tall = rows // per_col
    per_dest = per_row // n_col
    broad = width // per_dest
    part_rows = mine[0].shape[0]

    def kernel(slots_ref, at_ref, *refs):
        parts, out_ref, held, sems = refs[:4], refs[-3], refs[-2], refs[-1]
        copies = [
            pltpu.make_async_copy(
                part, held.at[i // 2, pl.ds((i % 2) * part_rows, part_rows)], sems.at[i]
            )
            for i, part in enumerate(parts)
        ]
        for copy in copies:
            copy.start()
        for copy in copies:
            copy.wait()
        group, row, col = at_ref[0], at_ref[1], at_ref[2]
        source = row ^ col ^ m
        left = col * per_row + row * per_dest

        @pl.loop(0, per_col)
        def _(block):
            to = pl.ds(pl.multiple_of(block * tall, tall), tall)
            for which in range(2):
                matrix = group if which == 0 else 1 - group
                base = ((matrix * n_col + source) * per_col + block) * n_blocks + left
                for tile in range(width // 128):
                    first, last, cut = lane_parts(tile, broad)
                    lanes = slice(tile * 128, tile * 128 + 128)
                    total = None
                    for part in range(first, last + 1):
                        slot = slots_ref[base + part]
                        keep = jnp.where(slot >= 0, 1.0, 0.0).astype(F32)
                        at = jnp.maximum(slot, 0)
                        val = held[which, pl.ds(pl.multiple_of(at * tall, tall), tall), lanes]
                        weight = jnp.full((1, 128), keep, F32)
                        if last != first:
                            lane = lax.broadcasted_iota(jnp.int32, (1, 128), 1)
                            side = lane < cut if part == first else lane >= cut
                            weight = jnp.where(side, weight, 0.0)
                        val = val * weight.astype(BF16)
                        total = val if total is None else total + val
                    start = tile * 256 + which * 128
                    out_ref[0, to, start : start + 128] = total

    args = [slots, where_at, *mine, *other]
    any_spec = pl.BlockSpec(memory_space=pl.ANY)
    specs = [any_spec] * 4
    aliases = {}
    if dense is not None:
        args.append(dense)
        specs.append(any_spec)
        aliases = {6: 0}
    return pl.pallas_call(
        kernel,
        grid_spec=pltpu.PrefetchScalarGridSpec(
            num_scalar_prefetch=2,
            grid=(1,),
            in_specs=specs,
            out_specs=pl.BlockSpec(
                (1, rows, 2 * width), lambda i, slots, at: (at[1] ^ at[2] ^ m, 0, 0)
            ),
            scratch_shapes=[
                pltpu.VMEM((2, 2 * part_rows, width), BF16),
                pltpu.SemaphoreType.DMA((4,)),
            ],
        ),
        out_shape=jax.ShapeDtypeStruct((n_col, rows, 2 * width), BF16),
        input_output_aliases=aliases,
        cost_estimate=pl.CostEstimate(flops=0, bytes_accessed=8 * rows * width, transcendentals=0),
    )(*args)


def norm_of(pieces, gain, where_at):
    tokens, depth = pieces[0].shape
    tall = tokens // 4

    def kernel(at_ref, p0, p1, p2, p3, gain_ref, out_ref):
        row = at_ref[1]
        parts = [p[...].astype(F32) for p in (p0, p1, p2, p3)]
        squares = sum(jnp.sum(v * v, axis=-1, keepdims=True) for v in parts)
        scale = lax.rsqrt(squares / (4 * depth) + 1e-05)
        for m, v in enumerate(parts):
            at = row ^ m
            normed = v * scale * gain_ref[at].astype(F32)
            out_ref[:, pl.ds(pl.multiple_of(at * depth, 128), depth)] = normed.astype(BF16)

    return pl.pallas_call(
        kernel,
        grid_spec=pltpu.PrefetchScalarGridSpec(
            num_scalar_prefetch=1,
            grid=(4,),
            in_specs=[pl.BlockSpec((tall, depth), lambda n, at: (n, 0))] * 4
            + [pl.BlockSpec((4, 1, depth), lambda n, at: (0, 0, 0))],
            out_specs=pl.BlockSpec((tall, 4 * depth), lambda n, at: (n, 0)),
        ),
        out_shape=jax.ShapeDtypeStruct((tokens, 4 * depth), BF16),
        cost_estimate=pl.CostEstimate(
            flops=4 * tokens * depth * 4, bytes_accessed=16 * tokens * depth, transcendentals=tokens
        ),
    )(where_at, *pieces, gain.reshape(4, 1, depth))


def mask_down(weight, wide):
    blocks, _, cols = wide.shape
    tall = weight.shape[0] // blocks

    def kernel(w_ref, mask_ref, out_ref):
        out_ref[...] = w_ref[...] * mask_ref[0]

    return pl.pallas_call(
        kernel,
        grid=(blocks,),
        in_specs=[
            pl.BlockSpec((tall, cols), lambda n: (n, 0)),
            pl.BlockSpec((1, 1, cols), lambda n: (n, 0, 0)),
        ],
        out_specs=pl.BlockSpec((tall, cols), lambda n: (n, 0)),
        out_shape=jax.ShapeDtypeStruct(weight.shape, BF16),
        cost_estimate=pl.CostEstimate(
            flops=weight.size, bytes_accessed=4 * weight.size, transcendentals=0
        ),
    )(weight, wide)


def gate_up(x, dense, where_at):
    tokens, depth = x.shape
    double = dense.shape[1]
    tiles = double // 256

    def kernel(at_ref, x_ref, w_ref, out_ref):
        total = jnp.dot(x_ref[...], w_ref[...], preferred_element_type=F32)
        mine, other = total[:, :128], total[:, 128:]
        gate = jnp.where(at_ref[0] == 0, mine, other)
        up = jnp.where(at_ref[0] == 0, other, mine)
        out_ref[...] = (gate / (1.0 + jnp.exp(-gate)) * up).astype(BF16)

    return pl.pallas_call(
        kernel,
        grid_spec=pltpu.PrefetchScalarGridSpec(
            num_scalar_prefetch=1,
            grid=(tiles,),
            in_specs=[
                pl.BlockSpec((tokens, depth), lambda n, at: (0, 0)),
                pl.BlockSpec((depth, 256), lambda n, at: (0, n)),
            ],
            out_specs=pl.BlockSpec((tokens, 128), lambda n, at: (0, n)),
        ),
        out_shape=jax.ShapeDtypeStruct((tokens, tiles * 128), BF16),
        cost_estimate=pl.CostEstimate(
            flops=2 * tokens * depth * double,
            bytes_accessed=2 * (tokens * depth + dense.size),
            transcendentals=tokens * tiles * 128,
        ),
    )(where_at, x, dense)


def down_part(pieces, weights, where_at, kind):
    tokens, depth = pieces[0].shape
    n_row, _, cols = weights.shape
    lanes = 256

    def kernel(at_ref, h0, h1, h2, h3, w_ref, out_ref):
        row = at_ref[1]
        total = None
        for m, h in enumerate((h0, h1, h2, h3)):
            part = jnp.dot(h[...], w_ref[row ^ m], preferred_element_type=F32)
            total = part if total is None else total + part
        out_ref[...] = total.astype(kind)

    out_spec = pl.BlockSpec((tokens, lanes), lambda n, at: (0, n))
    return pl.pallas_call(
        kernel,
        grid_spec=pltpu.PrefetchScalarGridSpec(
            num_scalar_prefetch=1,
            grid=(cols // lanes,),
            in_specs=[pl.BlockSpec((tokens, depth), lambda n, at: (0, 0))] * 4
            + [pl.BlockSpec((n_row, depth, lanes), lambda n, at: (0, 0, n))],
            out_specs=out_spec,
        ),
        out_shape=jax.ShapeDtypeStruct((tokens, cols), kind),
        cost_estimate=pl.CostEstimate(
            flops=2 * tokens * n_row * depth * cols,
            bytes_accessed=2 * (4 * tokens * depth + weights.size + tokens * cols * 2),
            transcendentals=0,
        ),
    )(where_at, *pieces, weights)


def body(*args):
    return layer(*args)


def layer(tokens, norm_gain, gate_weight, up_weight, down_weight, block_mask):
    n_row = lax.axis_size("row")
    n_col = lax.axis_size("col")
    group = lax.axis_index("group")
    row = lax.axis_index("row")
    col = lax.axis_index("col")
    n_blocks = block_mask.shape[-1]
    per_col = n_blocks // n_col
    per_row = n_blocks // n_row
    cap = cap_of(per_col)
    rows, cols = gate_weight.shape
    width = cols // n_col

    def beside(by):
        return [(i, i ^ by) for i in range(n_col)]

    swap = [(0, 1), (1, 0)]
    core = [(i, i ^ 1) for i in range(n_row)]
    across = [(i, i ^ 2) for i in range(n_row)]
    grid = [(r, c) for r in range(n_row) for c in range(n_col)]

    def in_plane(m):
        return [(r * n_col + c, (r ^ c ^ m) * n_col + c) for r, c in grid if c != m]

    def to_plane(m):
        return [(r * n_col + c, r * n_col + (r ^ c ^ m)) for r, c in grid if r != m]

    three = lax.iota(jnp.int32, 3)
    where_at = jnp.where(three == 0, group, jnp.where(three == 1, row, col)).astype(jnp.int32)
    grouped = block_mask[:2].reshape(2, n_col, per_col, n_blocks)
    ids = jnp.arange(per_col, dtype=jnp.int32)
    before = (ids[None, :] < ids[:, None]).astype(jnp.int32)
    rank = jnp.sum(before[None, None, :, :, None] * grouped[:, :, None, :, :], axis=3)
    slots = jnp.where(grouped > 0, rank, -1).astype(jnp.int32)
    wanted = jnp.arange(cap, dtype=jnp.int32)
    table = jnp.sum(
        jnp.where(
            slots[:, :, None, :, :] == wanted[None, None, :, None, None],
            ids[None, None, None, :, None],
            0,
        ),
        axis=3,
    ).astype(jnp.int32)
    slots = slots.reshape(-1)
    table = table.reshape(-1)

    far = lax.ppermute(tokens, "col", beside(2))
    near = lax.ppermute(tokens, "col", beside(1))
    shards = [tokens, near, far, lax.ppermute(far, "col", beside(1))]

    def over_row(v):
        far = lax.ppermute(v, "row", across)
        return v, lax.ppermute(v, "row", core), far, lax.ppermute(far, "row", core)

    normed = [norm_of(over_row(v), norm_gain, where_at) for v in shards]

    sizes = (rows, width, per_col, per_row, n_col, n_blocks)
    order = [0, 2, 1, 3]
    got = {}
    for m in order:
        halves = pack(gate_weight, up_weight, table, where_at, m, per_col, per_row, n_col, n_blocks)
        got[m] = []
        for v in halves:
            v = jnp.where(col == m, v, lax.ppermute(v, ("row", "col"), in_plane(m)))
            came = lax.ppermute(v, ("row", "col"), to_plane(m))
            v = jnp.where(row == m, v, came)
            got[m].append((v, lax.ppermute(v, "group", swap)))
    dense = None
    for m in order:
        (a, b), (c, d) = got[m]
        dense = expand((a, c), (b, d), slots, where_at, m, dense, sizes)
    dense = dense.reshape(-1, dense.shape[-1])

    tile = lax.dynamic_slice(block_mask[2], (col * per_col, row * per_row), (per_col, per_row))
    wide = jnp.repeat(tile.astype(BF16), down_weight.shape[1] // per_row, axis=1)
    weights = mask_down(down_weight, wide[:, None, :])
    weights = weights.reshape(n_row, -1, down_weight.shape[1])

    def part_of(j, kind):
        hidden = gate_up(normed[j], dense, where_at)
        return down_part(over_row(hidden), weights, where_at, kind)

    passing = lax.ppermute(part_of(3, BF16), "col", beside(1))
    passing = (part_of(2, F32) + passing.astype(F32)).astype(BF16)
    passing = lax.ppermute(passing, "col", beside(2))
    close = lax.ppermute(part_of(1, BF16), "col", beside(1))
    return (part_of(0, F32) + passing.astype(F32) + close.astype(F32)).astype(BF16)


def solution(mesh):
    in_specs = (
        P(("group", "col"), "row"),
        P(),
        P("col", "row"),
        P("col", "row"),
        P("col", "row"),
        P(),
    )
    out_specs = P(("group", "col"), "row")
    sizes = dict(mesh.shape)
    fits = sizes["row"] == 4 and sizes["col"] == 4 and sizes["group"] == 2

    def step(tokens, norm_gain, gate_weight, up_weight, down_weight, block_mask):
        lanes = gate_weight.shape[1] // (sizes["row"] * sizes["col"])
        chosen = body if fits and lanes % 128 == 0 else plain_body
        return jax.shard_map(
            chosen, mesh=mesh, in_specs=in_specs, out_specs=out_specs, check_vma=False
        )(tokens, norm_gain, gate_weight, up_weight, down_weight, block_mask)

    return step
```

time: 484 us -> 562 us (1.16)
  starting transfers between devices: 62.6 us -> 153 us
  waiting for transfers between devices: 251 us -> 200 us
  Pallas kernels: 134 us -> 176 us
  local copies, waits for them, and re-layouts: 18.7 us -> 8.26 us
    ppermute x44 -> x54, starting transfers between devices: 62.6 us -> 153 us  [the longest x8 66.6 us: over_row(): far = lax.ppermute(v, 'row', across)]
    ppermute x44 -> x54, waiting for transfers between devices: 251 us -> 200 us  [the longest x8 51.5 us: layer(): came = lax.ppermute(v, ('row', 'col'), to_plane(m))]
    pallas_call x0 -> x5, Pallas kernels: none -> 37.3 us  [the longest x4 25.7 us: norm_of(): pl.pallas_call(kernel, grid_spec=pltpu.PrefetchScalarGridSpec(num_scalar_...]
    unnamed x33 -> x68, local copies, waits for them, and re-layouts: 15.7 us -> 5.12 us
    select_n x4 -> x19, other arithmetic: 6.61 us -> 13.5 us  [the longest x8 6.41 us: layer(): v = jnp.where(row == m, v, came)]
    pallas_call x3 -> x4, Pallas kernels: 14.2 us -> 19 us  [pack(): pl.pallas_call(kernel, grid_spec=pltpu.PrefetchScalarGridSpec(num_scalar_...]
  transfers between devices with their start and end apart: 44 -> 54, of which waited for: 15 -> 16; matrix products, arithmetic and copies ran while one was open for 6% -> 3% of each run, Pallas kernels for 26% -> 31%
where the time goes in v2:
time: 562 us; the launch traced here: 558 us
  waiting for transfers between devices  200 us (36%)
  Pallas kernels  176 us (31%)
  starting transfers between devices  153 us (27%)
  other arithmetic  20 us (4%)
  local copies, waits for them, and re-layouts  8.26 us (1%)
    ppermute x8, starting transfers between devices, over_row(): far = lax.ppermute(v, 'row', across)  66.6 us
    pallas_call x4, Pallas kernels, gate_up(): pl.pallas_call(kernel, grid_spec=pltpu.PrefetchScalarGridSpec(num_scalar_...  57.3 us
    ppermute x8, waiting for transfers between devices, layer(): came = lax.ppermute(v, ('row', 'col'), to_plane(m))  51.5 us
    ppermute x8, waiting for transfers between devices, layer(): got[m].append((v, lax.ppermute(v, 'group', swap)))  48.2 us
    ppermute x8, waiting for transfers between devices, layer(): v = jnp.where(col == m, v, lax.ppermute(v, ('row', 'col'), in_plane(m)))  39.2 us
    pallas_call x4, Pallas kernels, down_part(): pl.pallas_call(kernel, grid_spec=pltpu.PrefetchScalarGridSpec(num_scalar_...  38.2 us
    pallas_call x4, Pallas kernels, norm_of(): pl.pallas_call(kernel, grid_spec=pltpu.PrefetchScalarGridSpec(num_scalar_...  25.7 us
    ppermute x1, waiting for transfers between devices, layer(): close = lax.ppermute(part_of(1, BF16), 'col', beside(1))  25.4 us
  transfers between devices with their start and end apart: 54, of which 16 were waited for; matrix products, arithmetic and copies ran while one was open for 3% of the time, Pallas kernels for 31%

profile of v2, /device:TPU:0, one launch (start us, length us, event | category | flops | bytes accessed | tf_op | source)
XLA Modules:
  0.0 558.5 jit_solution(4416360734898658080)
XLA Ops:
  3.5 4.7 shard_map.68
  8.9 1.5 collective-permute-start.23
  10.4 4.8 shard_map.67
  15.2 4.9 collective-permute-start.15
  20.1 1.9 collective-permute-start.17
  22.0 4.7 shard_map.66
  26.7 1.9 collective-permute-start.9
  28.7 4.8 shard_map.65
  34.4 2.4 collective-permute-start.11
  38.0 3.5 collective-permute-start.3
  41.7 9.1 %collective-permute-start.30 = (bf16[512,1024]{1,0:T(8,128)(2,1)}, bf16[512,1024]{1,0:T(8,128)(2,1)}, u32[]{:S(2)}, u32[]{:S(2)}) collective-permute-start(bf16[512,1024]{1,0:T(8,128)(2,1)} %p0.1), channel_id=1, source_target_pairs={{0,2},{1,3},{2,0},{3,1},{4,6},{5,7},{6,4},{7,5},{8,10},{9,11},{10,... | collective-permute-start | bytes 3145736 | tf_op jit(solution)/shard_map/ppermute | solution.py:360
  51.4 2.0 collective-permute-start.1
  53.4 1.9 collective-permute-start.5
  57.9 7.7 %collective-permute-done.3 = bf16[384,896]{1,0:T(8,128)(2,1)S(1)} collective-permute-done((bf16[384,896]{1,0:T(8,128)(2,1)}, bf16[384,896]{1,0:T(8,128)(2,1)S(1)}, u32[]{:S(2)}, u32[]{:S(2)}) %collective-permute-start.3) | collective-permute-done | bytes 688160 | tf_op jit(solution)/shard_map/ppermute | solution.py:377
  65.7 4.2 collective-permute-start.46
  71.1 30.7 %collective-permute-done.5 = bf16[384,896]{1,0:T(8,128)(2,1)S(1)} collective-permute-done((bf16[384,896]{1,0:T(8,128)(2,1)}, bf16[384,896]{1,0:T(8,128)(2,1)S(1)}, u32[]{:S(2)}, u32[]{:S(2)}) %collective-permute-start.5) | collective-permute-done | bytes 688160 | tf_op jit(solution)/shard_map/ppermute | solution.py:377
  103.3 1.9 collective-permute-start.16
  105.4 4.8 collective-permute-start.18
  110.3 15.1 %collective-permute-done.46.p0 = bf16[512,1024]{1,0:T(8,128)(2,1)S(1)} collective-permute-done((bf16[512,1024]{1,0:T(8,128)(2,1)}, bf16[512,1024]{1,0:T(8,128)(2,1)S(1)}, u32[]{:S(2)}, u32[]{:S(2)}) %collective-permute-start.46) | collective-permute-done | bytes 1048608 | tf_op jit(solution)/shard_map/ppermute | solution.py:361
  125.4 1.9 collective-permute-start.10
  127.4 3.9 collective-permute-start.12
  131.4 1.9 collective-permute-start.4
  133.3 13.4 %collective-permute-done.16 = bf16[384,896]{1,0:T(8,128)(2,1)S(1)} collective-permute-done((bf16[384,896]{1,0:T(8,128)(2,1)S(1)}, bf16[384,896]{1,0:T(8,128)(2,1)S(1)}, u32[]{:S(2)}, u32[]{:S(2)}) %collective-permute-start.16) | collective-permute-done | bytes 688160 | tf_op jit(solution)/shard_map/ppermute | solution.py:378
  146.7 1.9 collective-permute-start.6
  149.6 28.4 %collective-permute-done.18 = bf16[384,896]{1,0:T(8,128)(2,1)S(1)} collective-permute-done((bf16[384,896]{1,0:T(8,128)(2,1)S(1)}, bf16[384,896]{1,0:T(8,128)(2,1)S(1)}, u32[]{:S(2)}, u32[]{:S(2)}) %collective-permute-start.18) | collective-permute-done | bytes 688160 | tf_op jit(solution)/shard_map/ppermute | solution.py:378
  178.2 1.5 collective-permute-start.25
  179.7 9.7 %collective-permute-done.12 = bf16[384,896]{1,0:T(8,128)(2,1)S(1)} collective-permute-done((bf16[384,896]{1,0:T(8,128)(2,1)S(1)}, bf16[384,896]{1,0:T(8,128)(2,1)S(1)}, u32[]{:S(2)}, u32[]{:S(2)}) %collective-permute-start.12) | collective-permute-done | bytes 688160 | tf_op jit(solution)/shard_map/ppermute | solution.py:378
  197.5 5.1 collective-permute-done.26.refs_3_
  204.2 13.2 %collective-permute-done.19.refs_2_ = bf16[384,896]{1,0:T(8,128)(2,1)} collective-permute-done((bf16[384,896]{1,0:T(8,128)(2,1)S(1)}, bf16[384,896]{1,0:T(8,128)(2,1)}, u32[]{:S(2)}, u32[]{:S(2)}) %collective-permute-start.19) | collective-permute-done | bytes 688160 | tf_op jit(solution)/shard_map/ppermute | solution.py:380
  217.4 31.1 %collective-permute-start.32 = (bf16[512,1024]{1,0:T(8,128)(2,1)}, bf16[512,1024]{1,0:T(8,128)(2,1)}, u32[]{:S(2)}, u32[]{:S(2)}) collective-permute-start(bf16[512,1024]{1,0:T(8,128)(2,1)} %collective-permute-done.30.p0), channel_id=1, source_target_pairs={{0,8},{4,12},{8,0},{12,4},{1,9},{5,13},{9,1},{13,5},{2,10},{6,14},... | collective-permute-start | bytes 3145736 | tf_op jit(solution)/shard_map/ppermute | solution.py:365
  248.5 9.1 %collective-permute-start.2 = (bf16[512,1024]{1,0:T(8,128)(2,1)}, bf16[512,1024]{1,0:T(8,128)(2,1)}, u32[]{:S(2)}, u32[]{:S(2)}) collective-permute-start(bf16[512,1024]{1,0:T(8,128)(2,1)} %copy-done.13), channel_id=1, source_target_pairs={{0,4},{4,0},{8,12},{12,8},{1,5},{5,1},{9,13},{13,9},{2,6},{6,2},{1... | collective-permute-start | bytes 3145736 | tf_op jit(solution)/shard_map/ppermute | solution.py:366
  257.6 13.9 %collective-permute-start.39 = (bf16[512,1024]{1,0:T(8,128)(2,1)}, bf16[512,1024]{1,0:T(8,128)(2,1)}, u32[]{:S(2)}, u32[]{:S(2)}) collective-permute-start(bf16[512,1024]{1,0:T(8,128)(2,1)} %collective-permute-done.37.p0), channel_id=1, source_target_pairs={{0,8},{4,12},{8,0},{12,4},{1,9},{5,13},{9,1},{13,5},{2,10},{6,14},... | collective-permute-start | bytes 3145736 | tf_op jit(solution)/shard_map/ppermute | solution.py:365
  274.2 1.6 collective-permute-start.7
  276.3 16.3 %collective-permute-done.7.refs_2_ = bf16[384,896]{1,0:T(8,128)(2,1)S(1)} collective-permute-done((bf16[384,896]{1,0:T(8,128)(2,1)S(1)}, bf16[384,896]{1,0:T(8,128)(2,1)S(1)}, u32[]{:S(2)}, u32[]{:S(2)}) %collective-permute-start.7) | collective-permute-done | bytes 688160 | tf_op jit(solution)/shard_map/ppermute | solution.py:380
  292.6 13.5 %collective-permute-done.8.refs_3_ = bf16[384,896]{1,0:T(8,128)(2,1)S(1)} collective-permute-done((bf16[384,896]{1,0:T(8,128)(2,1)S(1)}, bf16[384,896]{1,0:T(8,128)(2,1)S(1)}, u32[]{:S(2)}, u32[]{:S(2)}) %collective-permute-start.8) | collective-permute-done | bytes 688160 | tf_op jit(solution)/shard_map/ppermute | solution.py:380
  306.9 15.5 %collective-permute-start.48 = (bf16[512,1024]{1,0:T(8,128)(2,1)}, bf16[512,1024]{1,0:T(8,128)(2,1)}, u32[]{:S(2)}, u32[]{:S(2)}) collective-permute-start(bf16[512,1024]{1,0:T(8,128)(2,1)} %copy-done.11), channel_id=1, source_target_pairs={{0,8},{4,12},{8,0},{12,4},{1,9},{5,13},{9,1},{13,5},{2,10},{6,14},... | collective-permute-start | bytes 3145736 | tf_op jit(solution)/shard_map/ppermute | solution.py:365
  322.4 3.9 collective-permute-start.33
  329.1 6.2 %shard_map.69.refs_4_ = bf16[4,1024,1792]{2,1,0:T(8,128)(2,1)} custom-call(s32[8192]{0:T(1024)} %broadcast_select_fusion.16.slots_ref, s32[3]{0:T(128)} %compare_select_fusion.2.at_ref, bf16[384,896]{1,0:T(8,128)(2,1)} %copy-done.6, bf16[384,896]{1,0:T(8,128)(2,1)} %broadcast_select_fusion.2.refs_1_, bf16[384,896]{1,0:T(8,128)(2,1)} %collective-permute-done.25.refs_2_, ...), custom_call_target="tpu_custom_call" | custom-call | bytes 7340032 | tf_op jit(solution)/shard_map/pallas_call | solution.py:174
  335.3 6.1 %shard_map.70.refs_4_ = bf16[4,1024,1792]{2,1,0:T(8,128)(2,1)} custom-call(s32[8192]{0:T(1024)} %broadcast_select_fusion.16.slots_ref, s32[3]{0:T(128)} %compare_select_fusion.2.at_ref, bf16[384,896]{1,0:T(8,128)(2,1)} %copy-done, bf16[384,896]{1,0:T(8,128)(2,1)} %copy-done.1, ...), custom_call_target="tpu_custom_call", output_to_operand_aliasing={{}: (6, {})} | custom-call | bytes 7340032 | tf_op jit(solution)/shard_map/pallas_call | solution.py:174
  341.5 6.2 %shard_map.71.refs_4_ = bf16[4,1024,1792]{2,1,0:T(8,128)(2,1)} custom-call(s32[8192]{0:T(1024)} %broadcast_select_fusion.16.slots_ref, s32[3]{0:T(128)} %compare_select_fusion.2.at_ref, bf16[384,896]{1,0:T(8,128)(2,1)} %copy-done.2, bf16[384,896]{1,0:T(8,128)(2,1)} %copy-done.3, ...), custom_call_target="tpu_custom_call", output_to_operand_aliasing={{}: (6, {})} | custom-call | bytes 7340032 | tf_op jit(solution)/shard_map/pallas_call | solution.py:174
  347.7 6.2 %shard_map.72 = bf16[4,1024,1792]{2,1,0:T(8,128)(2,1)} custom-call(s32[8192]{0:T(1024)} %broadcast_select_fusion.16.slots_ref, s32[3]{0:T(128)} %compare_select_fusion.2.at_ref, bf16[384,896]{1,0:T(8,128)(2,1)} %copy-done.4, bf16[384,896]{1,0:T(8,128)(2,1)} %copy-done.5, bf16[384,896]{1,0:T(8,128)(2,1)} %copy-done.17, ...), custom_call_target="tpu_custom_call", output_to_operand_aliasing={{}: (6, {})} | custom-call | bytes 7340032 | tf_op jit(solution)/shard_map/pallas_call | solution.py:174
  353.9 6.6 %shard_map.64.x_ref = bf16[512,4096]{1,0:T(8,128)(2,1)} custom-call(s32[3]{0:T(128)} %compare_select_fusion.2.at_ref, bf16[512,1024]{1,0:T(8,128)(2,1)} %p0.1, bf16[512,1024]{1,0:T(8,128)(2,1)} %copy-done.14, bf16[512,1024]{1,0:T(8,128)(2,1)} %copy-done.13, bf16[512,1024]{1,0:T(8,128)(2,1)} %collective-permute-done.2.p3, bf16[4,1,1024]{2,1,0:T(2,128)(2,1)} %reshape.50.gain_ref), custom_call_target="tpu_custom_call" | custom-call | flops 8388608 | bytes 8388608 | tf_op jit(solution)/shard_map/pallas_call | solution.py:208
  361.0 6.4 %shard_map.76.x_ref = bf16[512,4096]{1,0:T(8,128)(2,1)} custom-call(s32[3]{0:T(128)} %compare_select_fusion.2.at_ref, bf16[512,1024]{1,0:T(8,128)(2,1)} %collective-permute-done.30.p0, bf16[512,1024]{1,0:T(8,128)(2,1)} %collective-permute-done.31.p1, bf16[512,1024]{1,0:T(8,128)(2,1)} %collective-permute-done.32.p2, ...), custom_call_target="tpu_custom_call" | custom-call | flops 8388608 | bytes 8388608 | tf_op jit(solution)/shard_map/pallas_call | solution.py:208
  367.4 6.4 %shard_map.79.x_ref = bf16[512,4096]{1,0:T(8,128)(2,1)} custom-call(s32[3]{0:T(128)} %compare_select_fusion.2.at_ref, bf16[512,1024]{1,0:T(8,128)(2,1)} %collective-permute-done.37.p0, bf16[512,1024]{1,0:T(8,128)(2,1)} %collective-permute-done.38.p1, bf16[512,1024]{1,0:T(8,128)(2,1)} %collective-permute-done.39.p2, ...), custom_call_target="tpu_custom_call" | custom-call | flops 8388608 | bytes 8388608 | tf_op jit(solution)/shard_map/pallas_call | solution.py:208
  373.8 14.3 %shard_map.80.h0 = bf16[512,896]{1,0:T(8,128)(2,1)} custom-call(s32[3]{0:T(128)} %compare_select_fusion.2.at_ref, bf16[512,4096]{1,0:T(8,128)(2,1)} %shard_map.79.x_ref, bf16[4096,1792]{1,0:T(8,128)(2,1)} %bitcast.8), custom_call_target="tpu_custom_call" | custom-call | flops 7516192768 | bytes 18874368 | tf_op jit(solution)/shard_map/pallas_call | solution.py:258
  388.4 14.3 %shard_map.77.h0 = bf16[512,896]{1,0:T(8,128)(2,1)} custom-call(s32[3]{0:T(128)} %compare_select_fusion.2.at_ref, bf16[512,4096]{1,0:T(8,128)(2,1)} %shard_map.76.x_ref, bf16[4096,1792]{1,0:T(8,128)(2,1)} %bitcast.9), custom_call_target="tpu_custom_call" | custom-call | flops 7516192768 | bytes 18874368 | tf_op jit(solution)/shard_map/pallas_call | solution.py:258
  402.7 1.7 collective-permute-start.35
  406.5 6.3 %shard_map.82.x_ref = bf16[512,4096]{1,0:T(8,128)(2,1)} custom-call(s32[3]{0:T(128)} %compare_select_fusion.2.at_ref, bf16[512,1024]{1,0:T(8,128)(2,1)} %copy-done.11, bf16[512,1024]{1,0:T(8,128)(2,1)} %copy-done.15, bf16[512,1024]{1,0:T(8,128)(2,1)} %collective-permute-done.48.p2, bf16[512,1024]{1,0:T(8,128)(2,1)} %copy-done.16, ...), custom_call_target="tpu_custom_call" | custom-call | flops 8388608 | bytes 8388608 | tf_op jit(solution)/shard_map/pallas_call | solution.py:208
  412.9 14.4 %shard_map.83.h0 = bf16[512,896]{1,0:T(8,128)(2,1)} custom-call(s32[3]{0:T(128)} %compare_select_fusion.2.at_ref, bf16[512,4096]{1,0:T(8,128)(2,1)} %shard_map.82.x_ref, bf16[4096,1792]{1,0:T(8,128)(2,1)} %bitcast.10), custom_call_target="tpu_custom_call" | custom-call | flops 7516192768 | bytes 18874368 | tf_op jit(solution)/shard_map/pallas_call | solution.py:258
  428.1 14.3 %shard_map.73.h0 = bf16[512,896]{1,0:T(8,128)(2,1)} custom-call(s32[3]{0:T(128)} %compare_select_fusion.2.at_ref, bf16[512,4096]{1,0:T(8,128)(2,1)} %shard_map.64.x_ref, bf16[4096,1792]{1,0:T(8,128)(2,1)} %bitcast.11), custom_call_target="tpu_custom_call" | custom-call | flops 7516192768 | bytes 18874368 | tf_op jit(solution)/shard_map/pallas_call | solution.py:258
  442.4 1.7 collective-permute-start.28
  444.1 6.7 %collective-permute-done.51.h2 = bf16[512,896]{1,0:T(8,128)(2,1)} collective-permute-done((bf16[512,896]{1,0:T(8,128)(2,1)}, bf16[512,896]{1,0:T(8,128)(2,1)}, u32[]{:S(2)}, u32[]{:S(2)}) %collective-permute-start.51) | collective-permute-done | bytes 917536 | tf_op jit(solution)/shard_map/ppermute | solution.py:365
  451.8 11.6 %shard_map.74 = bf16[3584,1024]{1,0:T(8,128)(2,1)} custom-call(bf16[3584,1024]{1,0:T(8,128)(2,1)} %w_ref.1, bf16[16,1,1024]{2,1,0:T(2,128)(2,1)} %broadcast_in_dim_reshape.5.mask_ref), custom_call_target="tpu_custom_call" | custom-call | flops 3670016 | bytes 14680064 | tf_op jit(solution)/shard_map/pallas_call | solution.py:231
  464.0 9.4 %shard_map.81 = bf16[512,1024]{1,0:T(8,128)(2,1)} custom-call(s32[3]{0:T(128)} %compare_select_fusion.2.at_ref, bf16[512,896]{1,0:T(8,128)(2,1)} %shard_map.80.h0, bf16[512,896]{1,0:T(8,128)(2,1)} %collective-permute-done.41.h1, bf16[512,896]{1,0:T(8,128)(2,1)} %collective-permute-done.42.h2, bf16[512,896]{1,0:T(8,128)(2,1)} %collective-permute-done.43.h3, ...), custom_call_target="tpu_custom_call" | custom-call | flops 3758096384 | bytes 13107200 | tf_op jit(solution)/shard_map/pallas_call | solution.py:292
  473.5 6.2 %collective-permute-start.44 = (bf16[512,1024]{1,0:T(8,128)(2,1)}, bf16[512,1024]{1,0:T(8,128)(2,1)S(1)}, u32[]{:S(2)}, u32[]{:S(2)}) collective-permute-start(bf16[512,1024]{1,0:T(8,128)(2,1)} %shard_map.81), channel_id=1, source_target_pairs={{0,1},{1,0},{2,3},{3,2},{4,5},{5,4},{6,7},{7,6},{8,9},{9,8},{10,11... | collective-permute-start | bytes 3145736 | tf_op jit(solution)/shard_map/ppermute | solution.py:396
  480.2 9.4 %shard_map.84 = bf16[512,1024]{1,0:T(8,128)(2,1)} custom-call(s32[3]{0:T(128)} %compare_select_fusion.2.at_ref, bf16[512,896]{1,0:T(8,128)(2,1)} %shard_map.83.h0, bf16[512,896]{1,0:T(8,128)(2,1)} %collective-permute-done.50.h1, bf16[512,896]{1,0:T(8,128)(2,1)} %collective-permute-done.51.h2, bf16[512,896]{1,0:T(8,128)(2,1)} %collective-permute-done.52.h3, ...), custom_call_target="tpu_custom_call" | custom-call | flops 3758096384 | bytes 13107200 | tf_op jit(solution)/shard_map/pallas_call | solution.py:292
  489.7 9.7 %shard_map.78 = f32[512,1024]{1,0:T(8,128)} custom-call(s32[3]{0:T(128)} %compare_select_fusion.2.at_ref, bf16[512,896]{1,0:T(8,128)(2,1)} %shard_map.77.h0, bf16[512,896]{1,0:T(8,128)(2,1)} %collective-permute-done.34.h1, bf16[512,896]{1,0:T(8,128)(2,1)} %collective-permute-done.35.h2, bf16[512,896]{1,0:T(8,128)(2,1)} %collective-permute-done.36.h3, ...), custom_call_target="tpu_custom_call" | custom-call | flops 3758096384 | bytes 13107200 | tf_op jit(solution)/shard_map/pallas_call | solution.py:292
  499.4 4.5 collective-permute-done.44
  503.9 1.9 add_convert_fusion.1
  505.9 4.7 collective-permute-start.45
  510.5 9.7 %shard_map.75 = f32[512,1024]{1,0:T(8,128)} custom-call(s32[3]{0:T(128)} %compare_select_fusion.2.at_ref, bf16[512,896]{1,0:T(8,128)(2,1)} %shard_map.73.h0, bf16[512,896]{1,0:T(8,128)(2,1)} %collective-permute-done.27.h1, bf16[512,896]{1,0:T(8,128)(2,1)} %collective-permute-done.28.h2, bf16[512,896]{1,0:T(8,128)(2,1)} %collective-permute-done.29.h3, ...), custom_call_target="tpu_custom_call" | custom-call | flops 3758096384 | bytes 13107200 | tf_op jit(solution)/shard_map/pallas_call | solution.py:292
  520.2 25.4 %collective-permute-done.53 = bf16[512,1024]{1,0:T(8,128)(2,1)S(1)} collective-permute-done((bf16[512,1024]{1,0:T(8,128)(2,1)}, bf16[512,1024]{1,0:T(8,128)(2,1)S(1)}, u32[]{:S(2)}, u32[]{:S(2)}) %collective-permute-start.53) | collective-permute-done | bytes 1048608 | tf_op jit(solution)/shard_map/ppermute | solution.py:399
  545.7 9.7 %collective-permute-done.45 = bf16[512,1024]{1,0:T(8,128)(2,1)S(1)} collective-permute-done((bf16[512,1024]{1,0:T(8,128)(2,1)S(1)}, bf16[512,1024]{1,0:T(8,128)(2,1)S(1)}, u32[]{:S(2)}, u32[]{:S(2)}) %collective-permute-start.45) | collective-permute-done | bytes 1048608 | tf_op jit(solution)/shard_map/ppermute | solution.py:398
  555.4 3.1 add_convert_fusion
  (168 shorter events, 36.0 us)
Async XLA Ops:
  8.2 25.3 %collective-permute-start.21 = (bf16[384,896]{1,0:T(8,128)(2,1)}, bf16[384,896]{1,0:T(8,128)(2,1)S(1)}, u32[]{:S(2)}, u32[]{:S(2)}) collective-permute-start(bf16[384,896]{1,0:T(8,128)(2,1)} %get-tuple-element.19), channel_id=1, source_target_pairs={{1,5},{2,10},{3,15},{5,1},{6,14},{7,11},{9,13},{10,2},{11,7},{13,9... | collective-permute-start | bytes 2064392 | tf_op jit(solution)/shard_map/ppermute | solution.py:377
  8.9 29.1 %collective-permute-start.23 = (bf16[384,896]{1,0:T(8,128)(2,1)}, bf16[384,896]{1,0:T(8,128)(2,1)}, u32[]{:S(2)}, u32[]{:S(2)}) collective-permute-start(bf16[384,896]{1,0:T(8,128)(2,1)} %get-tuple-element.20), channel_id=1, source_target_pairs={{1,5},{2,10},{3,15},{5,1},{6,14},{7,11},{9,13},{10,2},{11,7},{13,9... | collective-permute-start | bytes 2064392 | tf_op jit(solution)/shard_map/ppermute | solution.py:377
  15.2 26.4 %collective-permute-start.15 = (bf16[384,896]{1,0:T(8,128)(2,1)}, bf16[384,896]{1,0:T(8,128)(2,1)}, u32[]{:S(2)}, u32[]{:S(2)}) collective-permute-start(bf16[384,896]{1,0:T(8,128)(2,1)} %get-tuple-element.17), channel_id=1, source_target_pairs={{0,8},{1,13},{3,7},{4,12},{5,9},{7,3},{8,0},{9,5},{11,15},{12,4},{... | collective-permute-start | bytes 2064392 | tf_op jit(solution)/shard_map/ppermute | solution.py:377
  20.1 31.3 %collective-permute-start.17 = (bf16[384,896]{1,0:T(8,128)(2,1)}, bf16[384,896]{1,0:T(8,128)(2,1)}, u32[]{:S(2)}, u32[]{:S(2)}) collective-permute-start(bf16[384,896]{1,0:T(8,128)(2,1)} %get-tuple-element.18), channel_id=1, source_target_pairs={{0,8},{1,13},{3,7},{4,12},{5,9},{7,3},{8,0},{9,5},{11,15},{12,4},{... | collective-permute-start | bytes 2064392 | tf_op jit(solution)/shard_map/ppermute | solution.py:377
  26.7 26.7 %collective-permute-start.9 = (bf16[384,896]{1,0:T(8,128)(2,1)}, bf16[384,896]{1,0:T(8,128)(2,1)}, u32[]{:S(2)}, u32[]{:S(2)}) collective-permute-start(bf16[384,896]{1,0:T(8,128)(2,1)} %get-tuple-element.15), channel_id=1, source_target_pairs={{0,4},{2,14},{3,11},{4,0},{6,10},{7,15},{8,12},{10,6},{11,3},{12,8... | collective-permute-start | bytes 2064392 | tf_op jit(solution)/shard_map/ppermute | solution.py:377
  34.4 22.2 %collective-permute-start.11 = (bf16[384,896]{1,0:T(8,128)(2,1)S(1)}, bf16[384,896]{1,0:T(8,128)(2,1)S(1)}, u32[]{:S(2)}, u32[]{:S(2)}) collective-permute-start(bf16[384,896]{1,0:T(8,128)(2,1)S(1)} %copy-done.23), channel_id=1, source_target_pairs={{0,4},{2,14},{3,11},{4,0},{6,10},{7,15},{8,12},{10,6},{11,3},{12,8... | collective-permute-start | bytes 2064392 | tf_op jit(solution)/shard_map/ppermute | solution.py:377
  38.0 27.7 %collective-permute-start.3 = (bf16[384,896]{1,0:T(8,128)(2,1)}, bf16[384,896]{1,0:T(8,128)(2,1)S(1)}, u32[]{:S(2)}, u32[]{:S(2)}) collective-permute-start(bf16[384,896]{1,0:T(8,128)(2,1)} %get-tuple-element.13), channel_id=1, source_target_pairs={{0,12},{1,9},{2,6},{4,8},{5,13},{6,2},{8,4},{9,1},{10,14},{12,0},{... | collective-permute-start | bytes 2064392 | tf_op jit(solution)/shard_map/ppermute | solution.py:377
  41.7 60.9 %collective-permute-start.30 = (bf16[512,1024]{1,0:T(8,128)(2,1)}, bf16[512,1024]{1,0:T(8,128)(2,1)}, u32[]{:S(2)}, u32[]{:S(2)}) collective-permute-start(bf16[512,1024]{1,0:T(8,128)(2,1)} %p0.1), channel_id=1, source_target_pairs={{0,2},{1,3},{2,0},{3,1},{4,6},{5,7},{6,4},{7,5},{8,10},{9,11},{10,... | collective-permute-start | bytes 3145736 | tf_op jit(solution)/shard_map/ppermute | solution.py:360
  51.4 51.9 %collective-permute-start.1 = (bf16[512,1024]{1,0:T(8,128)(2,1)}, bf16[512,1024]{1,0:T(8,128)(2,1)S(1)}, u32[]{:S(2)}, u32[]{:S(2)}) collective-permute-start(bf16[512,1024]{1,0:T(8,128)(2,1)} %p0.1), channel_id=1, source_target_pairs={{0,8},{4,12},{8,0},{12,4},{1,9},{5,13},{9,1},{13,5},{2,10},{6,14},... | collective-permute-start | bytes 3145736 | tf_op jit(solution)/shard_map/ppermute | solution.py:365
  53.4 48.3 %collective-permute-start.5 = (bf16[384,896]{1,0:T(8,128)(2,1)}, bf16[384,896]{1,0:T(8,128)(2,1)S(1)}, u32[]{:S(2)}, u32[]{:S(2)}) collective-permute-start(bf16[384,896]{1,0:T(8,128)(2,1)} %get-tuple-element.14), channel_id=1, source_target_pairs={{0,12},{1,9},{2,6},{4,8},{5,13},{6,2},{8,4},{9,1},{10,14},{12,0},{... | collective-permute-start | bytes 2064392 | tf_op jit(solution)/shard_map/ppermute | solution.py:377
  56.6 48.8 %collective-permute-start = (bf16[512,1024]{1,0:T(8,128)(2,1)}, bf16[512,1024]{1,0:T(8,128)(2,1)S(1)}, u32[]{:S(2)}, u32[]{:S(2)}) collective-permute-start(bf16[512,1024]{1,0:T(8,128)(2,1)} %p0.1), channel_id=1, source_target_pairs={{0,4},{4,0},{8,12},{12,8},{1,5},{5,1},{9,13},{13,9},{2,6},{6,2},{1... | collective-permute-start | bytes 3145736 | tf_op jit(solution)/shard_map/ppermute | solution.py:366
  65.7 59.8 %collective-permute-start.46 = (bf16[512,1024]{1,0:T(8,128)(2,1)}, bf16[512,1024]{1,0:T(8,128)(2,1)S(1)}, u32[]{:S(2)}, u32[]{:S(2)}) collective-permute-start(bf16[512,1024]{1,0:T(8,128)(2,1)} %p0.1), channel_id=1, source_target_pairs={{0,1},{1,0},{2,3},{3,2},{4,5},{5,4},{6,7},{7,6},{8,9},{9,8},{10,11... | collective-permute-start | bytes 3145736 | tf_op jit(solution)/shard_map/ppermute | solution.py:361
  71.0 78.6 %copy-start.9 = (bf16[384,896]{1,0:T(8,128)(2,1)}, bf16[384,896]{1,0:T(8,128)(2,1)S(1)}, u32[]{:S(2)}) copy-start(bf16[384,896]{1,0:T(8,128)(2,1)S(1)} %broadcast_select_fusion.9) | copy-start | bytes 2064388
  101.8 25.6 %collective-permute-start.22 = (bf16[384,896]{1,0:T(8,128)(2,1)S(1)}, bf16[384,896]{1,0:T(8,128)(2,1)S(1)}, u32[]{:S(2)}, u32[]{:S(2)}) collective-permute-start(bf16[384,896]{1,0:T(8,128)(2,1)S(1)} %broadcast_select_fusion.1), channel_id=1, source_target_pairs={{4,5},{5,4},{6,7},{7,6},{8,10},{9,11},{10,8},{11,9},{12,15},{13,14... | collective-permute-start | bytes 2064392 | tf_op jit(solution)/shard_map/ppermute | solution.py:378
  102.6 75.5 %copy-start.10 = (bf16[384,896]{1,0:T(8,128)(2,1)}, bf16[384,896]{1,0:T(8,128)(2,1)S(1)}, u32[]{:S(2)}) copy-start(bf16[384,896]{1,0:T(8,128)(2,1)S(1)} %broadcast_select_fusion.8) | copy-start | bytes 2064388
  102.6 28.8 %collective-permute-start.24 = (bf16[384,896]{1,0:T(8,128)(2,1)S(1)}, bf16[384,896]{1,0:T(8,128)(2,1)S(1)}, u32[]{:S(2)}, u32[]{:S(2)}) collective-permute-start(bf16[384,896]{1,0:T(8,128)(2,1)S(1)} %broadcast_select_fusion), channel_id=1, source_target_pairs={{4,5},{5,4},{6,7},{7,6},{8,10},{9,11},{10,8},{11,9},{12,15},{13,14... | collective-permute-start | bytes 2064392 | tf_op jit(solution)/shard_map/ppermute | solution.py:378
  103.3 43.4 %collective-permute-start.16 = (bf16[384,896]{1,0:T(8,128)(2,1)S(1)}, bf16[384,896]{1,0:T(8,128)(2,1)S(1)}, u32[]{:S(2)}, u32[]{:S(2)}) collective-permute-start(bf16[384,896]{1,0:T(8,128)(2,1)S(1)} %broadcast_select_fusion.5), channel_id=1, source_target_pairs={{0,2},{1,3},{2,0},{3,1},{4,7},{5,6},{6,5},{7,4},{12,13},{13,12},{1... | collective-permute-start | bytes 2064392 | tf_op jit(solution)/shard_map/ppermute | solution.py:378
  105.3 85.6 %copy-start.7 = (bf16[384,896]{1,0:T(8,128)(2,1)}, bf16[384,896]{1,0:T(8,128)(2,1)S(1)}, u32[]{:S(2)}) copy-start(bf16[384,896]{1,0:T(8,128)(2,1)S(1)} %broadcast_select_fusion.13) | copy-start | bytes 2064388
  105.4 85.6 %copy-start.14 = (bf16[512,1024]{1,0:T(8,128)(2,1)}, bf16[512,1024]{1,0:T(8,128)(2,1)S(1)}, u32[]{:S(2)}) copy-start(bf16[512,1024]{1,0:T(8,128)(2,1)S(1)} %collective-permute-done.p1) | copy-start | bytes 3145732
  105.4 72.6 %collective-permute-start.18 = (bf16[384,896]{1,0:T(8,128)(2,1)S(1)}, bf16[384,896]{1,0:T(8,128)(2,1)S(1)}, u32[]{:S(2)}, u32[]{:S(2)}) collective-permute-start(bf16[384,896]{1,0:T(8,128)(2,1)S(1)} %broadcast_select_fusion.4), channel_id=1, source_target_pairs={{0,2},{1,3},{2,0},{3,1},{4,7},{5,6},{6,5},{7,4},{12,13},{13,12},{1... | collective-permute-start | bytes 2064392 | tf_op jit(solution)/shard_map/ppermute | solution.py:378
  110.3 83.7 %copy-start.8 = (bf16[384,896]{1,0:T(8,128)(2,1)}, bf16[384,896]{1,0:T(8,128)(2,1)S(1)}, u32[]{:S(2)}) copy-start(bf16[384,896]{1,0:T(8,128)(2,1)S(1)} %broadcast_select_fusion.12) | copy-start | bytes 2064388
  125.4 52.7 %collective-permute-start.10 = (bf16[384,896]{1,0:T(8,128)(2,1)S(1)}, bf16[384,896]{1,0:T(8,128)(2,1)S(1)}, u32[]{:S(2)}, u32[]{:S(2)}) collective-permute-start(bf16[384,896]{1,0:T(8,128)(2,1)S(1)} %broadcast_select_fusion.9), channel_id=1, source_target_pairs={{0,1},{1,0},{2,3},{3,2},{8,11},{9,10},{10,9},{11,8},{12,14},{13,15... | collective-permute-start | bytes 2064392 | tf_op jit(solution)/shard_map/ppermute | solution.py:378
  127.4 62.0 %collective-permute-start.12 = (bf16[384,896]{1,0:T(8,128)(2,1)S(1)}, bf16[384,896]{1,0:T(8,128)(2,1)S(1)}, u32[]{:S(2)}, u32[]{:S(2)}) collective-permute-start(bf16[384,896]{1,0:T(8,128)(2,1)S(1)} %broadcast_select_fusion.8), channel_id=1, source_target_pairs={{0,1},{1,0},{2,3},{3,2},{8,11},{9,10},{10,9},{11,8},{12,14},{13,15... | collective-permute-start | bytes 2064392 | tf_op jit(solution)/shard_map/ppermute | solution.py:378
  131.4 59.6 %collective-permute-start.4 = (bf16[384,896]{1,0:T(8,128)(2,1)S(1)}, bf16[384,896]{1,0:T(8,128)(2,1)S(1)}, u32[]{:S(2)}, u32[]{:S(2)}) collective-permute-start(bf16[384,896]{1,0:T(8,128)(2,1)S(1)} %broadcast_select_fusion.13), channel_id=1, source_target_pairs={{0,3},{1,2},{2,1},{3,0},{4,6},{5,7},{6,4},{7,5},{8,9},{9,8},{10,11... | collective-permute-start | bytes 2064392 | tf_op jit(solution)/shard_map/ppermute | solution.py:378
  146.7 44.8 %collective-permute-start.6 = (bf16[384,896]{1,0:T(8,128)(2,1)S(1)}, bf16[384,896]{1,0:T(8,128)(2,1)S(1)}, u32[]{:S(2)}, u32[]{:S(2)}) collective-permute-start(bf16[384,896]{1,0:T(8,128)(2,1)S(1)} %broadcast_select_fusion.12), channel_id=1, source_target_pairs={{0,3},{1,2},{2,1},{3,0},{4,6},{5,7},{6,4},{7,5},{8,9},{9,8},{10,11... | collective-permute-start | bytes 2064392 | tf_op jit(solution)/shard_map/ppermute | solution.py:378
  178.0 79.7 %collective-permute-start.37 = (bf16[512,1024]{1,0:T(8,128)(2,1)}, bf16[512,1024]{1,0:T(8,128)(2,1)}, u32[]{:S(2)}, u32[]{:S(2)}) collective-permute-start(bf16[512,1024]{1,0:T(8,128)(2,1)} %collective-permute-done.30.p0), channel_id=1, source_target_pairs={{0,1},{1,0},{2,3},{3,2},{4,5},{5,4},{6,7},{7,6},{8,9},{9,8},{10,11... | collective-permute-start | bytes 3145736 | tf_op jit(solution)/shard_map/ppermute | solution.py:362
  178.1 96.1 %copy-start = (bf16[384,896]{1,0:T(8,128)(2,1)}, bf16[384,896]{1,0:T(8,128)(2,1)S(1)}, u32[]{:S(2)}) copy-start(bf16[384,896]{1,0:T(8,128)(2,1)S(1)} %broadcast_select_fusion.7.refs_0_) | copy-start | bytes 2064388
  178.2 18.5 %collective-permute-start.25 = (bf16[384,896]{1,0:T(8,128)(2,1)S(1)}, bf16[384,896]{1,0:T(8,128)(2,1)}, u32[]{:S(2)}, u32[]{:S(2)}) collective-permute-start(bf16[384,896]{1,0:T(8,128)(2,1)S(1)} %broadcast_select_fusion.3.refs_0_), channel_id=1, source_target_pairs={{0,16},{16,0},{1,17},{17,1},{2,18},{18,2},{3,19},{19,3},{4,20},{20... | collective-permute-start | bytes 2064392 | tf_op jit(solution)/shard_map/ppermute | solution.py:380
  189.3 13.3 %collective-permute-start.26 = (bf16[384,896]{1,0:T(8,128)(2,1)}, bf16[384,896]{1,0:T(8,128)(2,1)}, u32[]{:S(2)}, u32[]{:S(2)}) collective-permute-start(bf16[384,896]{1,0:T(8,128)(2,1)} %broadcast_select_fusion.2.refs_1_), channel_id=1, source_target_pairs={{0,16},{16,0},{1,17},{17,1},{2,18},{18,2},{3,19},{19,3},{4,20},{20... | collective-permute-start | bytes 2064392 | tf_op jit(solution)/shard_map/ppermute | solution.py:380
  190.9 136.8 %copy-start.1 = (bf16[384,896]{1,0:T(8,128)(2,1)}, bf16[384,896]{1,0:T(8,128)(2,1)S(1)}, u32[]{:S(2)}) copy-start(bf16[384,896]{1,0:T(8,128)(2,1)S(1)} %broadcast_select_fusion.6.refs_1_) | copy-start | bytes 2064388
  191.0 26.4 %collective-permute-start.19 = (bf16[384,896]{1,0:T(8,128)(2,1)S(1)}, bf16[384,896]{1,0:T(8,128)(2,1)}, u32[]{:S(2)}, u32[]{:S(2)}) collective-permute-start(bf16[384,896]{1,0:T(8,128)(2,1)S(1)} %broadcast_select_fusion.7.refs_0_), channel_id=1, source_target_pairs={{0,16},{16,0},{1,17},{17,1},{2,18},{18,2},{3,19},{19,3},{4,20},{20... | collective-permute-start | bytes 2064392 | tf_op jit(solution)/shard_map/ppermute | solution.py:380
  192.8 55.8 %collective-permute-start.20 = (bf16[384,896]{1,0:T(8,128)(2,1)S(1)}, bf16[384,896]{1,0:T(8,128)(2,1)}, u32[]{:S(2)}, u32[]{:S(2)}) collective-permute-start(bf16[384,896]{1,0:T(8,128)(2,1)S(1)} %broadcast_select_fusion.6.refs_1_), channel_id=1, source_target_pairs={{0,16},{16,0},{1,17},{17,1},{2,18},{18,2},{3,19},{19,3},{4,20},{20... | collective-permute-start | bytes 2064392 | tf_op jit(solution)/shard_map/ppermute | solution.py:380
  194.0 133.9 %copy-start.30 = (bf16[4096]{0:T(1024)(128)(2,1)S(1)}, bf16[4096]{0:T(1024)(128)(2,1)}, u32[]{:S(2)}) copy-start(bf16[4096]{0:T(1024)(128)(2,1)} %param.7) | copy-start | bytes 24580
  195.2 140.1 %copy-start.2 = (bf16[384,896]{1,0:T(8,128)(2,1)}, bf16[384,896]{1,0:T(8,128)(2,1)S(1)}, u32[]{:S(2)}) copy-start(bf16[384,896]{1,0:T(8,128)(2,1)S(1)} %broadcast_select_fusion.11.refs_0_) | copy-start | bytes 2064388
  196.7 138.7 %copy-start.3 = (bf16[384,896]{1,0:T(8,128)(2,1)}, bf16[384,896]{1,0:T(8,128)(2,1)S(1)}, u32[]{:S(2)}) copy-start(bf16[384,896]{1,0:T(8,128)(2,1)S(1)} %broadcast_select_fusion.10.refs_1_) | copy-start | bytes 2064388
  196.7 77.5 %collective-permute-start.13 = (bf16[384,896]{1,0:T(8,128)(2,1)S(1)}, bf16[384,896]{1,0:T(8,128)(2,1)}, u32[]{:S(2)}, u32[]{:S(2)}) collective-permute-start(bf16[384,896]{1,0:T(8,128)(2,1)S(1)} %broadcast_select_fusion.11.refs_0_), channel_id=1, source_target_pairs={{0,16},{16,0},{1,17},{17,1},{2,18},{18,2},{3,19},{19,3},{4,20},{20... | collective-permute-start | bytes 2064392 | tf_op jit(solution)/shard_map/ppermute | solution.py:380
  202.7 73.1 %collective-permute-start.14 = (bf16[384,896]{1,0:T(8,128)(2,1)S(1)}, bf16[384,896]{1,0:T(8,128)(2,1)}, u32[]{:S(2)}, u32[]{:S(2)}) collective-permute-start(bf16[384,896]{1,0:T(8,128)(2,1)S(1)} %broadcast_select_fusion.10.refs_1_), channel_id=1, source_target_pairs={{0,16},{16,0},{1,17},{17,1},{2,18},{18,2},{3,19},{19,3},{4,20},{20... | collective-permute-start | bytes 2064392 | tf_op jit(solution)/shard_map/ppermute | solution.py:380
  217.4 105.0 %collective-permute-start.32 = (bf16[512,1024]{1,0:T(8,128)(2,1)}, bf16[512,1024]{1,0:T(8,128)(2,1)}, u32[]{:S(2)}, u32[]{:S(2)}) collective-permute-start(bf16[512,1024]{1,0:T(8,128)(2,1)} %collective-permute-done.30.p0), channel_id=1, source_target_pairs={{0,8},{4,12},{8,0},{12,4},{1,9},{5,13},{9,1},{13,5},{2,10},{6,14},... | collective-permute-start | bytes 3145736 | tf_op jit(solution)/shard_map/ppermute | solution.py:365
  248.5 77.8 %collective-permute-start.2 = (bf16[512,1024]{1,0:T(8,128)(2,1)}, bf16[512,1024]{1,0:T(8,128)(2,1)}, u32[]{:S(2)}, u32[]{:S(2)}) collective-permute-start(bf16[512,1024]{1,0:T(8,128)(2,1)} %copy-done.13), channel_id=1, source_target_pairs={{0,4},{4,0},{8,12},{12,8},{1,5},{5,1},{9,13},{13,9},{2,6},{6,2},{1... | collective-permute-start | bytes 3145736 | tf_op jit(solution)/shard_map/ppermute | solution.py:366
  257.6 68.8 %collective-permute-start.39 = (bf16[512,1024]{1,0:T(8,128)(2,1)}, bf16[512,1024]{1,0:T(8,128)(2,1)}, u32[]{:S(2)}, u32[]{:S(2)}) collective-permute-start(bf16[512,1024]{1,0:T(8,128)(2,1)} %collective-permute-done.37.p0), channel_id=1, source_target_pairs={{0,8},{4,12},{8,0},{12,4},{1,9},{5,13},{9,1},{13,5},{2,10},{6,14},... | collective-permute-start | bytes 3145736 | tf_op jit(solution)/shard_map/ppermute | solution.py:365
  274.2 18.4 %collective-permute-start.7 = (bf16[384,896]{1,0:T(8,128)(2,1)S(1)}, bf16[384,896]{1,0:T(8,128)(2,1)S(1)}, u32[]{:S(2)}, u32[]{:S(2)}) collective-permute-start(bf16[384,896]{1,0:T(8,128)(2,1)S(1)} %broadcast_select_fusion.15.refs_0_), channel_id=1, source_target_pairs={{0,16},{16,0},{1,17},{17,1},{2,18},{18,2},{3,19},{19,3},{4,20},{20... | collective-permute-start | bytes 2064392 | tf_op jit(solution)/shard_map/ppermute | solution.py:380
  275.8 30.3 %collective-permute-start.8 = (bf16[384,896]{1,0:T(8,128)(2,1)S(1)}, bf16[384,896]{1,0:T(8,128)(2,1)S(1)}, u32[]{:S(2)}, u32[]{:S(2)}) collective-permute-start(bf16[384,896]{1,0:T(8,128)(2,1)S(1)} %broadcast_select_fusion.14.refs_1_), channel_id=1, source_target_pairs={{0,16},{16,0},{1,17},{17,1},{2,18},{18,2},{3,19},{19,3},{4,20},{20... | collective-permute-start | bytes 2064392 | tf_op jit(solution)/shard_map/ppermute | solution.py:380
  292.6 67.8 %collective-permute-start.31 = (bf16[512,1024]{1,0:T(8,128)(2,1)}, bf16[512,1024]{1,0:T(8,128)(2,1)}, u32[]{:S(2)}, u32[]{:S(2)}) collective-permute-start(bf16[512,1024]{1,0:T(8,128)(2,1)} %collective-permute-done.30.p0), channel_id=1, source_target_pairs={{0,4},{4,0},{8,12},{12,8},{1,5},{5,1},{9,13},{13,9},{2,6},{6,2},{1... | collective-permute-start | bytes 3145736 | tf_op jit(solution)/shard_map/ppermute | solution.py:366
  306.9 53.6 %collective-permute-start.48 = (bf16[512,1024]{1,0:T(8,128)(2,1)}, bf16[512,1024]{1,0:T(8,128)(2,1)}, u32[]{:S(2)}, u32[]{:S(2)}) collective-permute-start(bf16[512,1024]{1,0:T(8,128)(2,1)} %copy-done.11), channel_id=1, source_target_pairs={{0,8},{4,12},{8,0},{12,4},{1,9},{5,13},{9,1},{13,5},{2,10},{6,14},... | collective-permute-start | bytes 3145736 | tf_op jit(solution)/shard_map/ppermute | solution.py:365
  322.4 38.6 %collective-permute-start.33 = (bf16[512,1024]{1,0:T(8,128)(2,1)}, bf16[512,1024]{1,0:T(8,128)(2,1)}, u32[]{:S(2)}, u32[]{:S(2)}) collective-permute-start(bf16[512,1024]{1,0:T(8,128)(2,1)} %collective-permute-done.32.p2), channel_id=1, source_target_pairs={{0,4},{4,0},{8,12},{12,8},{1,5},{5,1},{9,13},{13,9},{2,6},{6,2},{1... | collective-permute-start | bytes 3145736 | tf_op jit(solution)/shard_map/ppermute | solution.py:366
  326.3 41.1 %collective-permute-start.38 = (bf16[512,1024]{1,0:T(8,128)(2,1)}, bf16[512,1024]{1,0:T(8,128)(2,1)}, u32[]{:S(2)}, u32[]{:S(2)}) collective-permute-start(bf16[512,1024]{1,0:T(8,128)(2,1)} %collective-permute-done.37.p0), channel_id=1, source_target_pairs={{0,4},{4,0},{8,12},{12,8},{1,5},{5,1},{9,13},{13,9},{2,6},{6,2},{1... | collective-permute-start | bytes 3145736 | tf_op jit(solution)/shard_map/ppermute | solution.py:366
  326.4 41.0 %collective-permute-start.40 = (bf16[512,1024]{1,0:T(8,128)(2,1)}, bf16[512,1024]{1,0:T(8,128)(2,1)}, u32[]{:S(2)}, u32[]{:S(2)}) collective-permute-start(bf16[512,1024]{1,0:T(8,128)(2,1)} %collective-permute-done.39.p2), channel_id=1, source_target_pairs={{0,4},{4,0},{8,12},{12,8},{1,5},{5,1},{9,13},{13,9},{2,6},{6,2},{1... | collective-permute-start | bytes 3145736 | tf_op jit(solution)/shard_map/ppermute | solution.py:366
  360.5 44.0 %collective-permute-start.47 = (bf16[512,1024]{1,0:T(8,128)(2,1)S(1)}, bf16[512,1024]{1,0:T(8,128)(2,1)S(1)}, u32[]{:S(2)}, u32[]{:S(2)}) collective-permute-start(bf16[512,1024]{1,0:T(8,128)(2,1)S(1)} %copy-done.12), channel_id=1, source_target_pairs={{0,4},{4,0},{8,12},{12,8},{1,5},{5,1},{9,13},{13,9},{2,6},{6,2},{1... | collective-permute-start | bytes 3145736 | tf_op jit(solution)/shard_map/ppermute | solution.py:366
  360.6 43.8 %collective-permute-start.49 = (bf16[512,1024]{1,0:T(8,128)(2,1)}, bf16[512,1024]{1,0:T(8,128)(2,1)S(1)}, u32[]{:S(2)}, u32[]{:S(2)}) collective-permute-start(bf16[512,1024]{1,0:T(8,128)(2,1)} %collective-permute-done.48.p2), channel_id=1, source_target_pairs={{0,4},{4,0},{8,12},{12,8},{1,5},{5,1},{9,13},{13,9},{2,6},{6,2},{1... | collective-permute-start | bytes 3145736 | tf_op jit(solution)/shard_map/ppermute | solution.py:366
  388.1 39.5 %collective-permute-start.42 = (bf16[512,896]{1,0:T(8,128)(2,1)}, bf16[512,896]{1,0:T(8,128)(2,1)}, u32[]{:S(2)}, u32[]{:S(2)}) collective-permute-start(bf16[512,896]{1,0:T(8,128)(2,1)} %shard_map.80.h0), channel_id=1, source_target_pairs={{0,8},{4,12},{8,0},{12,4},{1,9},{5,13},{9,1},{13,5},{2,10},{6,14},... | collective-permute-start | bytes 2752520 | tf_op jit(solution)/shard_map/ppermute | solution.py:365
  402.7 41.5 %collective-permute-start.35 = (bf16[512,896]{1,0:T(8,128)(2,1)}, bf16[512,896]{1,0:T(8,128)(2,1)}, u32[]{:S(2)}, u32[]{:S(2)}) collective-permute-start(bf16[512,896]{1,0:T(8,128)(2,1)} %shard_map.77.h0), channel_id=1, source_target_pairs={{0,8},{4,12},{8,0},{12,4},{1,9},{5,13},{9,1},{13,5},{2,10},{6,14},... | collective-permute-start | bytes 2752520 | tf_op jit(solution)/shard_map/ppermute | solution.py:365
  427.3 23.5 %collective-permute-start.51 = (bf16[512,896]{1,0:T(8,128)(2,1)}, bf16[512,896]{1,0:T(8,128)(2,1)}, u32[]{:S(2)}, u32[]{:S(2)}) collective-permute-start(bf16[512,896]{1,0:T(8,128)(2,1)} %shard_map.83.h0), channel_id=1, source_target_pairs={{0,8},{4,12},{8,0},{12,4},{1,9},{5,13},{9,1},{13,5},{2,10},{6,14},... | collective-permute-start | bytes 2752520 | tf_op jit(solution)/shard_map/ppermute | solution.py:365
  427.6 35.8 %collective-permute-start.41 = (bf16[512,896]{1,0:T(8,128)(2,1)S(1)}, bf16[512,896]{1,0:T(8,128)(2,1)}, u32[]{:S(2)}, u32[]{:S(2)}) collective-permute-start(bf16[512,896]{1,0:T(8,128)(2,1)S(1)} %copy-done.33), channel_id=1, source_target_pairs={{0,4},{4,0},{8,12},{12,8},{1,5},{5,1},{9,13},{13,9},{2,6},{6,2},{1... | collective-permute-start | bytes 2752520 | tf_op jit(solution)/shard_map/ppermute | solution.py:366
  427.6 36.4 %collective-permute-start.43 = (bf16[512,896]{1,0:T(8,128)(2,1)}, bf16[512,896]{1,0:T(8,128)(2,1)}, u32[]{:S(2)}, u32[]{:S(2)}) collective-permute-start(bf16[512,896]{1,0:T(8,128)(2,1)} %collective-permute-done.42.h2), channel_id=1, source_target_pairs={{0,4},{4,0},{8,12},{12,8},{1,5},{5,1},{9,13},{13,9},{2,6},{6,2},{1... | collective-permute-start | bytes 2752520 | tf_op jit(solution)/shard_map/ppermute | solution.py:366
  442.4 31.1 %collective-permute-start.28 = (bf16[512,896]{1,0:T(8,128)(2,1)}, bf16[512,896]{1,0:T(8,128)(2,1)}, u32[]{:S(2)}, u32[]{:S(2)}) collective-permute-start(bf16[512,896]{1,0:T(8,128)(2,1)} %shard_map.73.h0), channel_id=1, source_target_pairs={{0,8},{4,12},{8,0},{12,4},{1,9},{5,13},{9,1},{13,5},{2,10},{6,14},... | collective-permute-start | bytes 2752520 | tf_op jit(solution)/shard_map/ppermute | solution.py:365
  444.1 35.6 %collective-permute-start.50 = (bf16[512,896]{1,0:T(8,128)(2,1)S(1)}, bf16[512,896]{1,0:T(8,128)(2,1)}, u32[]{:S(2)}, u32[]{:S(2)}) collective-permute-start(bf16[512,896]{1,0:T(8,128)(2,1)S(1)} %copy-done.32), channel_id=1, source_target_pairs={{0,4},{4,0},{8,12},{12,8},{1,5},{5,1},{9,13},{13,9},{2,6},{6,2},{1... | collective-permute-start | bytes 2752520 | tf_op jit(solution)/shard_map/ppermute | solution.py:366
  450.8 29.0 %collective-permute-start.52 = (bf16[512,896]{1,0:T(8,128)(2,1)}, bf16[512,896]{1,0:T(8,128)(2,1)}, u32[]{:S(2)}, u32[]{:S(2)}) collective-permute-start(bf16[512,896]{1,0:T(8,128)(2,1)} %collective-permute-done.51.h2), channel_id=1, source_target_pairs={{0,4},{4,0},{8,12},{12,8},{1,5},{5,1},{9,13},{13,9},{2,6},{6,2},{1... | collective-permute-start | bytes 2752520 | tf_op jit(solution)/shard_map/ppermute | solution.py:366
  463.4 26.2 %collective-permute-start.34 = (bf16[512,896]{1,0:T(8,128)(2,1)S(1)}, bf16[512,896]{1,0:T(8,128)(2,1)}, u32[]{:S(2)}, u32[]{:S(2)}) collective-permute-start(bf16[512,896]{1,0:T(8,128)(2,1)S(1)} %copy-done.31), channel_id=1, source_target_pairs={{0,4},{4,0},{8,12},{12,8},{1,5},{5,1},{9,13},{13,9},{2,6},{6,2},{1... | collective-permute-start | bytes 2752520 | tf_op jit(solution)/shard_map/ppermute | solution.py:366
  463.9 25.8 %collective-permute-start.36 = (bf16[512,896]{1,0:T(8,128)(2,1)}, bf16[512,896]{1,0:T(8,128)(2,1)}, u32[]{:S(2)}, u32[]{:S(2)}) collective-permute-start(bf16[512,896]{1,0:T(8,128)(2,1)} %collective-permute-done.35.h2), channel_id=1, source_target_pairs={{0,4},{4,0},{8,12},{12,8},{1,5},{5,1},{9,13},{13,9},{2,6},{6,2},{1... | collective-permute-start | bytes 2752520 | tf_op jit(solution)/shard_map/ppermute | solution.py:366
  473.5 30.4 %collective-permute-start.44 = (bf16[512,1024]{1,0:T(8,128)(2,1)}, bf16[512,1024]{1,0:T(8,128)(2,1)S(1)}, u32[]{:S(2)}, u32[]{:S(2)}) collective-permute-start(bf16[512,1024]{1,0:T(8,128)(2,1)} %shard_map.81), channel_id=1, source_target_pairs={{0,1},{1,0},{2,3},{3,2},{4,5},{5,4},{6,7},{7,6},{8,9},{9,8},{10,11... | collective-permute-start | bytes 3145736 | tf_op jit(solution)/shard_map/ppermute | solution.py:396
  479.7 30.8 %collective-permute-start.27 = (bf16[512,896]{1,0:T(8,128)(2,1)}, bf16[512,896]{1,0:T(8,128)(2,1)}, u32[]{:S(2)}, u32[]{:S(2)}) collective-permute-start(bf16[512,896]{1,0:T(8,128)(2,1)} %shard_map.73.h0), channel_id=1, source_target_pairs={{0,4},{4,0},{8,12},{12,8},{1,5},{5,1},{9,13},{13,9},{2,6},{6,2},{1... | collective-permute-start | bytes 2752520 | tf_op jit(solution)/shard_map/ppermute | solution.py:366
  479.9 30.7 %collective-permute-start.29 = (bf16[512,896]{1,0:T(8,128)(2,1)}, bf16[512,896]{1,0:T(8,128)(2,1)}, u32[]{:S(2)}, u32[]{:S(2)}) collective-permute-start(bf16[512,896]{1,0:T(8,128)(2,1)} %collective-permute-done.28.h2), channel_id=1, source_target_pairs={{0,4},{4,0},{8,12},{12,8},{1,5},{5,1},{9,13},{13,9},{2,6},{6,2},{1... | collective-permute-start | bytes 2752520 | tf_op jit(solution)/shard_map/ppermute | solution.py:366
  489.6 56.0 %collective-permute-start.53 = (bf16[512,1024]{1,0:T(8,128)(2,1)}, bf16[512,1024]{1,0:T(8,128)(2,1)S(1)}, u32[]{:S(2)}, u32[]{:S(2)}) collective-permute-start(bf16[512,1024]{1,0:T(8,128)(2,1)} %shard_map.84), channel_id=1, source_target_pairs={{0,1},{1,0},{2,3},{3,2},{4,5},{5,4},{6,7},{7,6},{8,9},{9,8},{10,11... | collective-permute-start | bytes 3145736 | tf_op jit(solution)/shard_map/ppermute | solution.py:399
  505.9 49.5 %collective-permute-start.45 = (bf16[512,1024]{1,0:T(8,128)(2,1)S(1)}, bf16[512,1024]{1,0:T(8,128)(2,1)S(1)}, u32[]{:S(2)}, u32[]{:S(2)}) collective-permute-start(bf16[512,1024]{1,0:T(8,128)(2,1)S(1)} %add_convert_fusion.1), channel_id=1, source_target_pairs={{0,2},{1,3},{2,0},{3,1},{4,6},{5,7},{6,4},{7,5},{8,10},{9,11},{10,... | collective-permute-start | bytes 3145736 | tf_op jit(solution)/shard_map/ppermute | solution.py:398
  (25 other events, 620.0 us)

commit v3 on v2

--- a/solution.py
+++ b/solution.py
@@ -191,11 +191,12 @@
     )(*args)
 
 
-def norm_of(pieces, gain, where_at):
+def norm_of(pieces, gain, where_at, j, stack):
     tokens, depth = pieces[0].shape
     tall = tokens // 4
 
-    def kernel(at_ref, p0, p1, p2, p3, gain_ref, out_ref):
+    def kernel(at_ref, p0, p1, p2, p3, gain_ref, *rest):
+        out_ref = rest[-1]
         row = at_ref[1]
         parts = [p[...].astype(F32) for p in (p0, p1, p2, p3)]
         squares = sum(jnp.sum(v * v, axis=-1, keepdims=True) for v in parts)
@@ -205,20 +206,23 @@
             normed = v * scale * gain_ref[at].astype(F32)
             out_ref[:, pl.ds(pl.multiple_of(at * depth, 128), depth)] = normed.astype(BF16)
 
+    before = [] if stack is None else [stack]
     return pl.pallas_call(
         kernel,
         grid_spec=pltpu.PrefetchScalarGridSpec(
             num_scalar_prefetch=1,
             grid=(4,),
             in_specs=[pl.BlockSpec((tall, depth), lambda n, at: (n, 0))] * 4
-            + [pl.BlockSpec((4, 1, depth), lambda n, at: (0, 0, 0))],
-            out_specs=pl.BlockSpec((tall, 4 * depth), lambda n, at: (n, 0)),
-        ),
-        out_shape=jax.ShapeDtypeStruct((tokens, 4 * depth), BF16),
+            + [pl.BlockSpec((4, 1, depth), lambda n, at: (0, 0, 0))]
+            + [pl.BlockSpec(memory_space=pl.ANY)] * len(before),
+            out_specs=pl.BlockSpec((tall, 4 * depth), lambda n, at: ((at[2] ^ j) * 4 + n, 0)),
+        ),
+        out_shape=jax.ShapeDtypeStruct((4 * tokens, 4 * depth), BF16),
+        input_output_aliases={6: 0} if before else {},
         cost_estimate=pl.CostEstimate(
             flops=4 * tokens * depth * 4, bytes_accessed=16 * tokens * depth, transcendentals=tokens
         ),
-    )(where_at, *pieces, gain.reshape(4, 1, depth))
+    )(where_at, *pieces, gain.reshape(4, 1, depth), *before)
 
 
 def mask_down(weight, wide):
@@ -243,8 +247,8 @@
     )(weight, wide)
 
 
-def gate_up(x, dense, where_at):
-    tokens, depth = x.shape
+def gate_up(x, dense, where_at, s, n_col):
+    tokens, depth = x.shape[0] // n_col, x.shape[1]
     double = dense.shape[1]
     tiles = double // 256
 
@@ -261,7 +265,7 @@
             num_scalar_prefetch=1,
             grid=(tiles,),
             in_specs=[
-                pl.BlockSpec((tokens, depth), lambda n, at: (0, 0)),
+                pl.BlockSpec((tokens, depth), lambda n, at: (lax.rem(at[2] - s + n_col, n_col), 0)),
                 pl.BlockSpec((depth, 256), lambda n, at: (0, n)),
             ],
             out_specs=pl.BlockSpec((tokens, 128), lambda n, at: (0, n)),
@@ -365,7 +369,9 @@
         far = lax.ppermute(v, "row", across)
         return v, lax.ppermute(v, "row", core), far, lax.ppermute(far, "row", core)
 
-    normed = [norm_of(over_row(v), norm_gain, where_at) for v in shards]
+    normed = None
+    for i, v in enumerate(shards):
+        normed = norm_of(over_row(v), norm_gain, where_at, i, normed)
 
     sizes = (rows, width, per_col, per_row, n_col, n_blocks)
     order = [0, 2, 1, 3]
@@ -389,15 +395,16 @@
     weights = mask_down(down_weight, wide[:, None, :])
     weights = weights.reshape(n_row, -1, down_weight.shape[1])
 
-    def part_of(j, kind):
-        hidden = gate_up(normed[j], dense, where_at)
+    def part_of(s, kind):
+        hidden = gate_up(normed, dense, where_at, s, n_col)
         return down_part(over_row(hidden), weights, where_at, kind)
 
-    passing = lax.ppermute(part_of(3, BF16), "col", beside(1))
-    passing = (part_of(2, F32) + passing.astype(F32)).astype(BF16)
-    passing = lax.ppermute(passing, "col", beside(2))
-    close = lax.ppermute(part_of(1, BF16), "col", beside(1))
-    return (part_of(0, F32) + passing.astype(F32) + close.astype(F32)).astype(BF16)
+    ring = [(i, (i + 1) % n_col) for i in range(n_col)]
+    passing = lax.ppermute(part_of(1, BF16), "col", ring)
+    for s in range(2, n_col):
+        passing = (part_of(s, F32) + passing.astype(F32)).astype(BF16)
+        passing = lax.ppermute(passing, "col", ring)
+    return (part_of(0, F32) + passing.astype(F32)).astype(BF16)
 
 
 def solution(mesh):

time: 562 us -> 602 us (1.071)
  waiting for transfers between devices: 200 us -> 317 us
  starting transfers between devices: 153 us -> 84.5 us
    ppermute x8, waiting for transfers between devices: 51.5 us -> 121 us  [layer(): came = lax.ppermute(v, ('row', 'col'), to_plane(m))]
    ppermute x8, starting transfers between devices: 66.6 us -> 6.13 us  [over_row(): far = lax.ppermute(v, 'row', across)]
    ppermute x8, waiting for transfers between devices: 6.7 us -> 66.8 us  [over_row(): far = lax.ppermute(v, 'row', across)]
    ppermute x8, waiting for transfers between devices: 48.2 us -> 74.2 us  [layer(): got[m].append((v, lax.ppermute(v, 'group', swap)))]
    ppermute x1, starting transfers between devices: 0.01 us -> 23.1 us  [layer(): shards = [tokens, near, far, lax.ppermute(far, 'col', beside(1))]]
    ppermute x1, waiting for transfers between devices: 15.1 us -> 0.01 us  [layer(): near = lax.ppermute(tokens, 'col', beside(1))]
    ppermute x3, waiting for transfers between devices: 39.7 us -> 25.8 us  [the longest x2 24.4 us: layer(): passing = lax.ppermute(passing, 'col', ring)]
    ppermute x8, starting transfers between devices: 14.9 us -> 1.07 us  [over_row(): lax.ppermute(far, 'row', core)]
  transfers between devices with their start and end apart: 54 -> 54, of which waited for: 16 -> 20; matrix products, arithmetic and copies ran while one was open for 3% -> 2% of each run, Pallas kernels for 31% -> 25%
where the time goes in v3:
time: 602 us; the launch traced here: 598 us
  waiting for transfers between devices  317 us (53%)
  Pallas kernels  176 us (29%)
  starting transfers between devices  84.5 us (14%)
  other arithmetic  16 us (3%)
    ppermute x8, waiting for transfers between devices, layer(): came = lax.ppermute(v, ('row', 'col'), to_plane(m))  121 us
    ppermute x8, waiting for transfers between devices, layer(): got[m].append((v, lax.ppermute(v, 'group', swap)))  74.2 us
    ppermute x8, waiting for transfers between devices, over_row(): far = lax.ppermute(v, 'row', across)  66.8 us
    pallas_call x4, Pallas kernels, gate_up(): pl.pallas_call(kernel, grid_spec=pltpu.PrefetchScalarGridSpec(num_scalar_...  57.1 us
    pallas_call x4, Pallas kernels, down_part(): pl.pallas_call(kernel, grid_spec=pltpu.PrefetchScalarGridSpec(num_scalar_...  38.4 us
    ppermute x8, waiting for transfers between devices, layer(): v = jnp.where(col == m, v, lax.ppermute(v, ('row', 'col'), in_plane(m)))  28.9 us
    pallas_call x4, Pallas kernels, norm_of(): pl.pallas_call(kernel, grid_spec=pltpu.PrefetchScalarGridSpec(num_scalar_...  25.6 us
    pallas_call x4, Pallas kernels, expand(): pl.pallas_call(kernel, grid_spec=pltpu.PrefetchScalarGridSpec(num_scalar_...  24.6 us
  transfers between devices with their start and end apart: 54, of which 20 were waited for; matrix products, arithmetic and copies ran while one was open for 2% of the time, Pallas kernels for 25%

profile of v3, /device:TPU:0, one launch (start us, length us, event | category | flops | bytes accessed | tf_op | source)
XLA Modules:
  0.0 598.5 jit_solution(2282199943561621204)
XLA Ops:
  3.5 4.7 shard_map.71
  8.2 1.6 collective-permute-start.33
  9.8 1.5 collective-permute-start.35
  11.3 4.8 shard_map.70
  16.1 4.9 collective-permute-start.27
  20.9 1.9 collective-permute-start.29
  22.9 4.8 shard_map.69
  27.6 1.9 collective-permute-start.21
  29.6 4.8 shard_map.68
  34.4 2.5 collective-permute-start.23
  38.2 3.5 collective-permute-start.15
  41.9 2.0 collective-permute-start.17
  45.1 7.2 %collective-permute-done.29 = bf16[384,896]{1,0:T(8,128)(2,1)} collective-permute-done((bf16[384,896]{1,0:T(8,128)(2,1)}, bf16[384,896]{1,0:T(8,128)(2,1)}, u32[]{:S(2)}, u32[]{:S(2)}) %collective-permute-start.29) | collective-permute-done | bytes 688160 | tf_op jit(solution)/shard_map/ppermute | solution.py:383
  52.3 2.0 collective-permute-start.13
  56.8 2.1 collective-permute-start.8
  58.9 7.7 %collective-permute-done.15 = bf16[384,896]{1,0:T(8,128)(2,1)S(1)} collective-permute-done((bf16[384,896]{1,0:T(8,128)(2,1)}, bf16[384,896]{1,0:T(8,128)(2,1)S(1)}, u32[]{:S(2)}, u32[]{:S(2)}) %collective-permute-start.15) | collective-permute-done | bytes 688160 | tf_op jit(solution)/shard_map/ppermute | solution.py:383
  67.3 14.0 %collective-permute-done.17 = bf16[384,896]{1,0:T(8,128)(2,1)S(1)} collective-permute-done((bf16[384,896]{1,0:T(8,128)(2,1)}, bf16[384,896]{1,0:T(8,128)(2,1)S(1)}, u32[]{:S(2)}, u32[]{:S(2)}) %collective-permute-start.17) | collective-permute-done | bytes 688160 | tf_op jit(solution)/shard_map/ppermute | solution.py:383
  82.1 21.2 %collective-permute-done.13.p2 = bf16[512,1024]{1,0:T(8,128)(2,1)S(1)} collective-permute-done((bf16[512,1024]{1,0:T(8,128)(2,1)S(1)}, bf16[512,1024]{1,0:T(8,128)(2,1)S(1)}, u32[]{:S(2)}, u32[]{:S(2)}) %collective-permute-start.13) | collective-permute-done | bytes 1048608 | tf_op jit(solution)/shard_map/ppermute | solution.py:369
  103.3 1.9 collective-permute-start.28
  105.3 3.0 collective-permute-start
  108.3 1.9 collective-permute-start.30
  110.4 5.5 collective-permute-start.22
  115.9 1.9 collective-permute-start.24
  117.9 57.3 %collective-permute-done.28 = bf16[384,896]{1,0:T(8,128)(2,1)S(1)} collective-permute-done((bf16[384,896]{1,0:T(8,128)(2,1)S(1)}, bf16[384,896]{1,0:T(8,128)(2,1)S(1)}, u32[]{:S(2)}, u32[]{:S(2)}) %collective-permute-start.28) | collective-permute-done | bytes 688160 | tf_op jit(solution)/shard_map/ppermute | solution.py:384
  175.2 2.6 collective-permute-start.16
  177.9 49.3 %collective-permute-done.30 = bf16[384,896]{1,0:T(8,128)(2,1)S(1)} collective-permute-done((bf16[384,896]{1,0:T(8,128)(2,1)S(1)}, bf16[384,896]{1,0:T(8,128)(2,1)S(1)}, u32[]{:S(2)}, u32[]{:S(2)}) %collective-permute-start.30) | collective-permute-done | bytes 688160 | tf_op jit(solution)/shard_map/ppermute | solution.py:384
  227.2 2.8 collective-permute-start.18
  234.5 14.4 %collective-permute-done.18 = bf16[384,896]{1,0:T(8,128)(2,1)S(1)} collective-permute-done((bf16[384,896]{1,0:T(8,128)(2,1)S(1)}, bf16[384,896]{1,0:T(8,128)(2,1)S(1)}, u32[]{:S(2)}, u32[]{:S(2)}) %collective-permute-start.18) | collective-permute-done | bytes 688160 | tf_op jit(solution)/shard_map/ppermute | solution.py:384
  248.9 23.1 %collective-permute-start.1 = (bf16[512,1024]{1,0:T(8,128)(2,1)}, bf16[512,1024]{1,0:T(8,128)(2,1)}, u32[]{:S(2)}, u32[]{:S(2)}) collective-permute-start(bf16[512,1024]{1,0:T(8,128)(2,1)} %collective-permute-done.p0), channel_id=1, source_target_pairs={{0,1},{1,0},{2,3},{3,2},{4,5},{5,4},{6,7},{7,6},{8,9},{9,8},{10,11... | collective-permute-start | bytes 3145736 | tf_op jit(solution)/shard_map/ppermute | solution.py:366
  272.1 2.1 collective-permute-start.25
  274.3 3.7 collective-permute-done.31.refs_2_
  279.5 13.2 %collective-permute-done.32.refs_3_ = bf16[384,896]{1,0:T(8,128)(2,1)S(1)} collective-permute-done((bf16[384,896]{1,0:T(8,128)(2,1)S(1)}, bf16[384,896]{1,0:T(8,128)(2,1)S(1)}, u32[]{:S(2)}, u32[]{:S(2)}) %collective-permute-start.32) | collective-permute-done | bytes 688160 | tf_op jit(solution)/shard_map/ppermute | solution.py:386
  294.2 13.3 %collective-permute-done.25.refs_2_ = bf16[384,896]{1,0:T(8,128)(2,1)S(1)} collective-permute-done((bf16[384,896]{1,0:T(8,128)(2,1)S(1)}, bf16[384,896]{1,0:T(8,128)(2,1)S(1)}, u32[]{:S(2)}, u32[]{:S(2)}) %collective-permute-start.25) | collective-permute-done | bytes 688160 | tf_op jit(solution)/shard_map/ppermute | solution.py:386
  307.4 14.7 %collective-permute-done.26.refs_3_ = bf16[384,896]{1,0:T(8,128)(2,1)S(1)} collective-permute-done((bf16[384,896]{1,0:T(8,128)(2,1)S(1)}, bf16[384,896]{1,0:T(8,128)(2,1)S(1)}, u32[]{:S(2)}, u32[]{:S(2)}) %collective-permute-start.26) | collective-permute-done | bytes 688160 | tf_op jit(solution)/shard_map/ppermute | solution.py:386
  322.2 14.7 %collective-permute-done.19.refs_2_ = bf16[384,896]{1,0:T(8,128)(2,1)S(1)} collective-permute-done((bf16[384,896]{1,0:T(8,128)(2,1)S(1)}, bf16[384,896]{1,0:T(8,128)(2,1)S(1)}, u32[]{:S(2)}, u32[]{:S(2)}) %collective-permute-start.19) | collective-permute-done | bytes 688160 | tf_op jit(solution)/shard_map/ppermute | solution.py:386
  336.9 14.6 %collective-permute-done.20.refs_3_ = bf16[384,896]{1,0:T(8,128)(2,1)S(1)} collective-permute-done((bf16[384,896]{1,0:T(8,128)(2,1)S(1)}, bf16[384,896]{1,0:T(8,128)(2,1)S(1)}, u32[]{:S(2)}, u32[]{:S(2)}) %collective-permute-start.20) | collective-permute-done | bytes 688160 | tf_op jit(solution)/shard_map/ppermute | solution.py:386
  352.3 11.0 %collective-permute-done.6.p2 = bf16[512,1024]{1,0:T(8,128)(2,1)} collective-permute-done((bf16[512,1024]{1,0:T(8,128)(2,1)}, bf16[512,1024]{1,0:T(8,128)(2,1)}, u32[]{:S(2)}, u32[]{:S(2)}) %collective-permute-start.6) | collective-permute-done | bytes 1048608 | tf_op jit(solution)/shard_map/ppermute | solution.py:369
  364.8 19.9 %collective-permute-done.3.p2 = bf16[512,1024]{1,0:T(8,128)(2,1)} collective-permute-done((bf16[512,1024]{1,0:T(8,128)(2,1)}, bf16[512,1024]{1,0:T(8,128)(2,1)}, u32[]{:S(2)}, u32[]{:S(2)}) %collective-permute-start.3) | collective-permute-done | bytes 1048608 | tf_op jit(solution)/shard_map/ppermute | solution.py:369
  387.1 6.1 %shard_map.72.refs_4_ = bf16[4,1024,1792]{2,1,0:T(8,128)(2,1)} custom-call(s32[8192]{0:T(1024)} %broadcast_select_fusion.16.slots_ref, s32[3]{0:T(128)} %compare_select_fusion.2.at_ref, bf16[384,896]{1,0:T(8,128)(2,1)} %copy-done.6, bf16[384,896]{1,0:T(8,128)(2,1)} %copy-done.7, bf16[384,896]{1,0:T(8,128)(2,1)} %copy-done.21, bf16[384,896]{1,0:T(8,128)(2,1)} %copy-done.22), custom_call_target="tpu_custom_call" | custom-call | bytes 7340032 | tf_op jit(solution)/shard_map/pallas_call | solution.py:174
  393.3 6.1 %shard_map.73.refs_4_ = bf16[4,1024,1792]{2,1,0:T(8,128)(2,1)} custom-call(s32[8192]{0:T(1024)} %broadcast_select_fusion.16.slots_ref, s32[3]{0:T(128)} %compare_select_fusion.2.at_ref, bf16[384,896]{1,0:T(8,128)(2,1)} %copy-done, bf16[384,896]{1,0:T(8,128)(2,1)} %copy-done.1, bf16[384,896]{1,0:T(8,128)(2,1)} %copy-done.15, ...), custom_call_target="tpu_custom_call", output_to_operand_aliasing={{}: (6, {})} | custom-call | bytes 7340032 | tf_op jit(solution)/shard_map/pallas_call | solution.py:174
  399.5 6.2 %shard_map.74.refs_4_ = bf16[4,1024,1792]{2,1,0:T(8,128)(2,1)} custom-call(s32[8192]{0:T(1024)} %broadcast_select_fusion.16.slots_ref, s32[3]{0:T(128)} %compare_select_fusion.2.at_ref, bf16[384,896]{1,0:T(8,128)(2,1)} %copy-done.2, bf16[384,896]{1,0:T(8,128)(2,1)} %copy-done.3, bf16[384,896]{1,0:T(8,128)(2,1)} %copy-done.17, ...), custom_call_target="tpu_custom_call", output_to_operand_aliasing={{}: (6, {})} | custom-call | bytes 7340032 | tf_op jit(solution)/shard_map/pallas_call | solution.py:174
  405.6 6.2 %shard_map.75 = bf16[4,1024,1792]{2,1,0:T(8,128)(2,1)} custom-call(s32[8192]{0:T(1024)} %broadcast_select_fusion.16.slots_ref, s32[3]{0:T(128)} %compare_select_fusion.2.at_ref, bf16[384,896]{1,0:T(8,128)(2,1)} %copy-done.4, bf16[384,896]{1,0:T(8,128)(2,1)} %copy-done.5, bf16[384,896]{1,0:T(8,128)(2,1)} %copy-done.19, ...), custom_call_target="tpu_custom_call", output_to_operand_aliasing={{}: (6, {})} | custom-call | bytes 7340032 | tf_op jit(solution)/shard_map/pallas_call | solution.py:174
  411.8 6.4 %shard_map.64.rest_0_ = bf16[2048,4096]{1,0:T(8,128)(2,1)} custom-call(s32[3]{0:T(128)} %compare_select_fusion.2.at_ref, bf16[512,1024]{1,0:T(8,128)(2,1)} %p0.1, bf16[512,1024]{1,0:T(8,128)(2,1)} %copy-done.12, bf16[512,1024]{1,0:T(8,128)(2,1)} %copy-done.11, bf16[512,1024]{1,0:T(8,128)(2,1)} %copy-done.13, bf16[4,1,1024]{2,1,0:T(2,128)(2,1)} %reshape.50.gain_ref), custom_call_target="tpu_custom_call" | custom-call | flops 8388608 | bytes 8388608 | tf_op jit(solution)/shard_map/pallas_call | solution.py:210
  418.2 6.5 %shard_map.65.rest_0_ = bf16[2048,4096]{1,0:T(8,128)(2,1)} custom-call(s32[3]{0:T(128)} %compare_select_fusion.2.at_ref, bf16[512,1024]{1,0:T(8,128)(2,1)} %copy-done.8, bf16[512,1024]{1,0:T(8,128)(2,1)} %copy-done.9, bf16[512,1024]{1,0:T(8,128)(2,1)} %collective-permute-done.10.p2, ...), custom_call_target="tpu_custom_call", output_to_operand_aliasing={{}: (6, {})} | custom-call | flops 8388608 | bytes 8388608 | tf_op jit(solution)/shard_map/pallas_call | solution.py:210
  424.7 6.4 %shard_map.66.rest_0_ = bf16[2048,4096]{1,0:T(8,128)(2,1)} custom-call(s32[3]{0:T(128)} %compare_select_fusion.2.at_ref, bf16[512,1024]{1,0:T(8,128)(2,1)} %collective-permute-done.p0, bf16[512,1024]{1,0:T(8,128)(2,1)} %collective-permute-done.5.p1, bf16[512,1024]{1,0:T(8,128)(2,1)} %collective-permute-done.6.p2, ...), custom_call_target="tpu_custom_call", output_to_operand_aliasing={{}: (6, {})} | custom-call | flops 8388608 | bytes 8388608 | tf_op jit(solution)/shard_map/pallas_call | solution.py:210
  431.1 6.4 %shard_map.67.x_ref = bf16[2048,4096]{1,0:T(8,128)(2,1)} custom-call(s32[3]{0:T(128)} %compare_select_fusion.2.at_ref, bf16[512,1024]{1,0:T(8,128)(2,1)} %collective-permute-done.1.p0, bf16[512,1024]{1,0:T(8,128)(2,1)} %collective-permute-done.2.p1, bf16[512,1024]{1,0:T(8,128)(2,1)} %collective-permute-done.3.p2, ...), custom_call_target="tpu_custom_call", output_to_operand_aliasing={{}: (6, {})} | custom-call | flops 8388608 | bytes 8388608 | tf_op jit(solution)/shard_map/pallas_call | solution.py:210
  437.5 14.3 %shard_map.83.h0 = bf16[512,896]{1,0:T(8,128)(2,1)} custom-call(s32[3]{0:T(128)} %compare_select_fusion.2.at_ref, bf16[2048,4096]{1,0:T(8,128)(2,1)} %shard_map.67.x_ref, bf16[4096,1792]{1,0:T(8,128)(2,1)} %bitcast.8), custom_call_target="tpu_custom_call" | custom-call | flops 7516192768 | bytes 18874368 | tf_op jit(solution)/shard_map/pallas_call | solution.py:262
  452.2 14.3 %shard_map.81.h0 = bf16[512,896]{1,0:T(8,128)(2,1)} custom-call(s32[3]{0:T(128)} %compare_select_fusion.2.at_ref, bf16[2048,4096]{1,0:T(8,128)(2,1)} %shard_map.67.x_ref, bf16[4096,1792]{1,0:T(8,128)(2,1)} %bitcast.9), custom_call_target="tpu_custom_call" | custom-call | flops 7516192768 | bytes 18874368 | tf_op jit(solution)/shard_map/pallas_call | solution.py:262
  466.5 1.7 collective-permute-start.46
  468.2 6.9 %collective-permute-done.49.h2 = bf16[512,896]{1,0:T(8,128)(2,1)S(1)} collective-permute-done((bf16[512,896]{1,0:T(8,128)(2,1)}, bf16[512,896]{1,0:T(8,128)(2,1)S(1)}, u32[]{:S(2)}, u32[]{:S(2)}) %collective-permute-start.49) | collective-permute-done | bytes 917536 | tf_op jit(solution)/shard_map/ppermute | solution.py:369
  476.1 11.6 %shard_map.77 = bf16[3584,1024]{1,0:T(8,128)(2,1)} custom-call(bf16[3584,1024]{1,0:T(8,128)(2,1)} %w_ref.1, bf16[16,1,1024]{2,1,0:T(2,128)(2,1)} %broadcast_in_dim_reshape.5.mask_ref), custom_call_target="tpu_custom_call" | custom-call | flops 3670016 | bytes 14680064 | tf_op jit(solution)/shard_map/pallas_call | solution.py:235
  488.2 14.3 %shard_map.79.h0 = bf16[512,896]{1,0:T(8,128)(2,1)} custom-call(s32[3]{0:T(128)} %compare_select_fusion.2.at_ref, bf16[2048,4096]{1,0:T(8,128)(2,1)} %shard_map.67.x_ref, bf16[4096,1792]{1,0:T(8,128)(2,1)} %bitcast.10), custom_call_target="tpu_custom_call" | custom-call | flops 7516192768 | bytes 18874368 | tf_op jit(solution)/shard_map/pallas_call | solution.py:262
  503.3 9.4 %shard_map.84 = bf16[512,1024]{1,0:T(8,128)(2,1)} custom-call(s32[3]{0:T(128)} %compare_select_fusion.2.at_ref, bf16[512,896]{1,0:T(8,128)(2,1)} %shard_map.83.h0, bf16[512,896]{1,0:T(8,128)(2,1)} %collective-permute-done.48.h1, bf16[512,896]{1,0:T(8,128)(2,1)} %copy-done.29, bf16[512,896]{1,0:T(8,128)(2,1)} %collective-permute-done.50.h3, ...), custom_call_target="tpu_custom_call" | custom-call | flops 3758096384 | bytes 13107200 | tf_op jit(solution)/shard_map/pallas_call | solution.py:296
  512.7 14.3 %shard_map.76.h0 = bf16[512,896]{1,0:T(8,128)(2,1)} custom-call(s32[3]{0:T(128)} %compare_select_fusion.2.at_ref, bf16[2048,4096]{1,0:T(8,128)(2,1)} %shard_map.67.x_ref, bf16[4096,1792]{1,0:T(8,128)(2,1)} %bitcast.11), custom_call_target="tpu_custom_call" | custom-call | flops 7516192768 | bytes 18874368 | tf_op jit(solution)/shard_map/pallas_call | solution.py:262
  527.0 1.8 collective-permute-start.40
  528.8 9.7 %shard_map.82 = f32[512,1024]{1,0:T(8,128)} custom-call(s32[3]{0:T(128)} %compare_select_fusion.2.at_ref, bf16[512,896]{1,0:T(8,128)(2,1)} %shard_map.81.h0, bf16[512,896]{1,0:T(8,128)(2,1)} %collective-permute-done.45.h1, bf16[512,896]{1,0:T(8,128)(2,1)} %copy-done.28, bf16[512,896]{1,0:T(8,128)(2,1)} %collective-permute-done.47.h3, ...), custom_call_target="tpu_custom_call" | custom-call | flops 3758096384 | bytes 13107200 | tf_op jit(solution)/shard_map/pallas_call | solution.py:296
  539.9 1.9 add_convert_fusion.2
  542.0 7.7 %collective-permute-done.40.h2 = bf16[512,896]{1,0:T(8,128)(2,1)} collective-permute-done((bf16[512,896]{1,0:T(8,128)(2,1)}, bf16[512,896]{1,0:T(8,128)(2,1)}, u32[]{:S(2)}, u32[]{:S(2)}) %collective-permute-start.40) | collective-permute-done | bytes 917536 | tf_op jit(solution)/shard_map/ppermute | solution.py:369
  549.7 9.7 %shard_map.80 = f32[512,1024]{1,0:T(8,128)} custom-call(s32[3]{0:T(128)} %compare_select_fusion.2.at_ref, bf16[512,896]{1,0:T(8,128)(2,1)} %shard_map.79.h0, bf16[512,896]{1,0:T(8,128)(2,1)} %collective-permute-done.42.h1, bf16[512,896]{1,0:T(8,128)(2,1)} %collective-permute-done.43.h2, bf16[512,896]{1,0:T(8,128)(2,1)} %collective-permute-done.44.h3, ...), custom_call_target="tpu_custom_call" | custom-call | flops 3758096384 | bytes 13107200 | tf_op jit(solution)/shard_map/pallas_call | solution.py:296
  559.4 8.7 %collective-permute-done.52 = bf16[512,1024]{1,0:T(8,128)(2,1)S(1)} collective-permute-done((bf16[512,1024]{1,0:T(8,128)(2,1)S(1)}, bf16[512,1024]{1,0:T(8,128)(2,1)S(1)}, u32[]{:S(2)}, u32[]{:S(2)}) %collective-permute-start.52) | collective-permute-done | bytes 1048608 | tf_op jit(solution)/shard_map/ppermute | solution.py:406
  568.1 1.9 add_convert_fusion.1
  570.2 9.7 %shard_map.78 = f32[512,1024]{1,0:T(8,128)} custom-call(s32[3]{0:T(128)} %compare_select_fusion.2.at_ref, bf16[512,896]{1,0:T(8,128)(2,1)} %shard_map.76.h0, bf16[512,896]{1,0:T(8,128)(2,1)} %collective-permute-done.39.h1, bf16[512,896]{1,0:T(8,128)(2,1)} %collective-permute-done.40.h2, bf16[512,896]{1,0:T(8,128)(2,1)} %collective-permute-done.41.h3, ...), custom_call_target="tpu_custom_call" | custom-call | flops 3758096384 | bytes 13107200 | tf_op jit(solution)/shard_map/pallas_call | solution.py:296
  579.9 15.7 %collective-permute-done.53 = bf16[512,1024]{1,0:T(8,128)(2,1)S(1)} collective-permute-done((bf16[512,1024]{1,0:T(8,128)(2,1)S(1)}, bf16[512,1024]{1,0:T(8,128)(2,1)S(1)}, u32[]{:S(2)}, u32[]{:S(2)}) %collective-permute-start.53) | collective-permute-done | bytes 1048608 | tf_op jit(solution)/shard_map/ppermute | solution.py:406
  595.5 2.9 add_convert_fusion
  (161 shorter events, 26.9 us)
Async XLA Ops:
  8.2 26.2 %collective-permute-start.33 = (bf16[384,896]{1,0:T(8,128)(2,1)}, bf16[384,896]{1,0:T(8,128)(2,1)}, u32[]{:S(2)}, u32[]{:S(2)}) collective-permute-start(bf16[384,896]{1,0:T(8,128)(2,1)} %get-tuple-element.19), channel_id=1, source_target_pairs={{1,5},{2,10},{3,15},{5,1},{6,14},{7,11},{9,13},{10,2},{11,7},{13,9... | collective-permute-start | bytes 2064392 | tf_op jit(solution)/shard_map/ppermute | solution.py:383
  9.8 28.4 %collective-permute-start.35 = (bf16[384,896]{1,0:T(8,128)(2,1)}, bf16[384,896]{1,0:T(8,128)(2,1)}, u32[]{:S(2)}, u32[]{:S(2)}) collective-permute-start(bf16[384,896]{1,0:T(8,128)(2,1)} %get-tuple-element.20), channel_id=1, source_target_pairs={{1,5},{2,10},{3,15},{5,1},{6,14},{7,11},{9,13},{10,2},{11,7},{13,9... | collective-permute-start | bytes 2064392 | tf_op jit(solution)/shard_map/ppermute | solution.py:383
  16.1 25.8 %collective-permute-start.27 = (bf16[384,896]{1,0:T(8,128)(2,1)}, bf16[384,896]{1,0:T(8,128)(2,1)}, u32[]{:S(2)}, u32[]{:S(2)}) collective-permute-start(bf16[384,896]{1,0:T(8,128)(2,1)} %get-tuple-element.17), channel_id=1, source_target_pairs={{0,8},{1,13},{3,7},{4,12},{5,9},{7,3},{8,0},{9,5},{11,15},{12,4},{... | collective-permute-start | bytes 2064392 | tf_op jit(solution)/shard_map/ppermute | solution.py:383
  20.9 31.3 %collective-permute-start.29 = (bf16[384,896]{1,0:T(8,128)(2,1)}, bf16[384,896]{1,0:T(8,128)(2,1)}, u32[]{:S(2)}, u32[]{:S(2)}) collective-permute-start(bf16[384,896]{1,0:T(8,128)(2,1)} %get-tuple-element.18), channel_id=1, source_target_pairs={{0,8},{1,13},{3,7},{4,12},{5,9},{7,3},{8,0},{9,5},{11,15},{12,4},{... | collective-permute-start | bytes 2064392 | tf_op jit(solution)/shard_map/ppermute | solution.py:383
  27.6 27.8 %collective-permute-start.21 = (bf16[384,896]{1,0:T(8,128)(2,1)}, bf16[384,896]{1,0:T(8,128)(2,1)}, u32[]{:S(2)}, u32[]{:S(2)}) collective-permute-start(bf16[384,896]{1,0:T(8,128)(2,1)} %get-tuple-element.15), channel_id=1, source_target_pairs={{0,4},{2,14},{3,11},{4,0},{6,10},{7,15},{8,12},{10,6},{11,3},{12,8... | collective-permute-start | bytes 2064392 | tf_op jit(solution)/shard_map/ppermute | solution.py:383
  34.4 22.3 %collective-permute-start.23 = (bf16[384,896]{1,0:T(8,128)(2,1)S(1)}, bf16[384,896]{1,0:T(8,128)(2,1)S(1)}, u32[]{:S(2)}, u32[]{:S(2)}) collective-permute-start(bf16[384,896]{1,0:T(8,128)(2,1)S(1)} %copy-done.24), channel_id=1, source_target_pairs={{0,4},{2,14},{3,11},{4,0},{6,10},{7,15},{8,12},{10,6},{11,3},{12,8... | collective-permute-start | bytes 2064392 | tf_op jit(solution)/shard_map/ppermute | solution.py:383
  38.2 28.4 %collective-permute-start.15 = (bf16[384,896]{1,0:T(8,128)(2,1)}, bf16[384,896]{1,0:T(8,128)(2,1)S(1)}, u32[]{:S(2)}, u32[]{:S(2)}) collective-permute-start(bf16[384,896]{1,0:T(8,128)(2,1)} %get-tuple-element.13), channel_id=1, source_target_pairs={{0,12},{1,9},{2,6},{4,8},{5,13},{6,2},{8,4},{9,1},{10,14},{12,0},{... | collective-permute-start | bytes 2064392 | tf_op jit(solution)/shard_map/ppermute | solution.py:383
  41.9 39.4 %collective-permute-start.17 = (bf16[384,896]{1,0:T(8,128)(2,1)}, bf16[384,896]{1,0:T(8,128)(2,1)S(1)}, u32[]{:S(2)}, u32[]{:S(2)}) collective-permute-start(bf16[384,896]{1,0:T(8,128)(2,1)} %get-tuple-element.14), channel_id=1, source_target_pairs={{0,12},{1,9},{2,6},{4,8},{5,13},{6,2},{8,4},{9,1},{10,14},{12,0},{... | collective-permute-start | bytes 2064392 | tf_op jit(solution)/shard_map/ppermute | solution.py:383
  52.3 51.0 %collective-permute-start.13 = (bf16[512,1024]{1,0:T(8,128)(2,1)S(1)}, bf16[512,1024]{1,0:T(8,128)(2,1)S(1)}, u32[]{:S(2)}, u32[]{:S(2)}) collective-permute-start(bf16[512,1024]{1,0:T(8,128)(2,1)S(1)} %copy-done.10), channel_id=1, source_target_pairs={{0,8},{4,12},{8,0},{12,4},{1,9},{5,13},{9,1},{13,5},{2,10},{6,14},... | collective-permute-start | bytes 3145736 | tf_op jit(solution)/shard_map/ppermute | solution.py:369
  55.5 49.8 %collective-permute-start.12 = (bf16[512,1024]{1,0:T(8,128)(2,1)S(1)}, bf16[512,1024]{1,0:T(8,128)(2,1)S(1)}, u32[]{:S(2)}, u32[]{:S(2)}) collective-permute-start(bf16[512,1024]{1,0:T(8,128)(2,1)S(1)} %copy-done.10), channel_id=1, source_target_pairs={{0,4},{4,0},{8,12},{12,8},{1,5},{5,1},{9,13},{13,9},{2,6},{6,2},{1... | collective-permute-start | bytes 3145736 | tf_op jit(solution)/shard_map/ppermute | solution.py:370
  56.8 53.6 %collective-permute-start.8 = (bf16[512,1024]{1,0:T(8,128)(2,1)S(1)}, bf16[512,1024]{1,0:T(8,128)(2,1)S(1)}, u32[]{:S(2)}, u32[]{:S(2)}) collective-permute-start(bf16[512,1024]{1,0:T(8,128)(2,1)S(1)} %copy-done.10), channel_id=1, source_target_pairs={{0,1},{1,0},{2,3},{3,2},{4,5},{5,4},{6,7},{7,6},{8,9},{9,8},{10,11... | collective-permute-start | bytes 3145736 | tf_op jit(solution)/shard_map/ppermute | solution.py:365
  66.5 41.7 %collective-permute-start.34 = (bf16[384,896]{1,0:T(8,128)(2,1)S(1)}, bf16[384,896]{1,0:T(8,128)(2,1)S(1)}, u32[]{:S(2)}, u32[]{:S(2)}) collective-permute-start(bf16[384,896]{1,0:T(8,128)(2,1)S(1)} %broadcast_select_fusion.1), channel_id=1, source_target_pairs={{4,5},{5,4},{6,7},{7,6},{8,10},{9,11},{10,8},{11,9},{12,15},{13,14... | collective-permute-start | bytes 2064392 | tf_op jit(solution)/shard_map/ppermute | solution.py:384
  81.3 34.6 %collective-permute-start.36 = (bf16[384,896]{1,0:T(8,128)(2,1)S(1)}, bf16[384,896]{1,0:T(8,128)(2,1)S(1)}, u32[]{:S(2)}, u32[]{:S(2)}) collective-permute-start(bf16[384,896]{1,0:T(8,128)(2,1)S(1)} %broadcast_select_fusion), channel_id=1, source_target_pairs={{4,5},{5,4},{6,7},{7,6},{8,10},{9,11},{10,8},{11,9},{12,15},{13,14... | collective-permute-start | bytes 2064392 | tf_op jit(solution)/shard_map/ppermute | solution.py:384
  103.3 218.9 %copy-start.11 = (bf16[512,1024]{1,0:T(8,128)(2,1)}, bf16[512,1024]{1,0:T(8,128)(2,1)S(1)}, u32[]{:S(2)}) copy-start(bf16[512,1024]{1,0:T(8,128)(2,1)S(1)} %collective-permute-done.13.p2) | copy-start | bytes 3145732
  103.3 72.0 %collective-permute-start.28 = (bf16[384,896]{1,0:T(8,128)(2,1)S(1)}, bf16[384,896]{1,0:T(8,128)(2,1)S(1)}, u32[]{:S(2)}, u32[]{:S(2)}) collective-permute-start(bf16[384,896]{1,0:T(8,128)(2,1)S(1)} %broadcast_select_fusion.5), channel_id=1, source_target_pairs={{0,2},{1,3},{2,0},{3,1},{4,7},{5,6},{6,5},{7,4},{12,13},{13,12},{1... | collective-permute-start | bytes 2064392 | tf_op jit(solution)/shard_map/ppermute | solution.py:384
  105.3 174.2 %copy-start.12 = (bf16[512,1024]{1,0:T(8,128)(2,1)}, bf16[512,1024]{1,0:T(8,128)(2,1)S(1)}, u32[]{:S(2)}) copy-start(bf16[512,1024]{1,0:T(8,128)(2,1)S(1)} %collective-permute-done.12.p1) | copy-start | bytes 3145732
  105.3 124.8 %collective-permute-start = (bf16[512,1024]{1,0:T(8,128)(2,1)S(1)}, bf16[512,1024]{1,0:T(8,128)(2,1)}, u32[]{:S(2)}, u32[]{:S(2)}) collective-permute-start(bf16[512,1024]{1,0:T(8,128)(2,1)S(1)} %copy-done.10), channel_id=1, source_target_pairs={{0,2},{1,3},{2,0},{3,1},{4,6},{5,7},{6,4},{7,5},{8,10},{9,11},{10,... | collective-permute-start | bytes 3145736 | tf_op jit(solution)/shard_map/ppermute | solution.py:364
  108.3 118.9 %collective-permute-start.30 = (bf16[384,896]{1,0:T(8,128)(2,1)S(1)}, bf16[384,896]{1,0:T(8,128)(2,1)S(1)}, u32[]{:S(2)}, u32[]{:S(2)}) collective-permute-start(bf16[384,896]{1,0:T(8,128)(2,1)S(1)} %broadcast_select_fusion.4), channel_id=1, source_target_pairs={{0,2},{1,3},{2,0},{3,1},{4,7},{5,6},{6,5},{7,4},{12,13},{13,12},{1... | collective-permute-start | bytes 2064392 | tf_op jit(solution)/shard_map/ppermute | solution.py:384
  110.3 167.6 %copy-start.6 = (bf16[384,896]{1,0:T(8,128)(2,1)}, bf16[384,896]{1,0:T(8,128)(2,1)S(1)}, u32[]{:S(2)}) copy-start(bf16[384,896]{1,0:T(8,128)(2,1)S(1)} %broadcast_select_fusion.3.refs_0_) | copy-start | bytes 2064388
  110.3 275.6 %copy-start.27 = (bf16[4096]{0:T(1024)(128)(2,1)S(1)}, bf16[4096]{0:T(1024)(128)(2,1)}, u32[]{:S(2)}) copy-start(bf16[4096]{0:T(1024)(128)(2,1)} %param.7) | copy-start | bytes 24580
  110.4 241.4 %copy-start.8 = (bf16[512,1024]{1,0:T(8,128)(2,1)}, bf16[512,1024]{1,0:T(8,128)(2,1)S(1)}, u32[]{:S(2)}) copy-start(bf16[512,1024]{1,0:T(8,128)(2,1)S(1)} %collective-permute-done.8.p0) | copy-start | bytes 3145732
  110.4 121.3 %collective-permute-start.22 = (bf16[384,896]{1,0:T(8,128)(2,1)S(1)}, bf16[384,896]{1,0:T(8,128)(2,1)S(1)}, u32[]{:S(2)}, u32[]{:S(2)}) collective-permute-start(bf16[384,896]{1,0:T(8,128)(2,1)S(1)} %broadcast_select_fusion.9), channel_id=1, source_target_pairs={{0,1},{1,0},{2,3},{3,2},{8,11},{9,10},{10,9},{11,8},{12,14},{13,15... | collective-permute-start | bytes 2064392 | tf_op jit(solution)/shard_map/ppermute | solution.py:384
  115.9 116.3 %collective-permute-start.24 = (bf16[384,896]{1,0:T(8,128)(2,1)S(1)}, bf16[384,896]{1,0:T(8,128)(2,1)S(1)}, u32[]{:S(2)}, u32[]{:S(2)}) collective-permute-start(bf16[384,896]{1,0:T(8,128)(2,1)S(1)} %broadcast_select_fusion.8), channel_id=1, source_target_pairs={{0,1},{1,0},{2,3},{3,2},{8,11},{9,10},{10,9},{11,8},{12,14},{13,15... | collective-permute-start | bytes 2064392 | tf_op jit(solution)/shard_map/ppermute | solution.py:384
  117.9 233.7 %copy-start.7 = (bf16[384,896]{1,0:T(8,128)(2,1)}, bf16[384,896]{1,0:T(8,128)(2,1)S(1)}, u32[]{:S(2)}) copy-start(bf16[384,896]{1,0:T(8,128)(2,1)S(1)} %broadcast_select_fusion.2.refs_1_) | copy-start | bytes 2064388
  175.2 58.5 %collective-permute-start.16 = (bf16[384,896]{1,0:T(8,128)(2,1)S(1)}, bf16[384,896]{1,0:T(8,128)(2,1)S(1)}, u32[]{:S(2)}, u32[]{:S(2)}) collective-permute-start(bf16[384,896]{1,0:T(8,128)(2,1)S(1)} %broadcast_select_fusion.13), channel_id=1, source_target_pairs={{0,3},{1,2},{2,1},{3,0},{4,6},{5,7},{6,4},{7,5},{8,9},{9,8},{10,11... | collective-permute-start | bytes 2064392 | tf_op jit(solution)/shard_map/ppermute | solution.py:384
  177.9 215.3 %copy-start = (bf16[384,896]{1,0:T(8,128)(2,1)}, bf16[384,896]{1,0:T(8,128)(2,1)S(1)}, u32[]{:S(2)}) copy-start(bf16[384,896]{1,0:T(8,128)(2,1)S(1)} %broadcast_select_fusion.7.refs_0_) | copy-start | bytes 2064388
  227.2 21.7 %collective-permute-start.18 = (bf16[384,896]{1,0:T(8,128)(2,1)S(1)}, bf16[384,896]{1,0:T(8,128)(2,1)S(1)}, u32[]{:S(2)}, u32[]{:S(2)}) collective-permute-start(bf16[384,896]{1,0:T(8,128)(2,1)S(1)} %broadcast_select_fusion.12), channel_id=1, source_target_pairs={{0,3},{1,2},{2,1},{3,0},{4,6},{5,7},{6,4},{7,5},{8,9},{9,8},{10,11... | collective-permute-start | bytes 2064392 | tf_op jit(solution)/shard_map/ppermute | solution.py:384
  230.1 163.2 %copy-start.1 = (bf16[384,896]{1,0:T(8,128)(2,1)}, bf16[384,896]{1,0:T(8,128)(2,1)S(1)}, u32[]{:S(2)}) copy-start(bf16[384,896]{1,0:T(8,128)(2,1)S(1)} %broadcast_select_fusion.6.refs_1_) | copy-start | bytes 2064388
  230.1 42.0 %collective-permute-start.37 = (bf16[384,896]{1,0:T(8,128)(2,1)S(1)}, bf16[384,896]{1,0:T(8,128)(2,1)S(1)}, u32[]{:S(2)}, u32[]{:S(2)}) collective-permute-start(bf16[384,896]{1,0:T(8,128)(2,1)S(1)} %broadcast_select_fusion.3.refs_0_), channel_id=1, source_target_pairs={{0,16},{16,0},{1,17},{17,1},{2,18},{18,2},{3,19},{19,3},{4,20},{20... | collective-permute-start | bytes 2064392 | tf_op jit(solution)/shard_map/ppermute | solution.py:386
  231.6 42.6 %collective-permute-start.38 = (bf16[384,896]{1,0:T(8,128)(2,1)S(1)}, bf16[384,896]{1,0:T(8,128)(2,1)S(1)}, u32[]{:S(2)}, u32[]{:S(2)}) collective-permute-start(bf16[384,896]{1,0:T(8,128)(2,1)S(1)} %broadcast_select_fusion.2.refs_1_), channel_id=1, source_target_pairs={{0,16},{16,0},{1,17},{17,1},{2,18},{18,2},{3,19},{19,3},{4,20},{20... | collective-permute-start | bytes 2064392 | tf_op jit(solution)/shard_map/ppermute | solution.py:386
  232.2 45.8 %collective-permute-start.31 = (bf16[384,896]{1,0:T(8,128)(2,1)S(1)}, bf16[384,896]{1,0:T(8,128)(2,1)S(1)}, u32[]{:S(2)}, u32[]{:S(2)}) collective-permute-start(bf16[384,896]{1,0:T(8,128)(2,1)S(1)} %broadcast_select_fusion.7.refs_0_), channel_id=1, source_target_pairs={{0,16},{16,0},{1,17},{17,1},{2,18},{18,2},{3,19},{19,3},{4,20},{20... | collective-permute-start | bytes 2064392 | tf_op jit(solution)/shard_map/ppermute | solution.py:386
  233.7 159.5 %copy-start.2 = (bf16[384,896]{1,0:T(8,128)(2,1)}, bf16[384,896]{1,0:T(8,128)(2,1)S(1)}, u32[]{:S(2)}) copy-start(bf16[384,896]{1,0:T(8,128)(2,1)S(1)} %broadcast_select_fusion.11.refs_0_) | copy-start | bytes 2064388
  233.8 58.9 %collective-permute-start.32 = (bf16[384,896]{1,0:T(8,128)(2,1)S(1)}, bf16[384,896]{1,0:T(8,128)(2,1)S(1)}, u32[]{:S(2)}, u32[]{:S(2)}) collective-permute-start(bf16[384,896]{1,0:T(8,128)(2,1)S(1)} %broadcast_select_fusion.6.refs_1_), channel_id=1, source_target_pairs={{0,16},{16,0},{1,17},{17,1},{2,18},{18,2},{3,19},{19,3},{4,20},{20... | collective-permute-start | bytes 2064392 | tf_op jit(solution)/shard_map/ppermute | solution.py:386
  234.5 158.8 %copy-start.3 = (bf16[384,896]{1,0:T(8,128)(2,1)}, bf16[384,896]{1,0:T(8,128)(2,1)S(1)}, u32[]{:S(2)}) copy-start(bf16[384,896]{1,0:T(8,128)(2,1)S(1)} %broadcast_select_fusion.10.refs_1_) | copy-start | bytes 2064388
  248.9 102.9 %collective-permute-start.1 = (bf16[512,1024]{1,0:T(8,128)(2,1)}, bf16[512,1024]{1,0:T(8,128)(2,1)}, u32[]{:S(2)}, u32[]{:S(2)}) collective-permute-start(bf16[512,1024]{1,0:T(8,128)(2,1)} %collective-permute-done.p0), channel_id=1, source_target_pairs={{0,1},{1,0},{2,3},{3,2},{4,5},{5,4},{6,7},{7,6},{8,9},{9,8},{10,11... | collective-permute-start | bytes 3145736 | tf_op jit(solution)/shard_map/ppermute | solution.py:366
  272.1 35.3 %collective-permute-start.25 = (bf16[384,896]{1,0:T(8,128)(2,1)S(1)}, bf16[384,896]{1,0:T(8,128)(2,1)S(1)}, u32[]{:S(2)}, u32[]{:S(2)}) collective-permute-start(bf16[384,896]{1,0:T(8,128)(2,1)S(1)} %broadcast_select_fusion.11.refs_0_), channel_id=1, source_target_pairs={{0,16},{16,0},{1,17},{17,1},{2,18},{18,2},{3,19},{19,3},{4,20},{20... | collective-permute-start | bytes 2064392 | tf_op jit(solution)/shard_map/ppermute | solution.py:386
  274.2 48.0 %collective-permute-start.26 = (bf16[384,896]{1,0:T(8,128)(2,1)S(1)}, bf16[384,896]{1,0:T(8,128)(2,1)S(1)}, u32[]{:S(2)}, u32[]{:S(2)}) collective-permute-start(bf16[384,896]{1,0:T(8,128)(2,1)S(1)} %broadcast_select_fusion.10.refs_1_), channel_id=1, source_target_pairs={{0,16},{16,0},{1,17},{17,1},{2,18},{18,2},{3,19},{19,3},{4,20},{20... | collective-permute-start | bytes 2064392 | tf_op jit(solution)/shard_map/ppermute | solution.py:386
  278.0 59.0 %collective-permute-start.19 = (bf16[384,896]{1,0:T(8,128)(2,1)S(1)}, bf16[384,896]{1,0:T(8,128)(2,1)S(1)}, u32[]{:S(2)}, u32[]{:S(2)}) collective-permute-start(bf16[384,896]{1,0:T(8,128)(2,1)S(1)} %broadcast_select_fusion.15.refs_0_), channel_id=1, source_target_pairs={{0,16},{16,0},{1,17},{17,1},{2,18},{18,2},{3,19},{19,3},{4,20},{20... | collective-permute-start | bytes 2064392 | tf_op jit(solution)/shard_map/ppermute | solution.py:386
  292.7 58.9 %collective-permute-start.20 = (bf16[384,896]{1,0:T(8,128)(2,1)S(1)}, bf16[384,896]{1,0:T(8,128)(2,1)S(1)}, u32[]{:S(2)}, u32[]{:S(2)}) collective-permute-start(bf16[384,896]{1,0:T(8,128)(2,1)S(1)} %broadcast_select_fusion.14.refs_1_), channel_id=1, source_target_pairs={{0,16},{16,0},{1,17},{17,1},{2,18},{18,2},{3,19},{19,3},{4,20},{20... | collective-permute-start | bytes 2064392 | tf_op jit(solution)/shard_map/ppermute | solution.py:386
  307.4 44.3 %collective-permute-start.10 = (bf16[512,1024]{1,0:T(8,128)(2,1)S(1)}, bf16[512,1024]{1,0:T(8,128)(2,1)}, u32[]{:S(2)}, u32[]{:S(2)}) collective-permute-start(bf16[512,1024]{1,0:T(8,128)(2,1)S(1)} %collective-permute-done.8.p0), channel_id=1, source_target_pairs={{0,8},{4,12},{8,0},{12,4},{1,9},{5,13},{9,1},{13,5},{2,10},{6,14},... | collective-permute-start | bytes 3145736 | tf_op jit(solution)/shard_map/ppermute | solution.py:369
  322.2 30.0 %collective-permute-start.14 = (bf16[512,1024]{1,0:T(8,128)(2,1)S(1)}, bf16[512,1024]{1,0:T(8,128)(2,1)S(1)}, u32[]{:S(2)}, u32[]{:S(2)}) collective-permute-start(bf16[512,1024]{1,0:T(8,128)(2,1)S(1)} %collective-permute-done.13.p2), channel_id=1, source_target_pairs={{0,4},{4,0},{8,12},{12,8},{1,5},{5,1},{9,13},{13,9},{2,6},{6,2},{1... | collective-permute-start | bytes 3145736 | tf_op jit(solution)/shard_map/ppermute | solution.py:370
  336.9 26.3 %collective-permute-start.6 = (bf16[512,1024]{1,0:T(8,128)(2,1)}, bf16[512,1024]{1,0:T(8,128)(2,1)}, u32[]{:S(2)}, u32[]{:S(2)}) collective-permute-start(bf16[512,1024]{1,0:T(8,128)(2,1)} %collective-permute-done.p0), channel_id=1, source_target_pairs={{0,8},{4,12},{8,0},{12,4},{1,9},{5,13},{9,1},{13,5},{2,10},{6,14},... | collective-permute-start | bytes 3145736 | tf_op jit(solution)/shard_map/ppermute | solution.py:369
  351.6 11.7 %collective-permute-start.9 = (bf16[512,1024]{1,0:T(8,128)(2,1)S(1)}, bf16[512,1024]{1,0:T(8,128)(2,1)S(1)}, u32[]{:S(2)}, u32[]{:S(2)}) collective-permute-start(bf16[512,1024]{1,0:T(8,128)(2,1)S(1)} %collective-permute-done.8.p0), channel_id=1, source_target_pairs={{0,4},{4,0},{8,12},{12,8},{1,5},{5,1},{9,13},{13,9},{2,6},{6,2},{1... | collective-permute-start | bytes 3145736 | tf_op jit(solution)/shard_map/ppermute | solution.py:370
  351.7 33.0 %collective-permute-start.3 = (bf16[512,1024]{1,0:T(8,128)(2,1)}, bf16[512,1024]{1,0:T(8,128)(2,1)}, u32[]{:S(2)}, u32[]{:S(2)}) collective-permute-start(bf16[512,1024]{1,0:T(8,128)(2,1)} %collective-permute-done.1.p0), channel_id=1, source_target_pairs={{0,8},{4,12},{8,0},{12,4},{1,9},{5,13},{9,1},{13,5},{2,10},{6,14},... | collective-permute-start | bytes 3145736 | tf_op jit(solution)/shard_map/ppermute | solution.py:369
  351.7 66.4 %collective-permute-start.11 = (bf16[512,1024]{1,0:T(8,128)(2,1)}, bf16[512,1024]{1,0:T(8,128)(2,1)}, u32[]{:S(2)}, u32[]{:S(2)}) collective-permute-start(bf16[512,1024]{1,0:T(8,128)(2,1)} %collective-permute-done.10.p2), channel_id=1, source_target_pairs={{0,4},{4,0},{8,12},{12,8},{1,5},{5,1},{9,13},{13,9},{2,6},{6,2},{1... | collective-permute-start | bytes 3145736 | tf_op jit(solution)/shard_map/ppermute | solution.py:370
  352.2 72.5 %collective-permute-start.5 = (bf16[512,1024]{1,0:T(8,128)(2,1)}, bf16[512,1024]{1,0:T(8,128)(2,1)}, u32[]{:S(2)}, u32[]{:S(2)}) collective-permute-start(bf16[512,1024]{1,0:T(8,128)(2,1)} %collective-permute-done.p0), channel_id=1, source_target_pairs={{0,4},{4,0},{8,12},{12,8},{1,5},{5,1},{9,13},{13,9},{2,6},{6,2},{1... | collective-permute-start | bytes 3145736 | tf_op jit(solution)/shard_map/ppermute | solution.py:370
  363.3 61.4 %collective-permute-start.7 = (bf16[512,1024]{1,0:T(8,128)(2,1)}, bf16[512,1024]{1,0:T(8,128)(2,1)}, u32[]{:S(2)}, u32[]{:S(2)}) collective-permute-start(bf16[512,1024]{1,0:T(8,128)(2,1)} %collective-permute-done.6.p2), channel_id=1, source_target_pairs={{0,4},{4,0},{8,12},{12,8},{1,5},{5,1},{9,13},{13,9},{2,6},{6,2},{1... | collective-permute-start | bytes 3145736 | tf_op jit(solution)/shard_map/ppermute | solution.py:370
  364.3 66.8 %collective-permute-start.2 = (bf16[512,1024]{1,0:T(8,128)(2,1)}, bf16[512,1024]{1,0:T(8,128)(2,1)}, u32[]{:S(2)}, u32[]{:S(2)}) collective-permute-start(bf16[512,1024]{1,0:T(8,128)(2,1)} %collective-permute-done.1.p0), channel_id=1, source_target_pairs={{0,4},{4,0},{8,12},{12,8},{1,5},{5,1},{9,13},{13,9},{2,6},{6,2},{1... | collective-permute-start | bytes 3145736 | tf_op jit(solution)/shard_map/ppermute | solution.py:370
  384.8 46.3 %collective-permute-start.4 = (bf16[512,1024]{1,0:T(8,128)(2,1)}, bf16[512,1024]{1,0:T(8,128)(2,1)}, u32[]{:S(2)}, u32[]{:S(2)}) collective-permute-start(bf16[512,1024]{1,0:T(8,128)(2,1)} %collective-permute-done.3.p2), channel_id=1, source_target_pairs={{0,4},{4,0},{8,12},{12,8},{1,5},{5,1},{9,13},{13,9},{2,6},{6,2},{1... | collective-permute-start | bytes 3145736 | tf_op jit(solution)/shard_map/ppermute | solution.py:370
  451.7 23.4 %collective-permute-start.49 = (bf16[512,896]{1,0:T(8,128)(2,1)}, bf16[512,896]{1,0:T(8,128)(2,1)S(1)}, u32[]{:S(2)}, u32[]{:S(2)}) collective-permute-start(bf16[512,896]{1,0:T(8,128)(2,1)} %shard_map.83.h0), channel_id=1, source_target_pairs={{0,8},{4,12},{8,0},{12,4},{1,9},{5,13},{9,1},{13,5},{2,10},{6,14},... | collective-permute-start | bytes 2752520 | tf_op jit(solution)/shard_map/ppermute | solution.py:369
  452.0 50.8 %collective-permute-start.48 = (bf16[512,896]{1,0:T(8,128)(2,1)}, bf16[512,896]{1,0:T(8,128)(2,1)}, u32[]{:S(2)}, u32[]{:S(2)}) collective-permute-start(bf16[512,896]{1,0:T(8,128)(2,1)} %shard_map.83.h0), channel_id=1, source_target_pairs={{0,4},{4,0},{8,12},{12,8},{1,5},{5,1},{9,13},{13,9},{2,6},{6,2},{1... | collective-permute-start | bytes 2752520 | tf_op jit(solution)/shard_map/ppermute | solution.py:370
  466.5 36.3 %collective-permute-start.46 = (bf16[512,896]{1,0:T(8,128)(2,1)}, bf16[512,896]{1,0:T(8,128)(2,1)S(1)}, u32[]{:S(2)}, u32[]{:S(2)}) collective-permute-start(bf16[512,896]{1,0:T(8,128)(2,1)} %shard_map.81.h0), channel_id=1, source_target_pairs={{0,8},{4,12},{8,0},{12,4},{1,9},{5,13},{9,1},{13,5},{2,10},{6,14},... | collective-permute-start | bytes 2752520 | tf_op jit(solution)/shard_map/ppermute | solution.py:369
  475.2 28.2 %collective-permute-start.50 = (bf16[512,896]{1,0:T(8,128)(2,1)S(1)}, bf16[512,896]{1,0:T(8,128)(2,1)}, u32[]{:S(2)}, u32[]{:S(2)}) collective-permute-start(bf16[512,896]{1,0:T(8,128)(2,1)S(1)} %collective-permute-done.49.h2), channel_id=1, source_target_pairs={{0,4},{4,0},{8,12},{12,8},{1,5},{5,1},{9,13},{13,9},{2,6},{6,2},{1... | collective-permute-start | bytes 2752520 | tf_op jit(solution)/shard_map/ppermute | solution.py:370
  487.7 39.3 %collective-permute-start.45 = (bf16[512,896]{1,0:T(8,128)(2,1)S(1)}, bf16[512,896]{1,0:T(8,128)(2,1)}, u32[]{:S(2)}, u32[]{:S(2)}) collective-permute-start(bf16[512,896]{1,0:T(8,128)(2,1)S(1)} %copy-done.14), channel_id=1, source_target_pairs={{0,4},{4,0},{8,12},{12,8},{1,5},{5,1},{9,13},{13,9},{2,6},{6,2},{1... | collective-permute-start | bytes 2752520 | tf_op jit(solution)/shard_map/ppermute | solution.py:370
  502.5 26.3 %collective-permute-start.43 = (bf16[512,896]{1,0:T(8,128)(2,1)}, bf16[512,896]{1,0:T(8,128)(2,1)}, u32[]{:S(2)}, u32[]{:S(2)}) collective-permute-start(bf16[512,896]{1,0:T(8,128)(2,1)} %shard_map.79.h0), channel_id=1, source_target_pairs={{0,8},{4,12},{8,0},{12,4},{1,9},{5,13},{9,1},{13,5},{2,10},{6,14},... | collective-permute-start | bytes 2752520 | tf_op jit(solution)/shard_map/ppermute | solution.py:369
  502.8 46.9 %collective-permute-start.42 = (bf16[512,896]{1,0:T(8,128)(2,1)}, bf16[512,896]{1,0:T(8,128)(2,1)}, u32[]{:S(2)}, u32[]{:S(2)}) collective-permute-start(bf16[512,896]{1,0:T(8,128)(2,1)} %shard_map.79.h0), channel_id=1, source_target_pairs={{0,4},{4,0},{8,12},{12,8},{1,5},{5,1},{9,13},{13,9},{2,6},{6,2},{1... | collective-permute-start | bytes 2752520 | tf_op jit(solution)/shard_map/ppermute | solution.py:370
  502.8 26.0 %collective-permute-start.47 = (bf16[512,896]{1,0:T(8,128)(2,1)S(1)}, bf16[512,896]{1,0:T(8,128)(2,1)}, u32[]{:S(2)}, u32[]{:S(2)}) collective-permute-start(bf16[512,896]{1,0:T(8,128)(2,1)S(1)} %collective-permute-done.46.h2), channel_id=1, source_target_pairs={{0,4},{4,0},{8,12},{12,8},{1,5},{5,1},{9,13},{13,9},{2,6},{6,2},{1... | collective-permute-start | bytes 2752520 | tf_op jit(solution)/shard_map/ppermute | solution.py:370
  512.7 27.1 %collective-permute-start.51 = (bf16[512,1024]{1,0:T(8,128)(2,1)}, bf16[512,1024]{1,0:T(8,128)(2,1)S(1)}, u32[]{:S(2)}, u32[]{:S(2)}) collective-permute-start(bf16[512,1024]{1,0:T(8,128)(2,1)} %shard_map.84), channel_id=1, source_target_pairs={{0,1},{1,2},{2,3},{3,0},{4,5},{5,6},{6,7},{7,4},{8,9},{9,10},{10,1... | collective-permute-start | bytes 3145736 | tf_op jit(solution)/shard_map/ppermute | solution.py:403
  527.0 22.7 %collective-permute-start.40 = (bf16[512,896]{1,0:T(8,128)(2,1)}, bf16[512,896]{1,0:T(8,128)(2,1)}, u32[]{:S(2)}, u32[]{:S(2)}) collective-permute-start(bf16[512,896]{1,0:T(8,128)(2,1)} %shard_map.76.h0), channel_id=1, source_target_pairs={{0,8},{4,12},{8,0},{12,4},{1,9},{5,13},{9,1},{13,5},{2,10},{6,14},... | collective-permute-start | bytes 2752520 | tf_op jit(solution)/shard_map/ppermute | solution.py:369
  528.8 20.9 %collective-permute-start.44 = (bf16[512,896]{1,0:T(8,128)(2,1)}, bf16[512,896]{1,0:T(8,128)(2,1)}, u32[]{:S(2)}, u32[]{:S(2)}) collective-permute-start(bf16[512,896]{1,0:T(8,128)(2,1)} %collective-permute-done.43.h2), channel_id=1, source_target_pairs={{0,4},{4,0},{8,12},{12,8},{1,5},{5,1},{9,13},{13,9},{2,6},{6,2},{1... | collective-permute-start | bytes 2752520 | tf_op jit(solution)/shard_map/ppermute | solution.py:370
  541.8 26.3 %collective-permute-start.52 = (bf16[512,1024]{1,0:T(8,128)(2,1)S(1)}, bf16[512,1024]{1,0:T(8,128)(2,1)S(1)}, u32[]{:S(2)}, u32[]{:S(2)}) collective-permute-start(bf16[512,1024]{1,0:T(8,128)(2,1)S(1)} %add_convert_fusion.2), channel_id=1, source_target_pairs={{0,1},{1,2},{2,3},{3,0},{4,5},{5,6},{6,7},{7,4},{8,9},{9,10},{10,1... | collective-permute-start | bytes 3145736 | tf_op jit(solution)/shard_map/ppermute | solution.py:406
  541.9 28.3 %collective-permute-start.39 = (bf16[512,896]{1,0:T(8,128)(2,1)}, bf16[512,896]{1,0:T(8,128)(2,1)}, u32[]{:S(2)}, u32[]{:S(2)}) collective-permute-start(bf16[512,896]{1,0:T(8,128)(2,1)} %shard_map.76.h0), channel_id=1, source_target_pairs={{0,4},{4,0},{8,12},{12,8},{1,5},{5,1},{9,13},{13,9},{2,6},{6,2},{1... | collective-permute-start | bytes 2752520 | tf_op jit(solution)/shard_map/ppermute | solution.py:370
  549.7 20.5 %collective-permute-start.41 = (bf16[512,896]{1,0:T(8,128)(2,1)}, bf16[512,896]{1,0:T(8,128)(2,1)}, u32[]{:S(2)}, u32[]{:S(2)}) collective-permute-start(bf16[512,896]{1,0:T(8,128)(2,1)} %collective-permute-done.40.h2), channel_id=1, source_target_pairs={{0,4},{4,0},{8,12},{12,8},{1,5},{5,1},{9,13},{13,9},{2,6},{6,2},{1... | collective-permute-start | bytes 2752520 | tf_op jit(solution)/shard_map/ppermute | solution.py:370
  570.1 25.5 %collective-permute-start.53 = (bf16[512,1024]{1,0:T(8,128)(2,1)S(1)}, bf16[512,1024]{1,0:T(8,128)(2,1)S(1)}, u32[]{:S(2)}, u32[]{:S(2)}) collective-permute-start(bf16[512,1024]{1,0:T(8,128)(2,1)S(1)} %add_convert_fusion.1), channel_id=1, source_target_pairs={{0,1},{1,2},{2,3},{3,0},{4,5},{5,6},{6,7},{7,4},{8,9},{9,10},{10,1... | collective-permute-start | bytes 3145736 | tf_op jit(solution)/shard_map/ppermute | solution.py:406
  (21 other events, 954.4 us)
